TPU v7x, 32 devices: a whole 2x2x4 slice. The times are simulated.
32 devices in a mesh: comp: 4 (over z), lat: 8 (over y, x, core).
Axes of the slice: x: 2, y: 2, z: 4, core: 2. Of those that a mesh axis runs over, the one named last changes fastest.
Arguments:
- spectrum: float32 [1152, 16, 2048], P('comp', 'lat'), may hold values from 0.1 to 2
- courant_lat: float32 [1152], P('comp'), may hold values from -0.45 to 0.45
- courant_lon: float32 [1152], P('comp'), may hold values from -0.45 to 0.45
- sea_mask: int32 [16, 2048], P('lat'), may hold values from 0 to 1, as said below
- strength: float32 [1152], replicated, may hold values from 0.02 to 0.2
- quad_shift: int32 [4, 2], replicated, may hold values from -4 to 4
Outputs:
- spectrum_next: float32 [1152, 16, 2048], P('comp', 'lat')
Inputs may be any that keep to these rules, and one draw needn't show every extreme that they name: `quad_shift`: column 0 offsets frequency, column 1 offsets direction. `sea_mask`: each aligned block of 2 rows holds at most 3072 sea points, and some block holds exactly 3072.
All inputs are finite; a program needn't handle non-finite values.
Results may differ from a plain program's by a relative error of at most 0.00002.
Values sent between devices are 32-bit elements; how exact they have to be, the bound alone decides.
No kernel may reach another device: no remote copies, remote signals or barrier semaphores. Data moves between devices by JAX's collectives and lax.ppermute only.
A program may use at most 64 MiB of HBM per device.

v0:
```python
import jax
import jax.numpy as jnp
from jax import lax
from jax.sharding import PartitionSpec as P

NF = 36
ND = 32
NQ = 4


reach = 4


def extended(cells, sides, width):
    for axis, dim in sides:
        count = lax.axis_size(axis)
        ends = count - 1
        head = lax.slice_in_dim(cells, 0, width, axis=dim)
        tail = lax.slice_in_dim(cells, cells.shape[dim] - width, cells.shape[dim], axis=dim)
        cells = jnp.concatenate(
            [
                lax.ppermute(tail, axis, [(i, (i + 1) % count) for i in range(ends)]),
                cells,
                lax.ppermute(head, axis, [((i + 1) % count, i) for i in range(ends)]),
            ],
            axis=dim,
        )
    return cells


def upwind(field, along_lat, along_lon, maskf):
    padded = extended(field, (("lat", 1),), 1)
    south = padded[:, :-2, :]
    north = padded[:, 2:, :]
    west = jnp.roll(field, 1, axis=2)
    east = jnp.roll(field, -1, axis=2)
    plus_a = jnp.maximum(along_lat, 0.0)
    minus_a = jnp.minimum(along_lat, 0.0)
    plus_b = jnp.maximum(along_lon, 0.0)
    minus_b = jnp.minimum(along_lon, 0.0)
    moved = field - plus_a * (field - south) - minus_a * (north - field)
    moved = moved - plus_b * (field - west) - minus_b * (east - field)
    return moved * maskf


def interact(energy, strength, quad_shift):
    rest = energy.shape[1:]
    grid = energy.reshape((NF, ND) + rest)
    widths = ((reach, reach),) + ((0, 0),) * (grid.ndim - 1)
    padded = jnp.pad(grid, widths)
    total = jnp.zeros(grid.shape, jnp.float32)
    for index in range(NQ):
        offset_f = quad_shift[index, 0]
        offset_d = quad_shift[index, 1]
        partner = lax.dynamic_slice_in_dim(padded, reach + offset_f, NF, 0)
        partner = jnp.roll(partner, -offset_d, axis=1)
        total = total + partner * (partner - grid)
    coeff = strength.reshape((NF, ND) + (1,) * len(rest))
    return (coeff * grid * total).reshape(energy.shape)


def per_device(spectrum, courant_lat, courant_lon, sea_mask, strength, quad_shift):
    maskf = sea_mask.astype(jnp.float32)[None]
    along_lat = courant_lat[:, None, None]
    along_lon = courant_lon[:, None, None]
    field = upwind(spectrum, along_lat, along_lon, maskf)
    field = upwind(field, along_lat, along_lon, maskf)
    comp_dev, lat_dev, lon_count = field.shape
    point_count = lat_dev * lon_count
    flat = field.reshape(comp_dev, point_count)
    sea_most = 3 * point_count // 4
    land_first = 1 - sea_mask.reshape(point_count)
    ordering = jnp.argsort(land_first, stable=True)
    chosen = ordering[:sea_most]
    packed = jnp.take(flat, chosen, axis=1)
    spectra = lax.all_to_all(packed, "comp", split_axis=1, concat_axis=0, tiled=True)
    updated = spectra + interact(spectra, strength, quad_shift)
    returned = lax.all_to_all(updated, "comp", split_axis=0, concat_axis=1, tiled=True)
    result = jnp.zeros((comp_dev, point_count), jnp.float32).at[:, chosen].set(returned)
    return result.reshape(comp_dev, lat_dev, lon_count)


def solution(mesh):
    return jax.shard_map(
        per_device,
        mesh=mesh,
        in_specs=(P("comp", "lat", None), P("comp"), P("comp"), P("lat", None), P(), P()),
        out_specs=P("comp", "lat", None),
        check_vma=False,
    )
```

profile of v0, /device:TPU:2, one launch (start us, length us, event | category | flops | bytes accessed | tf_op | source)
XLA Modules:
  0.0 372.9 jit_solution(8586536082879812648)
XLA Ops:
  0.0 5.1 %copy.20 = f32[288,2,2048]{2,0,1:T(8,128)S(1)} copy(f32[288,2,2048]{2,1,0:T(2,128)} %param.8) | data formatting | bytes 9437184 | tf_op args[0]
  5.1 2.5 fusion.37
  7.6 1.9 collective-permute-start
  9.5 3.6 collective-permute-start.1
  13.4 1.9 fusion.35
  15.4 22.6 %collective-permute-done = f32[288,1,2048]{2,0,1:T(8,128)S(1)} collective-permute-done((f32[288,1,2048]{2,0,1:T(8,128)}, f32[288,1,2048]{2,0,1:T(8,128)S(1)}, u32[]{:S(2)}, u32[]{:S(2)}) %collective-permute-start) | collective-permute-done | bytes 2359328 | tf_op jit(solution)/shard_map/ppermute | solution.py:22
  38.0 24.4 %collective-permute-done.1 = f32[288,1,2048]{2,0,1:T(8,128)} collective-permute-done((f32[288,1,2048]{2,0,1:T(8,128)}, f32[288,1,2048]{2,0,1:T(8,128)}, u32[]{:S(2)}, u32[]{:S(2)}) %collective-permute-start.1) | collective-permute-done | bytes 2359328 | tf_op jit(solution)/shard_map/ppermute | solution.py:24
  62.4 4.8 %fusion.14 = f32[288,2,2048]{2,0,1:T(8,128)S(1)} fusion(f32[288,2,2048]{2,0,1:T(8,128)S(1)} %copy.20, f32[288,1,2048]{2,0,1:T(8,128)} %collective-permute-done.1, f32[288,1,2048]{2,0,1:T(8,128)S(1)} %collective-permute-done, f32[288,2,2047]{2,0,1:T(8,128)S(1)} %get-tuple-element.15, f32[288,2,1]{2,0,1:T(8,128)S(1)} %get-tuple-element.17, ...), kind=kLoop, calls=%fused_computation.35 | loop fusion | flops 20054016 | bytes 23613952 | tf_op jit(solution)/shard_map/mul | solution.py:43
  67.2 3.0 fusion.34
  70.8 3.7 collective-permute-start.2
  74.4 2.2 collective-permute-start.3
  76.7 5.8 %sort.17 = (s32[4096]{0:T(1024)}, s32[4096]{0:T(1024)S(1)}) sort(s32[4096]{0:T(1024)S(1)} %bitcast.42, s32[4096]{0:T(1024)S(1)} %iota.4), dimensions={0}, to_apply=%region_0.1 | sort | flops 49152 | bytes 65536 | tf_op jit(solution)/shard_map/jit(argsort)/sort | solution.py:73
  82.5 1.3 fusion.33
  83.9 5.6 %fusion.32 = (f32[288,2,2047]{2,0,1:T(8,128)S(1)}, f32[288,2,2047]{2,0,1:T(8,128)S(1)}) fusion(f32[288,2,2048]{2,0,1:T(8,128)} %copy-done), kind=kLoop, calls=%fused_computation.69 | loop fusion | bytes 18865152 | tf_op jit(solution)/shard_map/jit(_roll_static)/slice | solution.py:36
  89.5 11.8 %collective-permute-done.2 = f32[288,1,2048]{2,0,1:T(8,128)S(1)} collective-permute-done((f32[288,1,2048]{2,0,1:T(8,128)}, f32[288,1,2048]{2,0,1:T(8,128)S(1)}, u32[]{:S(2)}, u32[]{:S(2)}) %collective-permute-start.2) | collective-permute-done | bytes 2359328 | tf_op jit(solution)/shard_map/ppermute | solution.py:22
  101.3 24.4 %collective-permute-done.3 = f32[288,1,2048]{2,0,1:T(8,128)} collective-permute-done((f32[288,1,2048]{2,0,1:T(8,128)}, f32[288,1,2048]{2,0,1:T(8,128)}, u32[]{:S(2)}, u32[]{:S(2)}) %collective-permute-start.3) | collective-permute-done | bytes 2359328 | tf_op jit(solution)/shard_map/ppermute | solution.py:24
  125.7 6.4 %fusion.5 = f32[288,2,2048]{2,0,1:T(8,128)} fusion(f32[288,2,2048]{2,0,1:T(8,128)S(1)} %bitcast.34, f32[288,1,2048]{2,0,1:T(8,128)} %collective-permute-done.3, f32[288,1,2048]{2,0,1:T(8,128)S(1)} %collective-permute-done.2, f32[288,2,2047]{2,0,1:T(8,128)S(1)} %get-tuple-element.9, f32[288,2,1]{2,0,1:T(8,128)S(1)} %get-tuple-element.11, ...), kind=kLoop, calls=%fused_computation.24 | loop fusion | flops 20054016 | bytes 23613952 | tf_op jit(solution)/shard_map/mul | solution.py:43
  132.1 6.3 %copy.30 = f32[288,2,2048]{0,2,1:T(8,128)} copy(f32[288,2,2048]{2,0,1:T(8,128)} %fusion.5) | data formatting | bytes 9437184 | tf_op jit(solution)/shard_map/mul | solution.py:43
  138.3 15.8 %gather_fusion = f32[3072,288]{1,0:T(8,128)} fusion(f32[288,4096]{0,1:T(8,128)} %bitcast.32, s32[3072]{0:T(1024)S(1)} %get-tuple-element.25), kind=kCustom, calls=%fused_computation | custom fusion | bytes 7090176 | tf_op jit(solution)/shard_map/jit(_take)/gather | solution.py:75
  154.2 3.7 %copy.31 = f32[288,4,768]{2,0,1:T(8,128)S(1)} copy(f32[288,4,768]{0,2,1:T(8,128)} %bitcast.38) | data formatting | bytes 7077888 | tf_op jit(solution)/shard_map/jit(_take)/gather | solution.py:75
  157.9 2.1 broadcast_select_fusion
  160.0 5.0 %all-to-all-start = ((f32[288,4,768]{2,0,1:T(8,128)}), f32[288,4,768]{2,0,1:T(8,128)S(1)}, u32[]{:S(2)}, u32[]{:S(2)}) async-start(f32[288,4,768]{2,0,1:T(8,128)} %broadcast_select_fusion), calls=%async_computation | async-start | bytes 7077888 | tf_op jit(solution)/shard_map/all_to_all | solution.py:76
  165.0 0.7 fusion.40
  173.6 1.4 mul.110
  174.9 68.2 %all-to-all-done = f32[288,4,768]{2,0,1:T(8,128)S(1)} async-done(((f32[288,4,768]{2,0,1:T(8,128)}), f32[288,4,768]{2,0,1:T(8,128)S(1)}, u32[]{:S(2)}, u32[]{:S(2)}) %all-to-all-start) | async-done | bytes 3538976 | tf_op jit(solution)/shard_map/all_to_all | solution.py:76
  243.1 6.6 %pad_dynamic-slice_fusion.11 = (f32[36,32,768]{2,1,0:T(8,128)}, f32[36,32,768]{2,1,0:T(8,128)}, f32[36,32,768]{2,1,0:T(8,128)}, f32[36,32,768]{2,1,0:T(8,128)}) fusion(s32[]{:T(128)S(6)} %select_n.39, f32[36,32,768]{2,1,0:T(8,128)S(1)} %bitcast.35, s32[]{:T(128)S(6)} %select_n.41, s32[]{:T(128)S(6)} %select_n.40, s32[]{:T(128)S(6)} %select_n.42), kind=kLoop, calls=%fused_computation.17 | loop fusion | bytes 17694736 | tf_op jit(solution)/shard_map/dynamic_slice | solution.py:55
  249.7 9.1 %fusion.25 = f32[36,32,768]{2,1,0:T(8,128)S(1)} fusion(f32[36,32,768]{2,1,0:T(8,128)S(1)} %bitcast.36, s32[]{:T(128)S(6)} %select_n.56, f32[36,32,768]{2,1,0:T(8,128)} %get-tuple-element.23, s32[]{:T(128)S(6)} %select_n.54, f32[36,32,768]{2,1,0:T(8,128)} %get-tuple-element.21, s32[]{:T(128)S(6)} %select_n.52, f32[36,32,768]{2,1,0:T(8,128)} %get-tuple-element.22, ...), kind=kLoop, calls=%fused_computation.51 | loop fusion | flops 15040512 | bytes 21238288 | tf_op jit(solution)/shard_map/mul | solution.py:59
  259.3 81.2 %all_to_all.29 = f32[4,288,768]{2,1,0:T(8,128)S(1)} all-to-all(f32[4,288,768]{2,1,0:T(8,128)S(1)} %bitcast_add_fusion), channel_id=1, replica_groups=mesh['comp'=4,'lat'=8] {'comp'}, dimensions={0} | all-to-all | bytes 7077888 | tf_op jit(solution)/shard_map/all_to_all | solution.py:78
  340.5 2.2 copy.35
  342.7 5.5 %copy.33 = f32[3072,288]{1,0:T(8,128)} copy(f32[3072,288]{0,1:T(8,128)} %bitcast.40) | data formatting | bytes 7077888 | tf_op jit(solution)/shard_map/all_to_all | solution.py:78
  348.2 16.8 %scatter_custom_fusion = f32[288,4096]{0,1:T(8,128)} fusion(s32[3072]{0:T(1024)S(1)} %get-tuple-element.26, f32[3072,288]{1,0:T(8,128)} %copy.33, f32[]{:T(128)} %constant.50.clone.1), kind=kCustom, calls=%fused_computation.57 | custom fusion | bytes 4719104 | tf_op jit(solution)/shard_map/scatter | solution.py:79
  365.0 7.9 %copy.34 = f32[288,2,2048]{2,1,0:T(2,128)} copy(f32[288,2,2048]{0,2,1:T(8,128)} %bitcast.37) | data formatting | bytes 9437184 | tf_op jit(solution)/shard_map/reshape | solution.py:80
  (24 shorter events, 1.3 us)
Async XLA Ops:
  5.1 8.1 %copy-start.3 = (f32[288]{0:T(512)S(1)}, f32[288]{0:T(512)}, u32[]{:S(2)}) copy-start(f32[288]{0:T(512)} %param.10) | copy-start | bytes 3460
  5.1 8.1 %copy-start.4 = (f32[288]{0:T(512)S(1)}, f32[288]{0:T(512)}, u32[]{:S(2)}) copy-start(f32[288]{0:T(512)} %param.9) | copy-start | bytes 3460
  5.1 8.3 %copy-start.1 = (s32[2,2048]{1,0:T(2,128)S(1)}, s32[2,2048]{1,0:T(2,128)}, u32[]{:S(2)}) copy-start(s32[2,2048]{1,0:T(2,128)} %param.11) | copy-start | bytes 49156
  7.6 30.4 %collective-permute-start = (f32[288,1,2048]{2,0,1:T(8,128)}, f32[288,1,2048]{2,0,1:T(8,128)S(1)}, u32[]{:S(2)}, u32[]{:S(2)}) collective-permute-start(f32[288,1,2048]{2,0,1:T(8,128)} %get-tuple-element.18), channel_id=1, source_target_pairs={{0,1},{1,2},{2,3},{3,4},{4,5},{5,6},{6,7},{8,9},{9,10},{10,11},{11... | collective-permute-start | bytes 7077896 | tf_op jit(solution)/shard_map/ppermute | solution.py:22
  9.5 52.8 %collective-permute-start.1 = (f32[288,1,2048]{2,0,1:T(8,128)}, f32[288,1,2048]{2,0,1:T(8,128)}, u32[]{:S(2)}, u32[]{:S(2)}) collective-permute-start(f32[288,1,2048]{2,0,1:T(8,128)} %get-tuple-element.19), channel_id=1, source_target_pairs={{1,0},{2,1},{3,2},{4,3},{5,4},{6,5},{7,6},{9,8},{10,9},{11,10},{12... | collective-permute-start | bytes 7077896 | tf_op jit(solution)/shard_map/ppermute | solution.py:24
  67.2 3.6 copy-start
  70.8 30.5 %collective-permute-start.2 = (f32[288,1,2048]{2,0,1:T(8,128)}, f32[288,1,2048]{2,0,1:T(8,128)S(1)}, u32[]{:S(2)}, u32[]{:S(2)}) collective-permute-start(f32[288,1,2048]{2,0,1:T(8,128)} %get-tuple-element.12), channel_id=1, source_target_pairs={{0,1},{1,2},{2,3},{3,4},{4,5},{5,6},{6,7},{8,9},{9,10},{10,11},{11... | collective-permute-start | bytes 7077896 | tf_op jit(solution)/shard_map/ppermute | solution.py:22
  74.4 51.3 %collective-permute-start.3 = (f32[288,1,2048]{2,0,1:T(8,128)}, f32[288,1,2048]{2,0,1:T(8,128)}, u32[]{:S(2)}, u32[]{:S(2)}) collective-permute-start(f32[288,1,2048]{2,0,1:T(8,128)} %get-tuple-element.13), channel_id=1, source_target_pairs={{1,0},{2,1},{3,2},{4,3},{5,4},{6,5},{7,6},{9,8},{10,9},{11,10},{12... | collective-permute-start | bytes 7077896 | tf_op jit(solution)/shard_map/ppermute | solution.py:24
  82.5 43.2 %slice-start = ((s8[4718592]{0:T(1024)(128)(4,1)}), s8[4194304]{0:T(1024)(128)(4,1)S(1)}, s32[]{:S(2)}) async-start(s8[4718592]{0:T(1024)(128)(4,1)} %bitcast.33), calls=%async_computation.2 | async-start | bytes 8388608
  83.9 41.8 %slice-start.1 = ((s8[4718592]{0:T(1024)(128)(4,1)}), s8[524288]{0:T(1024)(128)(4,1)S(1)}, s32[]{:S(2)}) async-start(s8[4718592]{0:T(1024)(128)(4,1)} %bitcast.33), calls=%async_computation.3 | async-start | bytes 1048576
  160.0 5.0 %copy-start.2 = (s32[4,2]{0,1:T(2,128)S(1)}, s32[4,2]{0,1:T(2,128)}, u32[]{:S(2)}) copy-start(s32[4,2]{0,1:T(2,128)} %param.13) | copy-start | bytes 100
  160.0 83.1 %all-to-all-start = ((f32[288,4,768]{2,0,1:T(8,128)}), f32[288,4,768]{2,0,1:T(8,128)S(1)}, u32[]{:S(2)}, u32[]{:S(2)}) async-start(f32[288,4,768]{2,0,1:T(8,128)} %broadcast_select_fusion), calls=%async_computation | async-start | bytes 7077888 | tf_op jit(solution)/shard_map/all_to_all | solution.py:76
where the time goes:
time: 374 us; the launch traced here: 373 us
  waiting for transfers between devices  151 us (40%)
  local copies, waits for them, and re-layouts  87.1 us (23%)
  blocking collectives  81.2 us (22%)
  other arithmetic  28.6 us (8%)
  starting transfers between devices  16.5 us (4%)
  between operations  8.04 us (2%)
    all_to_all x1, blocking collectives, per_device(): lax.all_to_all(updated, 'comp', split_axis=0, concat_axis=1, tiled=True)  81.2 us
    all_to_all x1, waiting for transfers between devices, per_device(): lax.all_to_all(packed, 'comp', split_axis=1, concat_axis=0, tiled=True)  68.2 us
    ppermute x2, waiting for transfers between devices, extended(): lax.ppermute(head, axis, [((i + 1) % count, i) for i in range(ends)])  48.8 us
    ppermute x2, waiting for transfers between devices, extended(): lax.ppermute(tail, axis, [(i, (i + 1) % count) for i in range(ends)])  34.5 us
    gather x2, local copies, waits for them, and re-layouts, per_device(): packed = jnp.take(flat, chosen, axis=1)  19.6 us
    scatter x1, local copies, waits for them, and re-layouts, per_device(): jnp.zeros((comp_dev, point_count), jnp.float32).at[:, chosen].set(returned)  16.8 us
    mul x2, other arithmetic, upwind(): return moved * maskf  11.1 us
    mul x1, other arithmetic, interact(): return (coeff * grid * total).reshape(energy.shape)  9.11 us
  transfers between devices with their start and end apart: 5, of which 5 were waited for; matrix products, arithmetic and copies ran while one was open for 5% of the time, Pallas kernels for 0%

commit v1 on v0

--- a/solution.py
+++ b/solution.py
@@ -2,6 +2,8 @@
 import jax.numpy as jnp
 from jax import lax
 from jax.sharding import PartitionSpec as P
+from jax.experimental import pallas as pl
+from jax.experimental.pallas import tpu as pltpu
 
 NF = 36
 ND = 32
@@ -59,7 +61,7 @@
     return (coeff * grid * total).reshape(energy.shape)
 
 
-def per_device(spectrum, courant_lat, courant_lon, sea_mask, strength, quad_shift):
+def gathered_plan(spectrum, courant_lat, courant_lon, sea_mask, strength, quad_shift):
     maskf = sea_mask.astype(jnp.float32)[None]
     along_lat = courant_lat[:, None, None]
     along_lon = courant_lon[:, None, None]
@@ -80,6 +82,304 @@
     return result.reshape(comp_dev, lat_dev, lon_count)
 
 
+LANES = 128
+PAIR = 2
+
+
+def vmem(shape):
+    return pltpu.VMEM(shape, jnp.float32)
+
+
+def near_core(cells):
+    return pltpu.with_memory_space_constraint(cells, pltpu.VMEM)
+
+
+def whole(space):
+    return pl.BlockSpec(memory_space=space)
+
+
+def limits(mib):
+    return pltpu.CompilerParams(vmem_limit_bytes=mib * 2**20)
+
+
+def cost(flops, count):
+    return pl.CostEstimate(flops=flops, bytes_accessed=count, transcendentals=0)
+
+
+def tiled(cells):
+    comp_dev, lat_dev, lon_count = cells.shape
+    blocks = lon_count // LANES
+    cells = cells.reshape(comp_dev, lat_dev, blocks, LANES).transpose(0, 2, 1, 3)
+    return cells.reshape(comp_dev, blocks * lat_dev, LANES)
+
+
+def untiled(cells, lat_dev):
+    comp_dev, rows, _ = cells.shape
+    blocks = rows // lat_dev
+    cells = cells.reshape(comp_dev, blocks, lat_dev, LANES).transpose(0, 2, 1, 3)
+    return cells.reshape(comp_dev, lat_dev, blocks * LANES)
+
+
+def load(own, chunks):
+    spots = [(c, n, f) for c, freqs in enumerate(chunks) for n, f in enumerate(freqs)]
+    rows = own.shape[1]
+
+    def kernel(own_ref, *refs):
+        sems = refs[-1]
+        copies = [
+            pltpu.make_async_copy(own_ref.at[pl.ds(f * ND, ND)], refs[c].at[pl.ds(n * ND, ND)], sems.at[m])
+            for m, (c, n, f) in enumerate(spots)
+        ]
+        for one in copies:
+            one.start()
+        for one in copies:
+            one.wait()
+
+    return pl.pallas_call(
+        kernel,
+        out_shape=[vmem((len(freqs) * ND, rows, LANES)) for freqs in chunks],
+        in_specs=[whole(pltpu.HBM)],
+        out_specs=[whole(pltpu.VMEM)] * len(chunks),
+        scratch_shapes=[pltpu.SemaphoreType.DMA((len(spots),))],
+        compiler_params=limits(8),
+        cost_estimate=cost(0, 2 * len(spots) * ND * rows * LANES * 4),
+        name="load",
+    )(pltpu.with_memory_space_constraint(own, pltpu.HBM))
+
+
+def pack_message(own, mate, along_lat, place, freqs):
+    rows = own.shape[1]
+
+    def kernel(a_ref, place_ref, own_ref, mate_ref, out_ref):
+        odd = place_ref[0] > 0
+        for n, f in enumerate(freqs):
+            def one(i, carry):
+                k = f * ND + i
+                j = n * ND + i
+                from_own = (a_ref[k] > 0) == odd
+                out_ref[j] = jnp.where(from_own, own_ref[j], mate_ref[j])
+                return carry
+
+            lax.fori_loop(0, ND, one, 0, unroll=4)
+
+    return pl.pallas_call(
+        kernel,
+        out_shape=vmem((len(freqs) * ND, rows, LANES)),
+        in_specs=[whole(pltpu.SMEM)] * 2 + [whole(pltpu.VMEM)] * 2,
+        out_specs=whole(pltpu.VMEM),
+        compiler_params=limits(8),
+        cost_estimate=cost(0, 3 * len(freqs) * ND * rows * LANES * 4),
+        name="pack_message",
+    )(along_lat, place, near_core(own), near_core(mate))
+
+
+def propagate(own, mate, side, relay, along_lat, along_lon, place, masks, freqs):
+    rows = own.shape[1]
+    half = rows // PAIR
+
+    def kernel(a_ref, b_ref, place_ref, mask_ref, own_ref, mate_ref, side_ref, relay_ref, *out_refs):
+        odd = place_ref[0] > 0
+        relayed = place_ref[1] > 0
+        lane = lax.broadcasted_iota(jnp.int32, (half, LANES), 1)
+
+        def run(far_ref):
+            for n, f in enumerate(freqs):
+                def one(i, carry):
+                    k = f * ND + i
+                    j = n * ND + i
+                    a = a_ref[k]
+                    b = b_ref[k]
+                    south = a > 0
+                    near = south == odd
+                    west = b > 0
+                    fore = jnp.where(south, 0, 1)
+                    back = 1 - fore
+                    turn = jnp.where(west, 1, LANES - 1)
+                    edge = lane == jnp.where(west, 0, LANES - 1)
+                    a = jnp.abs(a)
+                    b = jnp.abs(b)
+
+                    def row(ref, at, which):
+                        return ref[at, pl.ds(which, half, stride=PAIR), :]
+
+                    def beside(x):
+                        turned = pltpu.roll(x, turn, 1)
+                        over = jnp.where(west, pltpu.roll(turned, 1, 0), pltpu.roll(turned, half - 1, 0))
+                        return jnp.where(edge, over, turned)
+
+                    def moved(x, before, mask):
+                        return (x - a * (x - before) - b * (x - beside(x))) * mask
+
+                    x0 = jnp.where(near, row(mate_ref, j, fore), row(far_ref, j, fore))
+                    x1 = jnp.where(near, row(mate_ref, j, back), row(far_ref, j, back))
+                    x2 = row(own_ref, j, fore)
+                    x3 = row(own_ref, j, back)
+                    y1 = moved(x1, x0, mask_ref[2 + fore])
+                    y2 = moved(x2, x1, mask_ref[fore])
+                    y3 = moved(x3, x2, mask_ref[back])
+                    z2 = moved(y2, y1, mask_ref[fore])
+                    z3 = moved(y3, y2, mask_ref[back])
+                    out_refs[n][i, pl.ds(fore, half, stride=PAIR), :] = z2
+                    out_refs[n][i, pl.ds(back, half, stride=PAIR), :] = z3
+                    return carry
+
+                lax.fori_loop(0, ND, one, 0, unroll=2)
+
+        @pl.when(relayed)
+        def _():
+            run(relay_ref)
+
+        @pl.when(jnp.logical_not(relayed))
+        def _():
+            run(side_ref)
+
+    operands = [along_lat, along_lon, place] + [near_core(x) for x in (masks, own, mate, side, relay)]
+    in_specs = [whole(pltpu.SMEM)] * 3 + [whole(pltpu.VMEM)] * 5
+    return pl.pallas_call(
+        kernel,
+        out_shape=[vmem((ND, rows, LANES))] * len(freqs),
+        in_specs=in_specs,
+        out_specs=[whole(pltpu.VMEM)] * len(freqs),
+        compiler_params=limits(8),
+        cost_estimate=cost(40 * len(freqs) * ND * rows * LANES, 5 * len(freqs) * ND * rows * LANES * 4),
+        name="propagate",
+    )(*operands)
+
+
+def quadruplets(window, parts, places, local, strength, shifts, first, freqs, into):
+    rows = parts[0].shape[1]
+    count = len(parts)
+
+    def kernel(strength_ref, shift_ref, first_ref, *refs):
+        part_refs = refs[:count]
+        held_ref, out_ref, done, sems, part_sems = refs[-5:]
+        arrivals = [
+            pltpu.make_async_copy(part_refs[n], held_ref.at[pl.ds(place * ND, ND)], part_sems.at[n])
+            for n, place in enumerate(places)
+        ]
+        for one in arrivals:
+            one.start()
+        for one in arrivals:
+            one.wait()
+        base = first_ref[0]
+        copies = []
+        for n, f in enumerate(freqs):
+            def one(d, carry):
+                energy = held_ref[(f + reach) * ND + d]
+                total = jnp.zeros_like(energy)
+                for q in range(NQ):
+                    turned = lax.rem(d + shift_ref[1, q] + ND, ND)
+                    partner = held_ref[(f + reach + shift_ref[0, q]) * ND + turned]
+                    total = total + partner * (partner - energy)
+                done[n * ND + d] = energy + strength_ref[base + f * ND + d] * energy * total
+                return carry
+
+            lax.fori_loop(0, ND, one, 0, unroll=4)
+            copies.append(
+                pltpu.make_async_copy(done.at[pl.ds(n * ND, ND)], out_ref.at[pl.ds(f * ND, ND)], sems.at[n])
+            )
+            copies[-1].start()
+        for one in copies:
+            one.wait()
+
+    operands = [strength, shifts, first] + parts
+    in_specs = [whole(pltpu.SMEM)] * 3 + [whole(pl.ANY)] * count
+    aliases = {}
+    if window is not None:
+        aliases = {len(operands): 0, len(operands) + 1: 1}
+        operands += [near_core(window), into]
+        in_specs += [whole(pltpu.VMEM), whole(pl.ANY)]
+    return pl.pallas_call(
+        kernel,
+        out_shape=[
+            vmem(((local + 2 * reach) * ND, rows, LANES)),
+            jax.ShapeDtypeStruct((local * ND, rows, LANES), jnp.float32),
+        ],
+        in_specs=in_specs,
+        out_specs=[whole(pltpu.VMEM), whole(pl.ANY)],
+        scratch_shapes=[
+            pltpu.VMEM((len(freqs) * ND, rows, LANES), jnp.float32),
+            pltpu.SemaphoreType.DMA((len(freqs),)),
+            pltpu.SemaphoreType.DMA((count,)),
+        ],
+        input_output_aliases=aliases,
+        compiler_params=limits(8),
+        cost_estimate=cost(15 * len(freqs) * ND * rows * LANES, 6 * len(freqs) * ND * rows * LANES * 4),
+        name="quadruplets",
+    )(*operands)
+
+
+def halo_plan(spectrum, courant_lat, courant_lon, sea_mask, strength, quad_shift):
+    comp_dev, lat_dev, _ = spectrum.shape
+    local = comp_dev // ND
+    lat_count = lax.axis_size("lat")
+    comp_count = lax.axis_size("comp")
+    at = lax.axis_index("lat")
+    first = (lax.axis_index("comp") * comp_dev)[None].astype(jnp.int32)
+    mates = [(i, i ^ 1) for i in range(lat_count)]
+    sides = [(i, i + 1) for i in range(1, lat_count, 4)] + [(i + 1, i) for i in range(1, lat_count, 4)]
+    relays = [(i - 2, i + 1) for i in range(3, lat_count - 1, 4)] + [(i + 3, i) for i in range(3, lat_count - 1, 4)]
+    place = jnp.stack([at % 2, jnp.where((at % 4 == 0) | (at % 4 == 3), 1, 0)]).astype(jnp.int32)
+    up = [(i, i + 1) for i in range(lat_count - 1)]
+    down = [(i + 1, i) for i in range(lat_count - 1)]
+    z_up = [(i, i + 1) for i in range(comp_count - 1)]
+    z_down = [(i + 1, i) for i in range(comp_count - 1)]
+
+    own = tiled(spectrum)
+    rows = own.shape[1]
+    maskf = sea_mask.astype(jnp.float32).reshape(lat_dev, rows // lat_dev, LANES)
+
+    pairs = [(c, local - 1 - c) for c in range(reach)]
+    middle = list(range(reach, local - reach))
+    chunks = [list(pair) for pair in pairs] + ([middle] if middle else [])
+    owns = load(own, chunks[:1]) + load(own, chunks[1:])
+    mask_south = lax.ppermute(maskf[1:], "lat", up)
+    mask_north = lax.ppermute(maskf[:1], "lat", down)
+    masks = jnp.concatenate([maskf, mask_south, mask_north])
+    mates_in = [lax.ppermute(part, "lat", mates) for part in owns]
+    sides_in = [
+        lax.ppermute(pack_message(owns[n], mates_in[n], courant_lat, place, freqs), "lat", sides)
+        for n, freqs in enumerate(chunks)
+    ]
+    relays_in = [lax.ppermute(side, "lat", relays) for side in sides_in]
+    parts = []
+    places = []
+    last = []
+    for n, freqs in enumerate(chunks):
+        made = propagate(
+            owns[n], mates_in[n], sides_in[n], relays_in[n], courant_lat, courant_lon, place, masks, freqs
+        )
+        parts += made
+        places += [reach + f for f in freqs]
+        if n < reach:
+            low, high = made
+            last = [lax.ppermute(high, "comp", z_up), lax.ppermute(low, "comp", z_down)]
+            last_places = [reach - 1 - n, reach + local + n]
+            if n < reach - 1:
+                parts += last
+                places += last_places
+    shifts = quad_shift.T
+    window, inner = quadruplets(
+        None, parts, places, local, strength, shifts, first, list(range(1, local - 1)), None
+    )
+    window, result = quadruplets(
+        window, last, last_places, local, strength, shifts, first, [0, local - 1], inner
+    )
+    return untiled(result, lat_dev)
+
+
+def fits(comp_dev, lat_count, lat_dev, lon_count):
+    local, left = divmod(comp_dev, ND)
+    return left == 0 and 0 < local - 2 * reach <= 1 and lat_count % 4 == 0 and lat_dev == 2 and lon_count % LANES == 0
+
+
+def per_device(spectrum, courant_lat, courant_lon, sea_mask, strength, quad_shift):
+    comp_dev, lat_dev, lon_count = spectrum.shape
+    if fits(comp_dev, lax.axis_size("lat"), lat_dev, lon_count):
+        return halo_plan(spectrum, courant_lat, courant_lon, sea_mask, strength, quad_shift)
+    return gathered_plan(spectrum, courant_lat, courant_lon, sea_mask, strength, quad_shift)
+
+
 def solution(mesh):
     return jax.shard_map(
         per_device,

time: 374 us -> 161 us (0.43)
  the two profiles are of different devices: /device:TPU:2 before, /device:TPU:19 now
where the time goes in v1:
time: 161 us; the launch traced here: 159 us
  starting transfers between devices  70.3 us (44%)
  Pallas kernels  53.7 us (33%)
  waiting for transfers between devices  23.8 us (15%)
  local copies, waits for them, and re-layouts  10.8 us (7%)
    ppermute x5, starting transfers between devices, halo_plan(): mates_in = [lax.ppermute(part, 'lat', mates) for part in owns]  32.7 us
    pallas_call x5, Pallas kernels, propagate(): pl.pallas_call(kernel, out_shape=[vmem((ND, rows, LANES))] * len(freqs),...  32.2 us
    ppermute x8, starting transfers between devices, halo_plan(): last = [lax.ppermute(high, 'comp', z_up), lax.ppermute(low, 'comp', z_down)]  22 us
    ppermute x5, waiting for transfers between devices, halo_plan(): relays_in = [lax.ppermute(side, 'lat', relays) for side in sides_in]  12.7 us
    unnamed x54, local copies, waits for them, and re-layouts  10.8 us
    pallas_call x2, Pallas kernels, quadruplets(): pl.pallas_call(kernel, out_shape=[vmem(((local + 2 * reach) * ND, rows, L...  10 us
    ppermute x1, waiting for transfers between devices, halo_plan(): mask_south = lax.ppermute(maskf[1:], 'lat', up)  7.77 us
    pallas_call x5, Pallas kernels, pack_message(): pl.pallas_call(kernel, out_shape=vmem((len(freqs) * ND, rows, LANES)), in...  6.88 us
  transfers between devices with their start and end apart: 25, of which 6 were waited for; matrix products, arithmetic and copies ran while one was open for 0% of the time, Pallas kernels for 31%

profile of v1, /device:TPU:19, one launch (start us, length us, event | category | flops | bytes accessed | tf_op | source)
XLA Modules:
  0.0 159.3 jit_solution(11694686229586590293)
XLA Ops:
  2.0 3.4 %load.2 = (f32[64,32,128]{2,1,0:T(8,128)}, f32[64,32,128]{2,1,0:T(8,128)}, f32[64,32,128]{2,1,0:T(8,128)S(1)}, f32[32,32,128]{2,1,0:T(8,128)S(1)}) custom-call(f32[288,32,128]{2,1,0:T(8,128)} %bitcast.23), custom_call_target="tpu_custom_call" | custom-call | bytes 7340032 | tf_op jit(solution)/shard_map/load/pallas_call | solution.py:138
  6.8 1.5 pack_message.6
  9.3 1.9 %pack_message.7 = f32[64,32,128]{2,1,0:T(8,128)S(1)} custom-call(f32[288]{0:T(512)S(1)} %copy-done.21, s32[2]{0:T(128)S(1)} %pad_add_fusion.place_ref, f32[64,32,128]{2,1,0:T(8,128)} %get-tuple-element.25.own_ref, f32[64,32,128]{2,1,0:T(8,128)} %collective-permute-done.12.mate_ref), custom_call_target="tpu_custom_call" | custom-call | bytes 3145728 | tf_op jit(solution)/shard_map/pack_message/pallas_call | solution.py:165
  11.9 1.9 %pack_message.8 = f32[64,32,128]{2,1,0:T(8,128)S(1)} custom-call(f32[288]{0:T(512)S(1)} %copy-done.21, s32[2]{0:T(128)S(1)} %pad_add_fusion.place_ref, f32[64,32,128]{2,1,0:T(8,128)} %get-tuple-element.28.own_ref, f32[64,32,128]{2,1,0:T(8,128)} %collective-permute-done.17.mate_ref), custom_call_target="tpu_custom_call" | custom-call | bytes 3145728 | tf_op jit(solution)/shard_map/pack_message/pallas_call | solution.py:165
  16.2 3.5 %collective-permute-start = (f32[1,16,128]{2,1,0:T(8,128)S(1)}, f32[1,16,128]{2,1,0:T(8,128)S(1)}, u32[]{:S(2)}, u32[]{:S(2)}) collective-permute-start(f32[1,16,128]{2,1,0:T(8,128)S(1)} %bitcast.25), channel_id=1, source_target_pairs={{0,1},{1,2},{2,3},{3,4},{4,5},{5,6},{6,7},{8,9},{9,10},{10,11},{11... | collective-permute-start | bytes 24584 | tf_op jit(solution)/shard_map/ppermute | solution.py:336
  19.7 7.8 %collective-permute-done = f32[1,16,128]{2,1,0:T(8,128)S(1)} collective-permute-done((f32[1,16,128]{2,1,0:T(8,128)S(1)}, f32[1,16,128]{2,1,0:T(8,128)S(1)}, u32[]{:S(2)}, u32[]{:S(2)}) %collective-permute-start) | collective-permute-done | bytes 8224 | tf_op jit(solution)/shard_map/ppermute | solution.py:336
  27.5 31.5 %collective-permute-start.22 = (f32[32,32,128]{2,1,0:T(8,128)S(1)}, f32[32,32,128]{2,1,0:T(8,128)S(1)}, u32[]{:S(2)}, u32[]{:S(2)}) collective-permute-start(f32[32,32,128]{2,1,0:T(8,128)S(1)} %copy-done.1), channel_id=1, source_target_pairs={{0,1},{1,0},{2,3},{3,2},{4,5},{5,4},{6,7},{7,6},{8,9},{9,8},{10,11... | collective-permute-start | bytes 1572872 | tf_op jit(solution)/shard_map/ppermute | solution.py:339
  58.9 1.3 collective-permute-start.9
  60.2 1.3 collective-permute-start.14
  61.5 1.3 collective-permute-start.19
  62.9 1.9 %collective-permute-start.1 = (f32[1,16,128]{2,1,0:T(8,128)S(1)}, f32[1,16,128]{2,1,0:T(8,128)S(1)}, u32[]{:S(2)}, u32[]{:S(2)}) collective-permute-start(f32[1,16,128]{2,1,0:T(8,128)S(1)} %bitcast.24), channel_id=1, source_target_pairs={{1,0},{2,1},{3,2},{4,3},{5,4},{6,5},{7,6},{9,8},{10,9},{11,10},{12... | collective-permute-start | bytes 24584 | tf_op jit(solution)/shard_map/ppermute | solution.py:337
  65.5 3.3 %collective-permute-done.1 = f32[1,16,128]{2,1,0:T(8,128)S(1)} collective-permute-done((f32[1,16,128]{2,1,0:T(8,128)S(1)}, f32[1,16,128]{2,1,0:T(8,128)S(1)}, u32[]{:S(2)}, u32[]{:S(2)}) %collective-permute-start.1) | collective-permute-done | bytes 8224 | tf_op jit(solution)/shard_map/ppermute | solution.py:337
  69.5 1.3 collective-permute-start.4
  70.9 1.3 collective-permute-start.24
  72.2 3.2 %collective-permute-done.9.relay_ref = f32[64,32,128]{2,1,0:T(8,128)S(1)} collective-permute-done((f32[64,32,128]{2,1,0:T(8,128)S(1)}, f32[64,32,128]{2,1,0:T(8,128)S(1)}, u32[]{:S(2)}, u32[]{:S(2)}) %collective-permute-start.9) | collective-permute-done | bytes 1048608 | tf_op jit(solution)/shard_map/ppermute | solution.py:344
  75.4 6.5 %propagate.6 = (f32[32,32,128]{2,1,0:T(8,128)S(1)}, f32[32,32,128]{2,1,0:T(8,128)S(1)}) custom-call(f32[288]{0:T(512)S(1)} %copy-done.21, f32[288]{0:T(512)S(1)} %copy-done.22, s32[2]{0:T(128)S(1)} %pad_add_fusion.place_ref, f32[4,16,128]{2,1,0:T(8,128)S(1)} %constant_dynamic-update-slice_fusion.mask_ref, f32[64,32,128]{2,1,0:T(8,128)S(1)} %load.3.own_ref, ...), custom_call_target="tpu_custom_call" | custom-call | flops 10485760 | bytes 5242880 | tf_op jit(solution)/shard_map/propagate/pallas_call | solution.py:238
  82.0 2.1 %collective-permute-start.11 = (f32[32,32,128]{2,1,0:T(8,128)S(1)}, f32[32,32,128]{2,1,0:T(8,128)S(1)}, u32[]{:S(2)}, u32[]{:S(2)}) collective-permute-start(f32[32,32,128]{2,1,0:T(8,128)S(1)} %get-tuple-element.23.refs_0_), channel_id=1, source_target_pairs={{8,0},{16,8},{24,16},{9,1},{17,9},{25,17},{10,2},{18,10},{26,18},{... | collective-permute-start | bytes 1572872 | tf_op jit(solution)/shard_map/ppermute | solution.py:356
  84.1 2.3 %collective-permute-done.14.relay_ref = f32[64,32,128]{2,1,0:T(8,128)S(1)} collective-permute-done((f32[64,32,128]{2,1,0:T(8,128)S(1)}, f32[64,32,128]{2,1,0:T(8,128)S(1)}, u32[]{:S(2)}, u32[]{:S(2)}) %collective-permute-start.14) | collective-permute-done | bytes 1048608 | tf_op jit(solution)/shard_map/ppermute | solution.py:344
  86.4 3.2 %collective-permute-start.10 = (f32[32,32,128]{2,1,0:T(8,128)S(1)}, f32[32,32,128]{2,1,0:T(8,128)S(1)}, u32[]{:S(2)}, u32[]{:S(2)}) collective-permute-start(f32[32,32,128]{2,1,0:T(8,128)S(1)} %get-tuple-element.24.refs_1_), channel_id=1, source_target_pairs={{0,8},{8,16},{16,24},{1,9},{9,17},{17,25},{2,10},{10,18},{18,26},{... | collective-permute-start | bytes 1572872 | tf_op jit(solution)/shard_map/ppermute | solution.py:356
  89.6 7.7 %propagate.7 = (f32[32,32,128]{2,1,0:T(8,128)S(1)}, f32[32,32,128]{2,1,0:T(8,128)}) custom-call(f32[288]{0:T(512)S(1)} %copy-done.21, f32[288]{0:T(512)S(1)} %copy-done.22, s32[2]{0:T(128)S(1)} %pad_add_fusion.place_ref, f32[4,16,128]{2,1,0:T(8,128)S(1)} %constant_dynamic-update-slice_fusion.mask_ref, f32[64,32,128]{2,1,0:T(8,128)} %get-tuple-element.25.own_ref, ...), custom_call_target="tpu_custom_call" | custom-call | flops 10485760 | bytes 5242880 | tf_op jit(solution)/shard_map/propagate/pallas_call | solution.py:238
  97.9 2.2 %collective-permute-start.16 = (f32[32,32,128]{2,1,0:T(8,128)S(1)}, f32[32,32,128]{2,1,0:T(8,128)S(1)}, u32[]{:S(2)}, u32[]{:S(2)}) collective-permute-start(f32[32,32,128]{2,1,0:T(8,128)S(1)} %get-tuple-element.26.refs_4_), channel_id=1, source_target_pairs={{8,0},{16,8},{24,16},{9,1},{17,9},{25,17},{10,2},{18,10},{26,18},{... | collective-permute-start | bytes 1572872 | tf_op jit(solution)/shard_map/ppermute | solution.py:356
  100.1 7.9 %propagate.8 = (f32[32,32,128]{2,1,0:T(8,128)}, f32[32,32,128]{2,1,0:T(8,128)}) custom-call(f32[288]{0:T(512)S(1)} %copy-done.21, f32[288]{0:T(512)S(1)} %copy-done.22, s32[2]{0:T(128)S(1)} %pad_add_fusion.place_ref, f32[4,16,128]{2,1,0:T(8,128)S(1)} %constant_dynamic-update-slice_fusion.mask_ref, f32[64,32,128]{2,1,0:T(8,128)} %get-tuple-element.28.own_ref, ...), custom_call_target="tpu_custom_call" | custom-call | flops 10485760 | bytes 5242880 | tf_op jit(solution)/shard_map/propagate/pallas_call | solution.py:238
  108.0 6.5 %collective-permute-done.24.relay_ref = f32[32,32,128]{2,1,0:T(8,128)S(1)} collective-permute-done((f32[32,32,128]{2,1,0:T(8,128)S(1)}, f32[32,32,128]{2,1,0:T(8,128)S(1)}, u32[]{:S(2)}, u32[]{:S(2)}) %collective-permute-start.24) | collective-permute-done | bytes 524320 | tf_op jit(solution)/shard_map/ppermute | solution.py:344
  114.5 3.2 %collective-permute-start.15 = (f32[32,32,128]{2,1,0:T(8,128)}, f32[32,32,128]{2,1,0:T(8,128)}, u32[]{:S(2)}, u32[]{:S(2)}) collective-permute-start(f32[32,32,128]{2,1,0:T(8,128)} %get-tuple-element.27.refs_5_), channel_id=1, source_target_pairs={{0,8},{8,16},{16,24},{1,9},{9,17},{17,25},{2,10},{10,18},{18,26},{... | collective-permute-start | bytes 1572872 | tf_op jit(solution)/shard_map/ppermute | solution.py:356
  117.7 2.1 %collective-permute-start.21 = (f32[32,32,128]{2,1,0:T(8,128)}, f32[32,32,128]{2,1,0:T(8,128)}, u32[]{:S(2)}, u32[]{:S(2)}) collective-permute-start(f32[32,32,128]{2,1,0:T(8,128)} %get-tuple-element.29.refs_8_), channel_id=1, source_target_pairs={{8,0},{16,8},{24,16},{9,1},{17,9},{25,17},{10,2},{18,10},{26,18},{... | collective-permute-start | bytes 1572872 | tf_op jit(solution)/shard_map/ppermute | solution.py:356
  119.8 4.0 %collective-permute-start.20 = (f32[32,32,128]{2,1,0:T(8,128)}, f32[32,32,128]{2,1,0:T(8,128)}, u32[]{:S(2)}, u32[]{:S(2)}) collective-permute-start(f32[32,32,128]{2,1,0:T(8,128)} %get-tuple-element.30.refs_9_), channel_id=1, source_target_pairs={{0,8},{8,16},{16,24},{1,9},{9,17},{17,25},{2,10},{10,18},{18,26},{... | collective-permute-start | bytes 1572872 | tf_op jit(solution)/shard_map/ppermute | solution.py:356
  123.8 6.9 %propagate.5 = (f32[32,32,128]{2,1,0:T(8,128)}, f32[32,32,128]{2,1,0:T(8,128)}) custom-call(f32[288]{0:T(512)S(1)} %copy-done.21, f32[288]{0:T(512)S(1)} %copy-done.22, s32[2]{0:T(128)S(1)} %pad_add_fusion.place_ref, f32[4,16,128]{2,1,0:T(8,128)S(1)} %constant_dynamic-update-slice_fusion.mask_ref, f32[64,32,128]{2,1,0:T(8,128)S(1)} %get-tuple-element.20.own_ref, ...), custom_call_target="tpu_custom_call" | custom-call | flops 10485760 | bytes 5242880 | tf_op jit(solution)/shard_map/propagate/pallas_call | solution.py:238
  131.5 1.9 %collective-permute-start.5 = (f32[32,32,128]{2,1,0:T(8,128)}, f32[32,32,128]{2,1,0:T(8,128)S(1)}, u32[]{:S(2)}, u32[]{:S(2)}) collective-permute-start(f32[32,32,128]{2,1,0:T(8,128)} %get-tuple-element.21.refs_13_), channel_id=1, source_target_pairs={{0,8},{8,16},{16,24},{1,9},{9,17},{17,25},{2,10},{10,18},{18,26},{... | collective-permute-start | bytes 1572872 | tf_op jit(solution)/shard_map/ppermute | solution.py:356
  134.2 3.3 %collective-permute-start.6 = (f32[32,32,128]{2,1,0:T(8,128)}, f32[32,32,128]{2,1,0:T(8,128)S(1)}, u32[]{:S(2)}, u32[]{:S(2)}) collective-permute-start(f32[32,32,128]{2,1,0:T(8,128)} %get-tuple-element.22.refs_12_), channel_id=1, source_target_pairs={{8,0},{16,8},{24,16},{9,1},{17,9},{25,17},{10,2},{18,10},{26,18},{... | collective-permute-start | bytes 1572872 | tf_op jit(solution)/shard_map/ppermute | solution.py:356
  139.7 3.3 %propagate.9.refs_14_ = f32[32,32,128]{2,1,0:T(8,128)S(1)} custom-call(f32[288]{0:T(512)S(1)} %copy-done.21, f32[288]{0:T(512)S(1)} %copy-done.22, s32[2]{0:T(128)S(1)} %pad_add_fusion.place_ref, f32[4,16,128]{2,1,0:T(8,128)S(1)} %constant_dynamic-update-slice_fusion.mask_ref, f32[32,32,128]{2,1,0:T(8,128)S(1)} %copy-done.2, f32[32,32,128]{2,1,0:T(8,128)S(1)} %copy-done.4, ...), custom_call_target="tpu_custom_call" | custom-call | flops 5242880 | bytes 2621440 | tf_op jit(solution)/shard_map/propagate/pallas_call | solution.py:238
  149.2 7.5 %quadruplets.2 = (f32[544,32,128]{2,1,0:T(8,128)S(1)}, f32[288,32,128]{2,1,0:T(8,128)}) custom-call(f32[1152]{0:T(1024)S(1)} %copy-done.23, s32[2,4]{1,0:T(2,128)S(1)} %bitcast.20, s32[1]{0:T(128)} %bitcast.1.first_ref, f32[32,32,128]{2,1,0:T(8,128)S(1)} %copy-done.6, f32[32,32,128]{2,1,0:T(8,128)S(1)} %copy-done.8, f32[32,32,128]{2,1,0:T(8,128)S(1)} %copy-done.12, ...), custom_call_target="tpu_custom_call" | custom-call | flops 13762560 | bytes 22020096 | tf_op jit(solution)/shard_map/quadruplets/pallas_call | solution.py:292
  156.7 2.5 %quadruplets.3 = (f32[544,32,128]{2,1,0:T(8,128)S(1)}, f32[288,32,128]{2,1,0:T(8,128)}) custom-call(f32[1152]{0:T(1024)S(1)} %copy-done.23, s32[2,4]{1,0:T(2,128)S(1)} %bitcast.21, s32[1]{0:T(128)} %bitcast.1.first_ref, f32[32,32,128]{2,1,0:T(8,128)S(1)} %collective-permute-done.5.refs_0_, ...), custom_call_target="tpu_custom_call", output_to_operand_aliasing={{0}: (5, {}), {1}: (6, {})} | custom-call | flops 3932160 | bytes 6291456 | tf_op jit(solution)/shard_map/quadruplets/pallas_call | solution.py:292
  (90 shorter events, 19.4 us)
Async XLA Ops:
  1.2 5.6 %collective-permute-start.7 = (f32[64,32,128]{2,1,0:T(8,128)S(1)}, f32[64,32,128]{2,1,0:T(8,128)}, u32[]{:S(2)}, u32[]{:S(2)}) collective-permute-start(f32[64,32,128]{2,1,0:T(8,128)S(1)} %load.3.own_ref), channel_id=1, source_target_pairs={{0,1},{1,0},{2,3},{3,2},{4,5},{5,4},{6,7},{7,6},{8,9},{9,8},{10,11... | collective-permute-start | bytes 3145736 | tf_op jit(solution)/shard_map/ppermute | solution.py:339
  6.2 3.1 %collective-permute-start.12 = (f32[64,32,128]{2,1,0:T(8,128)}, f32[64,32,128]{2,1,0:T(8,128)}, u32[]{:S(2)}, u32[]{:S(2)}) collective-permute-start(f32[64,32,128]{2,1,0:T(8,128)} %get-tuple-element.25.own_ref), channel_id=1, source_target_pairs={{0,1},{1,0},{2,3},{3,2},{4,5},{5,4},{6,7},{7,6},{8,9},{9,8},{10,11... | collective-permute-start | bytes 3145736 | tf_op jit(solution)/shard_map/ppermute | solution.py:339
  6.2 5.7 %collective-permute-start.17 = (f32[64,32,128]{2,1,0:T(8,128)}, f32[64,32,128]{2,1,0:T(8,128)}, u32[]{:S(2)}, u32[]{:S(2)}) collective-permute-start(f32[64,32,128]{2,1,0:T(8,128)} %get-tuple-element.28.own_ref), channel_id=1, source_target_pairs={{0,1},{1,0},{2,3},{3,2},{4,5},{5,4},{6,7},{7,6},{8,9},{9,8},{10,11... | collective-permute-start | bytes 3145736 | tf_op jit(solution)/shard_map/ppermute | solution.py:339
  6.7 7.8 %collective-permute-start.2 = (f32[64,32,128]{2,1,0:T(8,128)S(1)}, f32[64,32,128]{2,1,0:T(8,128)S(1)}, u32[]{:S(2)}, u32[]{:S(2)}) collective-permute-start(f32[64,32,128]{2,1,0:T(8,128)S(1)} %get-tuple-element.20.own_ref), channel_id=1, source_target_pairs={{0,1},{1,0},{2,3},{3,2},{4,5},{5,4},{6,7},{7,6},{8,9},{9,8},{10,11... | collective-permute-start | bytes 3145736 | tf_op jit(solution)/shard_map/ppermute | solution.py:339
  8.4 50.5 %collective-permute-start.8 = (f32[64,32,128]{2,1,0:T(8,128)S(1)}, f32[64,32,128]{2,1,0:T(8,128)S(1)}, u32[]{:S(2)}, u32[]{:S(2)}) collective-permute-start(f32[64,32,128]{2,1,0:T(8,128)S(1)} %pack_message.6), channel_id=1, source_target_pairs={{1,2},{5,6},{2,1},{6,5},{9,10},{13,14},{10,9},{14,13},{17,18},{21,... | collective-permute-start | bytes 3145736 | tf_op jit(solution)/shard_map/ppermute | solution.py:341
  11.1 64.3 %copy-start.22 = (f32[288]{0:T(512)S(1)}, f32[288]{0:T(512)}, u32[]{:S(2)}) copy-start(f32[288]{0:T(512)} %b_ref.9) | copy-start | bytes 3460
  11.2 49.1 %collective-permute-start.13 = (f32[64,32,128]{2,1,0:T(8,128)S(1)}, f32[64,32,128]{2,1,0:T(8,128)S(1)}, u32[]{:S(2)}, u32[]{:S(2)}) collective-permute-start(f32[64,32,128]{2,1,0:T(8,128)S(1)} %pack_message.7), channel_id=1, source_target_pairs={{1,2},{5,6},{2,1},{6,5},{9,10},{13,14},{10,9},{14,13},{17,18},{21,... | collective-permute-start | bytes 3145736 | tf_op jit(solution)/shard_map/ppermute | solution.py:341
  13.8 47.8 %collective-permute-start.18 = (f32[64,32,128]{2,1,0:T(8,128)S(1)}, f32[64,32,128]{2,1,0:T(8,128)S(1)}, u32[]{:S(2)}, u32[]{:S(2)}) collective-permute-start(f32[64,32,128]{2,1,0:T(8,128)S(1)} %pack_message.8), channel_id=1, source_target_pairs={{1,2},{5,6},{2,1},{6,5},{9,10},{13,14},{10,9},{14,13},{17,18},{21,... | collective-permute-start | bytes 3145736 | tf_op jit(solution)/shard_map/ppermute | solution.py:341
  15.4 54.1 %collective-permute-start.3 = (f32[64,32,128]{2,1,0:T(8,128)S(1)}, f32[64,32,128]{2,1,0:T(8,128)S(1)}, u32[]{:S(2)}, u32[]{:S(2)}) collective-permute-start(f32[64,32,128]{2,1,0:T(8,128)S(1)} %pack_message.5), channel_id=1, source_target_pairs={{1,2},{5,6},{2,1},{6,5},{9,10},{13,14},{10,9},{14,13},{17,18},{21,... | collective-permute-start | bytes 3145736 | tf_op jit(solution)/shard_map/ppermute | solution.py:341
  16.2 11.3 %collective-permute-start = (f32[1,16,128]{2,1,0:T(8,128)S(1)}, f32[1,16,128]{2,1,0:T(8,128)S(1)}, u32[]{:S(2)}, u32[]{:S(2)}) collective-permute-start(f32[1,16,128]{2,1,0:T(8,128)S(1)} %bitcast.25), channel_id=1, source_target_pairs={{0,1},{1,2},{2,3},{3,4},{4,5},{5,6},{6,7},{8,9},{9,10},{10,11},{11... | collective-permute-start | bytes 24584 | tf_op jit(solution)/shard_map/ppermute | solution.py:336
  27.5 35.4 %collective-permute-start.22 = (f32[32,32,128]{2,1,0:T(8,128)S(1)}, f32[32,32,128]{2,1,0:T(8,128)S(1)}, u32[]{:S(2)}, u32[]{:S(2)}) collective-permute-start(f32[32,32,128]{2,1,0:T(8,128)S(1)} %copy-done.1), channel_id=1, source_target_pairs={{0,1},{1,0},{2,3},{3,2},{4,5},{5,4},{6,7},{7,6},{8,9},{9,8},{10,11... | collective-permute-start | bytes 1572872 | tf_op jit(solution)/shard_map/ppermute | solution.py:339
  58.9 16.5 %collective-permute-start.9 = (f32[64,32,128]{2,1,0:T(8,128)S(1)}, f32[64,32,128]{2,1,0:T(8,128)S(1)}, u32[]{:S(2)}, u32[]{:S(2)}) collective-permute-start(f32[64,32,128]{2,1,0:T(8,128)S(1)} %collective-permute-done.8.side_ref), channel_id=1, source_target_pairs={{1,4},{6,3},{9,12},{14,11},{17,20},{22,19},{25,28},{30,27}} | collective-permute-start | bytes 3145736 | tf_op jit(solution)/shard_map/ppermute | solution.py:344
  60.2 26.1 %collective-permute-start.14 = (f32[64,32,128]{2,1,0:T(8,128)S(1)}, f32[64,32,128]{2,1,0:T(8,128)S(1)}, u32[]{:S(2)}, u32[]{:S(2)}) collective-permute-start(f32[64,32,128]{2,1,0:T(8,128)S(1)} %collective-permute-done.13.side_ref), channel_id=1, source_target_pairs={{1,4},{6,3},{9,12},{14,11},{17,20},{22,19},{25,28},{30,27}} | collective-permute-start | bytes 3145736 | tf_op jit(solution)/shard_map/ppermute | solution.py:344
  61.5 36.4 %collective-permute-start.19 = (f32[64,32,128]{2,1,0:T(8,128)S(1)}, f32[64,32,128]{2,1,0:T(8,128)S(1)}, u32[]{:S(2)}, u32[]{:S(2)}) collective-permute-start(f32[64,32,128]{2,1,0:T(8,128)S(1)} %collective-permute-done.18.side_ref), channel_id=1, source_target_pairs={{1,4},{6,3},{9,12},{14,11},{17,20},{22,19},{25,28},{30,27}} | collective-permute-start | bytes 3145736 | tf_op jit(solution)/shard_map/ppermute | solution.py:344
  62.9 6.0 %collective-permute-start.1 = (f32[1,16,128]{2,1,0:T(8,128)S(1)}, f32[1,16,128]{2,1,0:T(8,128)S(1)}, u32[]{:S(2)}, u32[]{:S(2)}) collective-permute-start(f32[1,16,128]{2,1,0:T(8,128)S(1)} %bitcast.24), channel_id=1, source_target_pairs={{1,0},{2,1},{3,2},{4,3},{5,4},{6,5},{7,6},{9,8},{10,9},{11,10},{12... | collective-permute-start | bytes 24584 | tf_op jit(solution)/shard_map/ppermute | solution.py:337
  68.8 2.0 %collective-permute-start.23 = (f32[32,32,128]{2,1,0:T(8,128)S(1)}, f32[32,32,128]{2,1,0:T(8,128)S(1)}, u32[]{:S(2)}, u32[]{:S(2)}) collective-permute-start(f32[32,32,128]{2,1,0:T(8,128)S(1)} %pack_message.9), channel_id=1, source_target_pairs={{1,2},{5,6},{2,1},{6,5},{9,10},{13,14},{10,9},{14,13},{17,18},{21,... | collective-permute-start | bytes 1572872 | tf_op jit(solution)/shard_map/ppermute | solution.py:341
  69.5 48.1 %collective-permute-start.4 = (f32[64,32,128]{2,1,0:T(8,128)S(1)}, f32[64,32,128]{2,1,0:T(8,128)S(1)}, u32[]{:S(2)}, u32[]{:S(2)}) collective-permute-start(f32[64,32,128]{2,1,0:T(8,128)S(1)} %collective-permute-done.3.side_ref), channel_id=1, source_target_pairs={{1,4},{6,3},{9,12},{14,11},{17,20},{22,19},{25,28},{30,27}} | collective-permute-start | bytes 3145736 | tf_op jit(solution)/shard_map/ppermute | solution.py:344
  70.9 43.6 %collective-permute-start.24 = (f32[32,32,128]{2,1,0:T(8,128)S(1)}, f32[32,32,128]{2,1,0:T(8,128)S(1)}, u32[]{:S(2)}, u32[]{:S(2)}) collective-permute-start(f32[32,32,128]{2,1,0:T(8,128)S(1)} %collective-permute-done.23.side_ref), channel_id=1, source_target_pairs={{1,4},{6,3},{9,12},{14,11},{17,20},{22,19},{25,28},{30,27}} | collective-permute-start | bytes 1572872 | tf_op jit(solution)/shard_map/ppermute | solution.py:344
  82.0 48.7 %copy-start.5 = (f32[32,32,128]{2,1,0:T(8,128)}, f32[32,32,128]{2,1,0:T(8,128)S(1)}, u32[]{:S(2)}) copy-start(f32[32,32,128]{2,1,0:T(8,128)S(1)} %get-tuple-element.23.refs_0_) | copy-start | bytes 1572868
  82.0 48.7 %copy-start.7 = (f32[32,32,128]{2,1,0:T(8,128)}, f32[32,32,128]{2,1,0:T(8,128)S(1)}, u32[]{:S(2)}) copy-start(f32[32,32,128]{2,1,0:T(8,128)S(1)} %get-tuple-element.24.refs_1_) | copy-start | bytes 1572868
  82.0 37.8 %collective-permute-start.11 = (f32[32,32,128]{2,1,0:T(8,128)S(1)}, f32[32,32,128]{2,1,0:T(8,128)S(1)}, u32[]{:S(2)}, u32[]{:S(2)}) collective-permute-start(f32[32,32,128]{2,1,0:T(8,128)S(1)} %get-tuple-element.23.refs_0_), channel_id=1, source_target_pairs={{8,0},{16,8},{24,16},{9,1},{17,9},{25,17},{10,2},{18,10},{26,18},{... | collective-permute-start | bytes 1572872 | tf_op jit(solution)/shard_map/ppermute | solution.py:356
  86.4 44.3 %collective-permute-start.10 = (f32[32,32,128]{2,1,0:T(8,128)S(1)}, f32[32,32,128]{2,1,0:T(8,128)S(1)}, u32[]{:S(2)}, u32[]{:S(2)}) collective-permute-start(f32[32,32,128]{2,1,0:T(8,128)S(1)} %get-tuple-element.24.refs_1_), channel_id=1, source_target_pairs={{0,8},{8,16},{16,24},{1,9},{9,17},{17,25},{2,10},{10,18},{18,26},{... | collective-permute-start | bytes 1572872 | tf_op jit(solution)/shard_map/ppermute | solution.py:356
  97.2 40.4 %copy-start.2 = (f32[32,32,128]{2,1,0:T(8,128)S(1)}, f32[32,32,128]{2,1,0:T(8,128)}, u32[]{:S(2)}) copy-start(f32[32,32,128]{2,1,0:T(8,128)} %copy-done) | copy-start | bytes 1572868
  97.2 40.4 %copy-start.4 = (f32[32,32,128]{2,1,0:T(8,128)S(1)}, f32[32,32,128]{2,1,0:T(8,128)}, u32[]{:S(2)}) copy-start(f32[32,32,128]{2,1,0:T(8,128)} %copy-done.3) | copy-start | bytes 1572868
  97.9 45.1 %copy-start.23 = (f32[1152]{0:T(1024)S(1)}, f32[1152]{0:T(1024)}, u32[]{:S(2)}) copy-start(f32[1152]{0:T(1024)} %strength_ref.3) | copy-start | bytes 13828
  97.9 45.1 %copy-start.24 = (s32[4,2]{0,1:T(2,128)S(1)}, s32[4,2]{0,1:T(2,128)}, u32[]{:S(2)}) copy-start(s32[4,2]{0,1:T(2,128)} %param.11) | copy-start | bytes 100
  97.9 35.5 %collective-permute-start.16 = (f32[32,32,128]{2,1,0:T(8,128)S(1)}, f32[32,32,128]{2,1,0:T(8,128)S(1)}, u32[]{:S(2)}, u32[]{:S(2)}) collective-permute-start(f32[32,32,128]{2,1,0:T(8,128)S(1)} %get-tuple-element.26.refs_4_), channel_id=1, source_target_pairs={{8,0},{16,8},{24,16},{9,1},{17,9},{25,17},{10,2},{18,10},{26,18},{... | collective-permute-start | bytes 1572872 | tf_op jit(solution)/shard_map/ppermute | solution.py:356
  114.5 28.5 %collective-permute-start.15 = (f32[32,32,128]{2,1,0:T(8,128)}, f32[32,32,128]{2,1,0:T(8,128)}, u32[]{:S(2)}, u32[]{:S(2)}) collective-permute-start(f32[32,32,128]{2,1,0:T(8,128)} %get-tuple-element.27.refs_5_), channel_id=1, source_target_pairs={{0,8},{8,16},{16,24},{1,9},{9,17},{17,25},{2,10},{10,18},{18,26},{... | collective-permute-start | bytes 1572872 | tf_op jit(solution)/shard_map/ppermute | solution.py:356
  117.7 25.3 %collective-permute-start.21 = (f32[32,32,128]{2,1,0:T(8,128)}, f32[32,32,128]{2,1,0:T(8,128)}, u32[]{:S(2)}, u32[]{:S(2)}) collective-permute-start(f32[32,32,128]{2,1,0:T(8,128)} %get-tuple-element.29.refs_8_), channel_id=1, source_target_pairs={{8,0},{16,8},{24,16},{9,1},{17,9},{25,17},{10,2},{18,10},{26,18},{... | collective-permute-start | bytes 1572872 | tf_op jit(solution)/shard_map/ppermute | solution.py:356
  119.8 23.2 %collective-permute-start.20 = (f32[32,32,128]{2,1,0:T(8,128)}, f32[32,32,128]{2,1,0:T(8,128)}, u32[]{:S(2)}, u32[]{:S(2)}) collective-permute-start(f32[32,32,128]{2,1,0:T(8,128)} %get-tuple-element.30.refs_9_), channel_id=1, source_target_pairs={{0,8},{8,16},{16,24},{1,9},{9,17},{17,25},{2,10},{10,18},{18,26},{... | collective-permute-start | bytes 1572872 | tf_op jit(solution)/shard_map/ppermute | solution.py:356
  131.5 25.3 %collective-permute-start.5 = (f32[32,32,128]{2,1,0:T(8,128)}, f32[32,32,128]{2,1,0:T(8,128)S(1)}, u32[]{:S(2)}, u32[]{:S(2)}) collective-permute-start(f32[32,32,128]{2,1,0:T(8,128)} %get-tuple-element.21.refs_13_), channel_id=1, source_target_pairs={{0,8},{8,16},{16,24},{1,9},{9,17},{17,25},{2,10},{10,18},{18,26},{... | collective-permute-start | bytes 1572872 | tf_op jit(solution)/shard_map/ppermute | solution.py:356
  134.2 22.5 %collective-permute-start.6 = (f32[32,32,128]{2,1,0:T(8,128)}, f32[32,32,128]{2,1,0:T(8,128)S(1)}, u32[]{:S(2)}, u32[]{:S(2)}) collective-permute-start(f32[32,32,128]{2,1,0:T(8,128)} %get-tuple-element.22.refs_12_), channel_id=1, source_target_pairs={{8,0},{16,8},{24,16},{9,1},{17,9},{25,17},{10,2},{18,10},{26,18},{... | collective-permute-start | bytes 1572872 | tf_op jit(solution)/shard_map/ppermute | solution.py:356
  (19 other events, 148.3 us)

commit v2 on v1

--- a/solution.py
+++ b/solution.py
@@ -94,6 +94,10 @@
     return pltpu.with_memory_space_constraint(cells, pltpu.VMEM)
 
 
+def far_from_core(cells):
+    return pltpu.with_memory_space_constraint(cells, pltpu.HBM)
+
+
 def whole(space):
     return pl.BlockSpec(memory_space=space)
 
@@ -120,130 +124,203 @@
     return cells.reshape(comp_dev, lat_dev, blocks * LANES)
 
 
-def load(own, chunks):
+def load(own, chunks, extra=None):
     spots = [(c, n, f) for c, freqs in enumerate(chunks) for n, f in enumerate(freqs)]
     rows = own.shape[1]
+    ends = [len(freqs) * ND for freqs in chunks]
+    sizes = list(ends)
+    operands = [own]
+    if extra is not None:
+        sizes[0] += 1
+        operands.append(extra)
 
     def kernel(own_ref, *refs):
         sems = refs[-1]
+        out_refs = refs[len(operands) - 1:-1]
         copies = [
-            pltpu.make_async_copy(own_ref.at[pl.ds(f * ND, ND)], refs[c].at[pl.ds(n * ND, ND)], sems.at[m])
+            pltpu.make_async_copy(own_ref.at[pl.ds(f * ND, ND)], out_refs[c].at[pl.ds(n * ND, ND)], sems.at[m])
             for m, (c, n, f) in enumerate(spots)
         ]
         for one in copies:
             one.start()
+        if extra is not None:
+            out_refs[0][ends[0]] = refs[0][0]
         for one in copies:
             one.wait()
 
     return pl.pallas_call(
         kernel,
-        out_shape=[vmem((len(freqs) * ND, rows, LANES)) for freqs in chunks],
-        in_specs=[whole(pltpu.HBM)],
+        out_shape=[vmem((size, rows, LANES)) for size in sizes],
+        in_specs=[whole(pltpu.HBM)] + [whole(pltpu.VMEM)] * (len(operands) - 1),
         out_specs=[whole(pltpu.VMEM)] * len(chunks),
         scratch_shapes=[pltpu.SemaphoreType.DMA((len(spots),))],
         compiler_params=limits(8),
         cost_estimate=cost(0, 2 * len(spots) * ND * rows * LANES * 4),
         name="load",
-    )(pltpu.with_memory_space_constraint(own, pltpu.HBM))
-
-
-def pack_message(own, mate, along_lat, place, freqs):
+    )(far_from_core(own), *operands[1:])
+
+
+def pack_first(own, mate, along_lat, place, freqs):
     rows = own.shape[1]
+    size = len(freqs) * ND
 
     def kernel(a_ref, place_ref, own_ref, mate_ref, out_ref):
         odd = place_ref[0] > 0
         for n, f in enumerate(freqs):
             def one(i, carry):
-                k = f * ND + i
                 j = n * ND + i
-                from_own = (a_ref[k] > 0) == odd
+                from_own = (a_ref[f * ND + i] > 0) == odd
                 out_ref[j] = jnp.where(from_own, own_ref[j], mate_ref[j])
                 return carry
 
-            lax.fori_loop(0, ND, one, 0, unroll=4)
+            lax.fori_loop(0, ND, one, 0, unroll=8)
+        out_ref[size] = own_ref[size]
+        out_ref[size + 1] = mate_ref[size]
 
     return pl.pallas_call(
         kernel,
-        out_shape=vmem((len(freqs) * ND, rows, LANES)),
+        out_shape=vmem((size + 2, rows, LANES)),
         in_specs=[whole(pltpu.SMEM)] * 2 + [whole(pltpu.VMEM)] * 2,
         out_specs=whole(pltpu.VMEM),
         compiler_params=limits(8),
+        cost_estimate=cost(0, 3 * size * rows * LANES * 4),
+        name="pack_first",
+    )(along_lat, place, near_core(own), near_core(mate))
+
+
+def pack_message(own, other, along_lat, place, freqs):
+    rows = own.shape[1]
+
+    def kernel(a_ref, place_ref, own_ref, other_ref, out_ref, held_ref, sems):
+        odd = place_ref[0] > 0
+        copies = [
+            pltpu.make_async_copy(own_ref.at[pl.ds(f * ND, ND)], held_ref.at[pl.ds(n * ND, ND)], sems.at[n])
+            for n, f in enumerate(freqs)
+        ]
+        for one in copies:
+            one.start()
+        for n, f in enumerate(freqs):
+            copies[n].wait()
+
+            def one(i, carry):
+                j = n * ND + i
+                from_own = (a_ref[f * ND + i] > 0) == odd
+                out_ref[j] = jnp.where(from_own, held_ref[j], other_ref[j])
+                return carry
+
+            lax.fori_loop(0, ND, one, 0, unroll=8)
+
+    shape = (len(freqs) * ND, rows, LANES)
+    return pl.pallas_call(
+        kernel,
+        out_shape=vmem(shape),
+        in_specs=[whole(pltpu.SMEM)] * 2 + [whole(pltpu.HBM), whole(pltpu.VMEM)],
+        out_specs=whole(pltpu.VMEM),
+        scratch_shapes=[vmem(shape), pltpu.SemaphoreType.DMA((len(freqs),))],
+        compiler_params=limits(8),
         cost_estimate=cost(0, 3 * len(freqs) * ND * rows * LANES * 4),
         name="pack_message",
-    )(along_lat, place, near_core(own), near_core(mate))
-
-
-def propagate(own, mate, side, relay, along_lat, along_lon, place, masks, freqs):
+    )(along_lat, place, far_from_core(own), near_core(other))
+
+
+def propagate(own, mate, side, hand, along_lat, along_lon, place, masks, freqs):
     rows = own.shape[1]
     half = rows // PAIR
-
-    def kernel(a_ref, b_ref, place_ref, mask_ref, own_ref, mate_ref, side_ref, relay_ref, *out_refs):
+    size = len(freqs) * ND
+
+    def kernel(a_ref, b_ref, place_ref, mask_ref, own_hbm, mate_hbm, side_ref, hand_ref, *refs):
+        out_refs = refs[:len(freqs)]
+        own_ref, mate_ref, done_ref, sems, out_sems = refs[len(freqs):]
         odd = place_ref[0] > 0
-        relayed = place_ref[1] > 0
+        handed = place_ref[1] > 0
         lane = lax.broadcasted_iota(jnp.int32, (half, LANES), 1)
-
-        def run(far_ref):
-            for n, f in enumerate(freqs):
-                def one(i, carry):
-                    k = f * ND + i
-                    j = n * ND + i
-                    a = a_ref[k]
-                    b = b_ref[k]
-                    south = a > 0
-                    near = south == odd
-                    west = b > 0
-                    fore = jnp.where(south, 0, 1)
-                    back = 1 - fore
-                    turn = jnp.where(west, 1, LANES - 1)
-                    edge = lane == jnp.where(west, 0, LANES - 1)
-                    a = jnp.abs(a)
-                    b = jnp.abs(b)
-
-                    def row(ref, at, which):
-                        return ref[at, pl.ds(which, half, stride=PAIR), :]
-
-                    def beside(x):
-                        turned = pltpu.roll(x, turn, 1)
-                        over = jnp.where(west, pltpu.roll(turned, 1, 0), pltpu.roll(turned, half - 1, 0))
-                        return jnp.where(edge, over, turned)
-
-                    def moved(x, before, mask):
-                        return (x - a * (x - before) - b * (x - beside(x))) * mask
-
-                    x0 = jnp.where(near, row(mate_ref, j, fore), row(far_ref, j, fore))
-                    x1 = jnp.where(near, row(mate_ref, j, back), row(far_ref, j, back))
-                    x2 = row(own_ref, j, fore)
-                    x3 = row(own_ref, j, back)
-                    y1 = moved(x1, x0, mask_ref[2 + fore])
-                    y2 = moved(x2, x1, mask_ref[fore])
-                    y3 = moved(x3, x2, mask_ref[back])
-                    z2 = moved(y2, y1, mask_ref[fore])
-                    z3 = moved(y3, y2, mask_ref[back])
-                    out_refs[n][i, pl.ds(fore, half, stride=PAIR), :] = z2
-                    out_refs[n][i, pl.ds(back, half, stride=PAIR), :] = z3
-                    return carry
-
-                lax.fori_loop(0, ND, one, 0, unroll=2)
-
-        @pl.when(relayed)
-        def _():
-            run(relay_ref)
-
-        @pl.when(jnp.logical_not(relayed))
-        def _():
-            run(side_ref)
-
-    operands = [along_lat, along_lon, place] + [near_core(x) for x in (masks, own, mate, side, relay)]
-    in_specs = [whole(pltpu.SMEM)] * 3 + [whole(pltpu.VMEM)] * 5
+        arrivals = [
+            [
+                pltpu.make_async_copy(src.at[pl.ds(f * ND, ND)], dst.at[pl.ds(n * ND, ND)], sems.at[n, m])
+                for m, (src, dst) in enumerate(((own_hbm, own_ref), (mate_hbm, mate_ref)))
+            ]
+            for n, f in enumerate(freqs)
+        ]
+        for pair in arrivals:
+            for one in pair:
+                one.start()
+        leaving = [
+            pltpu.make_async_copy(done_ref.at[pl.ds(n * ND, ND)], out_refs[n], out_sems.at[n])
+            for n in range(len(freqs))
+        ]
+
+        def run(far_ref, n, f):
+            def one(i, carry):
+                k = f * ND + i
+                j = n * ND + i
+                a = a_ref[k]
+                b = b_ref[k]
+                south = a > 0
+                near = south == odd
+                west = b > 0
+                fore = jnp.where(south, 0, 1)
+                back = 1 - fore
+                turn = jnp.where(west, 1, LANES - 1)
+                edge = lane == jnp.where(west, 0, LANES - 1)
+                a = jnp.abs(a)
+                b = jnp.abs(b)
+
+                def row(ref, at, which):
+                    return ref[at, pl.ds(which, half, stride=PAIR), :]
+
+                def beside(x):
+                    turned = pltpu.roll(x, turn, 1)
+                    over = jnp.where(west, pltpu.roll(turned, 1, 0), pltpu.roll(turned, half - 1, 0))
+                    return jnp.where(edge, over, turned)
+
+                def moved(x, before, mask):
+                    return (x - a * (x - before) - b * (x - beside(x))) * mask
+
+                fore_mask = row(mask_ref, 0, fore)
+                back_mask = row(mask_ref, 0, back)
+                x0 = jnp.where(near, row(mate_ref, j, fore), row(far_ref, j, fore))
+                x1 = jnp.where(near, row(mate_ref, j, back), row(far_ref, j, back))
+                x2 = row(own_ref, j, fore)
+                x3 = row(own_ref, j, back)
+                y1 = moved(x1, x0, row(mask_ref, jnp.where(near, 1, 2), back))
+                y2 = moved(x2, x1, fore_mask)
+                y3 = moved(x3, x2, back_mask)
+                done_ref[j, pl.ds(fore, half, stride=PAIR), :] = moved(y2, y1, fore_mask)
+                done_ref[j, pl.ds(back, half, stride=PAIR), :] = moved(y3, y2, back_mask)
+                return carry
+
+            lax.fori_loop(0, ND, one, 0, unroll=4)
+
+        for n, f in enumerate(freqs):
+            for one in arrivals[n]:
+                one.wait()
+
+            @pl.when(handed)
+            def _():
+                run(hand_ref, n, f)
+
+            @pl.when(jnp.logical_not(handed))
+            def _():
+                run(side_ref, n, f)
+
+            leaving[n].start()
+        for one in leaving:
+            one.wait()
+
     return pl.pallas_call(
         kernel,
-        out_shape=[vmem((ND, rows, LANES))] * len(freqs),
-        in_specs=in_specs,
-        out_specs=[whole(pltpu.VMEM)] * len(freqs),
+        out_shape=[jax.ShapeDtypeStruct((ND, rows, LANES), jnp.float32)] * len(freqs),
+        in_specs=[whole(pltpu.SMEM)] * 3 + [whole(pltpu.VMEM)] + [whole(pltpu.HBM)] * 2 + [whole(pltpu.VMEM)] * 2,
+        out_specs=[whole(pltpu.HBM)] * len(freqs),
+        scratch_shapes=[vmem((size, rows, LANES))] * 3
+        + [pltpu.SemaphoreType.DMA((len(freqs), 2)), pltpu.SemaphoreType.DMA((len(freqs),))],
         compiler_params=limits(8),
-        cost_estimate=cost(40 * len(freqs) * ND * rows * LANES, 5 * len(freqs) * ND * rows * LANES * 4),
+        cost_estimate=cost(40 * size * rows * LANES, 5 * size * rows * LANES * 4),
         name="propagate",
-    )(*operands)
+    )(
+        along_lat, along_lon, place, near_core(masks),
+        far_from_core(own), far_from_core(mate), near_core(side), near_core(hand),
+    )
 
 
 def quadruplets(window, parts, places, local, strength, shifts, first, freqs, into):
@@ -317,37 +394,43 @@
     at = lax.axis_index("lat")
     first = (lax.axis_index("comp") * comp_dev)[None].astype(jnp.int32)
     mates = [(i, i ^ 1) for i in range(lat_count)]
+    corners = range(3, lat_count - 1, 4)
     sides = [(i, i + 1) for i in range(1, lat_count, 4)] + [(i + 1, i) for i in range(1, lat_count, 4)]
-    relays = [(i - 2, i + 1) for i in range(3, lat_count - 1, 4)] + [(i + 3, i) for i in range(3, lat_count - 1, 4)]
-    place = jnp.stack([at % 2, jnp.where((at % 4 == 0) | (at % 4 == 3), 1, 0)]).astype(jnp.int32)
-    up = [(i, i + 1) for i in range(lat_count - 1)]
-    down = [(i + 1, i) for i in range(lat_count - 1)]
+    relays = [(i - 2, i + 1) for i in corners] + [(i + 3, i) for i in corners]
+    aheads = [(i, i + 3) for i in corners] + [(i + 1, i - 2) for i in corners]
+    hands = [(i + 2, i + 1) for i in corners] + [(i - 1, i) for i in corners]
+    handed = (at % 4 == 0) | (at % 4 == 3)
+    place = jnp.stack([at % 2, jnp.where(handed, 1, 0)]).astype(jnp.int32)
     z_up = [(i, i + 1) for i in range(comp_count - 1)]
     z_down = [(i + 1, i) for i in range(comp_count - 1)]
 
     own = tiled(spectrum)
-    rows = own.shape[1]
-    maskf = sea_mask.astype(jnp.float32).reshape(lat_dev, rows // lat_dev, LANES)
+    mask = tiled(sea_mask.astype(jnp.float32)[None])
 
     pairs = [(c, local - 1 - c) for c in range(reach)]
     middle = list(range(reach, local - reach))
     chunks = [list(pair) for pair in pairs] + ([middle] if middle else [])
-    owns = load(own, chunks[:1]) + load(own, chunks[1:])
-    mask_south = lax.ppermute(maskf[1:], "lat", up)
-    mask_north = lax.ppermute(maskf[:1], "lat", down)
-    masks = jnp.concatenate([maskf, mask_south, mask_north])
-    mates_in = [lax.ppermute(part, "lat", mates) for part in owns]
-    sides_in = [
-        lax.ppermute(pack_message(owns[n], mates_in[n], courant_lat, place, freqs), "lat", sides)
-        for n, freqs in enumerate(chunks)
-    ]
-    relays_in = [lax.ppermute(side, "lat", relays) for side in sides_in]
+    (head,) = load(own, chunks[:1], mask)
+    mate_head = lax.ppermute(head, "lat", mates)
+    ahead = [None] + [lax.ppermute(part, "lat", aheads) for part in load(own, chunks[1:])]
+    mate = lax.ppermute(own, "lat", mates)
+    sides_in = [lax.ppermute(pack_first(head, mate_head, courant_lat, place, chunks[0]), "lat", sides)]
+    hands_in = [lax.ppermute(sides_in[0], "lat", relays)]
+    for n, freqs in enumerate(chunks):
+        if n:
+            message = pack_message(own, ahead[n], courant_lat, place, freqs)
+            sides_in.append(lax.ppermute(message, "lat", sides))
+            hands_in.append(lax.ppermute(sides_in[n], "lat", hands))
+    size = len(chunks[0]) * ND
+    masks = jnp.concatenate([
+        mask, mate_head[size:], jnp.where(handed, hands_in[0][size + 1:], sides_in[0][size:size + 1])
+    ])
     parts = []
     places = []
     last = []
     for n, freqs in enumerate(chunks):
         made = propagate(
-            owns[n], mates_in[n], sides_in[n], relays_in[n], courant_lat, courant_lon, place, masks, freqs
+            own, mate, sides_in[n], hands_in[n], courant_lat, courant_lon, place, masks, freqs
         )
         parts += made
         places += [reach + f for f in freqs]

time: 161 us -> 172 us (1.068)
  the two profiles are of different devices: /device:TPU:19 before, /device:TPU:2 now
where the time goes in v2:
time: 172 us; the launch traced here: 170 us
  starting transfers between devices  86.7 us (50%)
  Pallas kernels  50.6 us (29%)
  waiting for transfers between devices  28.2 us (16%)
  local copies, waits for them, and re-layouts  2.9 us (2%)
    ppermute x1, starting transfers between devices, halo_plan(): lax.ppermute(pack_first(head, mate_head, courant_lat, place, chunks[0]),...  39.3 us
    ppermute x4, waiting for transfers between devices, halo_plan(): sides_in.append(lax.ppermute(message, 'lat', sides))  28.2 us
    pallas_call x5, Pallas kernels, propagate(): pl.pallas_call(kernel, out_shape=[jax.ShapeDtypeStruct((ND, rows, LANES),...  24.5 us
    ppermute x8, starting transfers between devices, halo_plan(): last = [lax.ppermute(high, 'comp', z_up), lax.ppermute(low, 'comp', z_down)]  24 us
    ppermute x4, starting transfers between devices, halo_plan(): sides_in.append(lax.ppermute(message, 'lat', sides))  11.1 us
    pallas_call x2, Pallas kernels, quadruplets(): pl.pallas_call(kernel, out_shape=[vmem(((local + 2 * reach) * ND, rows, L...  10.9 us
    pallas_call x4, Pallas kernels, pack_message(): pl.pallas_call(kernel, out_shape=vmem(shape), in_specs=[whole(pltpu.SMEM)...  9.29 us
    ppermute x4, starting transfers between devices, halo_plan(): lax.ppermute(part, 'lat', aheads)  5.57 us
  transfers between devices with their start and end apart: 24, of which 4 were waited for; matrix products, arithmetic and copies ran while one was open for 0% of the time, Pallas kernels for 28%

profile of v2, /device:TPU:2, one launch (start us, length us, event | category | flops | bytes accessed | tf_op | source)
XLA Modules:
  0.0 169.8 jit_solution(4630422524175057923)
XLA Ops:
  2.5 3.9 %load.3 = (f32[64,32,128]{2,1,0:T(8,128)}, f32[64,32,128]{2,1,0:T(8,128)}, f32[64,32,128]{2,1,0:T(8,128)}, f32[32,32,128]{2,1,0:T(8,128)}) custom-call(f32[288,32,128]{2,1,0:T(8,128)} %bitcast.25), custom_call_target="tpu_custom_call" | custom-call | bytes 7340032 | tf_op jit(solution)/shard_map/load/pallas_call | solution.py:151
  6.4 1.7 %collective-permute-start.16 = (f32[64,32,128]{2,1,0:T(8,128)}, f32[64,32,128]{2,1,0:T(8,128)}, u32[]{:S(2)}, u32[]{:S(2)}) collective-permute-start(f32[64,32,128]{2,1,0:T(8,128)} %get-tuple-element.28), channel_id=1, source_target_pairs={{3,6},{4,1},{11,14},{12,9},{19,22},{20,17},{27,30},{28,25}} | collective-permute-start | bytes 3145736 | tf_op jit(solution)/shard_map/ppermute | solution.py:415
  8.2 1.7 collective-permute-start.11
  10.6 1.5 collective-permute-start.21
  12.9 39.3 %collective-permute-start.1 = (f32[66,32,128]{2,1,0:T(8,128)S(1)}, f32[66,32,128]{2,1,0:T(8,128)S(1)}, u32[]{:S(2)}, u32[]{:S(2)}) collective-permute-start(f32[66,32,128]{2,1,0:T(8,128)S(1)} %pack_first.1), channel_id=1, source_target_pairs={{1,2},{5,6},{2,1},{6,5},{9,10},{13,14},{10,9},{14,13},{17,18},{21,... | collective-permute-start | bytes 3244040 | tf_op jit(solution)/shard_map/ppermute | solution.py:417
  52.3 2.2 %pack_message.7 = f32[32,32,128]{2,1,0:T(8,128)S(1)} custom-call(f32[288]{0:T(512)S(1)} %copy-done.6, s32[2]{0:T(128)S(1)} %pad_add_fusion.place_ref, f32[288,32,128]{2,1,0:T(8,128)} %bitcast.26, f32[32,32,128]{2,1,0:T(8,128)} %collective-permute-done.21.other_ref), custom_call_target="tpu_custom_call" | custom-call | bytes 1572864 | tf_op jit(solution)/shard_map/pack_message/pallas_call | solution.py:214
  54.5 1.9 %collective-permute-start.22 = (f32[32,32,128]{2,1,0:T(8,128)S(1)}, f32[32,32,128]{2,1,0:T(8,128)S(1)}, u32[]{:S(2)}, u32[]{:S(2)}) collective-permute-start(f32[32,32,128]{2,1,0:T(8,128)S(1)} %pack_message.7), channel_id=1, source_target_pairs={{1,2},{5,6},{2,1},{6,5},{9,10},{13,14},{10,9},{14,13},{17,18},{21,... | collective-permute-start | bytes 1572872 | tf_op jit(solution)/shard_map/ppermute | solution.py:422
  56.4 2.6 %pack_message.6 = f32[64,32,128]{2,1,0:T(8,128)S(1)} custom-call(f32[288]{0:T(512)S(1)} %copy-done.6, s32[2]{0:T(128)S(1)} %pad_add_fusion.place_ref, f32[288,32,128]{2,1,0:T(8,128)} %bitcast.27, f32[64,32,128]{2,1,0:T(8,128)} %collective-permute-done.16.other_ref), custom_call_target="tpu_custom_call" | custom-call | bytes 3145728 | tf_op jit(solution)/shard_map/pack_message/pallas_call | solution.py:214
  59.0 3.6 %collective-permute-start.17 = (f32[64,32,128]{2,1,0:T(8,128)S(1)}, f32[64,32,128]{2,1,0:T(8,128)S(1)}, u32[]{:S(2)}, u32[]{:S(2)}) collective-permute-start(f32[64,32,128]{2,1,0:T(8,128)S(1)} %pack_message.6), channel_id=1, source_target_pairs={{1,2},{5,6},{2,1},{6,5},{9,10},{13,14},{10,9},{14,13},{17,18},{21,... | collective-permute-start | bytes 3145736 | tf_op jit(solution)/shard_map/ppermute | solution.py:422
  62.7 2.6 %pack_message.5 = f32[64,32,128]{2,1,0:T(8,128)S(1)} custom-call(f32[288]{0:T(512)S(1)} %copy-done.6, s32[2]{0:T(128)S(1)} %pad_add_fusion.place_ref, f32[288,32,128]{2,1,0:T(8,128)} %bitcast.28, f32[64,32,128]{2,1,0:T(8,128)} %collective-permute-done.11.other_ref), custom_call_target="tpu_custom_call" | custom-call | bytes 3145728 | tf_op jit(solution)/shard_map/pack_message/pallas_call | solution.py:214
  65.3 1.9 %collective-permute-start.12 = (f32[64,32,128]{2,1,0:T(8,128)S(1)}, f32[64,32,128]{2,1,0:T(8,128)S(1)}, u32[]{:S(2)}, u32[]{:S(2)}) collective-permute-start(f32[64,32,128]{2,1,0:T(8,128)S(1)} %pack_message.5), channel_id=1, source_target_pairs={{1,2},{5,6},{2,1},{6,5},{9,10},{13,14},{10,9},{14,13},{17,18},{21,... | collective-permute-start | bytes 3145736 | tf_op jit(solution)/shard_map/ppermute | solution.py:422
  67.2 1.9 %pack_message.4 = f32[64,32,128]{2,1,0:T(8,128)S(1)} custom-call(f32[288]{0:T(512)S(1)} %copy-done.6, s32[2]{0:T(128)S(1)} %pad_add_fusion.place_ref, f32[288,32,128]{2,1,0:T(8,128)} %bitcast.29, f32[64,32,128]{2,1,0:T(8,128)S(1)} %collective-permute-done.4.other_ref), custom_call_target="tpu_custom_call" | custom-call | bytes 3145728 | tf_op jit(solution)/shard_map/pack_message/pallas_call | solution.py:214
  69.1 1.6 collective-permute-done.22.side_ref
  70.7 3.6 %collective-permute-start.5 = (f32[64,32,128]{2,1,0:T(8,128)S(1)}, f32[64,32,128]{2,1,0:T(8,128)S(1)}, u32[]{:S(2)}, u32[]{:S(2)}) collective-permute-start(f32[64,32,128]{2,1,0:T(8,128)S(1)} %pack_message.4), channel_id=1, source_target_pairs={{1,2},{5,6},{2,1},{6,5},{9,10},{13,14},{10,9},{14,13},{17,18},{21,... | collective-permute-start | bytes 3145736 | tf_op jit(solution)/shard_map/ppermute | solution.py:422
  75.1 6.8 %collective-permute-done.17.side_ref = f32[64,32,128]{2,1,0:T(8,128)S(1)} collective-permute-done((f32[64,32,128]{2,1,0:T(8,128)S(1)}, f32[64,32,128]{2,1,0:T(8,128)S(1)}, u32[]{:S(2)}, u32[]{:S(2)}) %collective-permute-start.17) | collective-permute-done | bytes 1048608 | tf_op jit(solution)/shard_map/ppermute | solution.py:422
  81.9 1.3 collective-permute-start.18
  83.3 9.9 %collective-permute-done.12.side_ref = f32[64,32,128]{2,1,0:T(8,128)S(1)} collective-permute-done((f32[64,32,128]{2,1,0:T(8,128)S(1)}, f32[64,32,128]{2,1,0:T(8,128)S(1)}, u32[]{:S(2)}, u32[]{:S(2)}) %collective-permute-start.12) | collective-permute-done | bytes 1048608 | tf_op jit(solution)/shard_map/ppermute | solution.py:422
  93.2 1.3 collective-permute-start.13
  94.5 9.9 %collective-permute-done.5.side_ref = f32[64,32,128]{2,1,0:T(8,128)S(1)} collective-permute-done((f32[64,32,128]{2,1,0:T(8,128)S(1)}, f32[64,32,128]{2,1,0:T(8,128)S(1)}, u32[]{:S(2)}, u32[]{:S(2)}) %collective-permute-start.5) | collective-permute-done | bytes 1048608 | tf_op jit(solution)/shard_map/ppermute | solution.py:422
  104.4 1.3 collective-permute-start.6
  105.8 1.3 collective-permute-start.23
  107.2 4.9 %propagate.6 = (f32[32,32,128]{2,1,0:T(8,128)S(1)}, f32[32,32,128]{2,1,0:T(8,128)S(1)}) custom-call(f32[288]{0:T(512)S(1)} %copy-done.6, f32[288]{0:T(512)S(1)} %copy-done.7, s32[2]{0:T(128)S(1)} %pad_add_fusion.place_ref, f32[3,32,128]{2,1,0:T(8,128)S(1)} %pad_maximum_fusion.mask_ref, f32[288,32,128]{2,1,0:T(8,128)} %bitcast.30, ...), custom_call_target="tpu_custom_call" | custom-call | flops 10485760 | bytes 5242880 | tf_op jit(solution)/shard_map/propagate/pallas_call | solution.py:310
  113.4 5.1 %collective-permute-start.9 = (f32[32,32,128]{2,1,0:T(8,128)S(1)}, f32[32,32,128]{2,1,0:T(8,128)S(1)}, u32[]{:S(2)}, u32[]{:S(2)}) collective-permute-start(f32[32,32,128]{2,1,0:T(8,128)S(1)} %get-tuple-element.24.refs_1_), channel_id=1, source_target_pairs={{0,8},{8,16},{16,24},{1,9},{9,17},{17,25},{2,10},{10,18},{18,26},{... | collective-permute-start | bytes 1572872 | tf_op jit(solution)/shard_map/ppermute | solution.py:439
  118.5 4.9 %propagate.8 = (f32[32,32,128]{2,1,0:T(8,128)S(1)}, f32[32,32,128]{2,1,0:T(8,128)S(1)}) custom-call(f32[288]{0:T(512)S(1)} %copy-done.6, f32[288]{0:T(512)S(1)} %copy-done.7, s32[2]{0:T(128)S(1)} %pad_add_fusion.place_ref, f32[3,32,128]{2,1,0:T(8,128)S(1)} %pad_maximum_fusion.mask_ref, f32[288,32,128]{2,1,0:T(8,128)} %bitcast.31, ...), custom_call_target="tpu_custom_call" | custom-call | flops 10485760 | bytes 5242880 | tf_op jit(solution)/shard_map/propagate/pallas_call | solution.py:310
  124.8 5.6 %propagate.7 = (f32[32,32,128]{2,1,0:T(8,128)}, f32[32,32,128]{2,1,0:T(8,128)}) custom-call(f32[288]{0:T(512)S(1)} %copy-done.6, f32[288]{0:T(512)S(1)} %copy-done.7, s32[2]{0:T(128)S(1)} %pad_add_fusion.place_ref, f32[3,32,128]{2,1,0:T(8,128)S(1)} %pad_maximum_fusion.mask_ref, f32[288,32,128]{2,1,0:T(8,128)} %bitcast.32, ...), custom_call_target="tpu_custom_call" | custom-call | flops 10485760 | bytes 5242880 | tf_op jit(solution)/shard_map/propagate/pallas_call | solution.py:310
  130.4 5.4 %collective-permute-start.19 = (f32[32,32,128]{2,1,0:T(8,128)S(1)}, f32[32,32,128]{2,1,0:T(8,128)}, u32[]{:S(2)}, u32[]{:S(2)}) collective-permute-start(f32[32,32,128]{2,1,0:T(8,128)S(1)} %get-tuple-element.30.refs_9_), channel_id=1, source_target_pairs={{0,8},{8,16},{16,24},{1,9},{9,17},{17,25},{2,10},{10,18},{18,26},{... | collective-permute-start | bytes 1572872 | tf_op jit(solution)/shard_map/ppermute | solution.py:439
  137.1 5.4 %collective-permute-start.14 = (f32[32,32,128]{2,1,0:T(8,128)}, f32[32,32,128]{2,1,0:T(8,128)}, u32[]{:S(2)}, u32[]{:S(2)}) collective-permute-start(f32[32,32,128]{2,1,0:T(8,128)} %get-tuple-element.27.refs_5_), channel_id=1, source_target_pairs={{0,8},{8,16},{16,24},{1,9},{9,17},{17,25},{2,10},{10,18},{18,26},{... | collective-permute-start | bytes 1572872 | tf_op jit(solution)/shard_map/ppermute | solution.py:439
  142.5 5.6 %propagate.5 = (f32[32,32,128]{2,1,0:T(8,128)}, f32[32,32,128]{2,1,0:T(8,128)}) custom-call(f32[288]{0:T(512)S(1)} %copy-done.6, f32[288]{0:T(512)S(1)} %copy-done.7, s32[2]{0:T(128)S(1)} %pad_add_fusion.place_ref, f32[3,32,128]{2,1,0:T(8,128)S(1)} %pad_maximum_fusion.mask_ref, f32[288,32,128]{2,1,0:T(8,128)} %bitcast.33, ...), custom_call_target="tpu_custom_call" | custom-call | flops 10485760 | bytes 5242880 | tf_op jit(solution)/shard_map/propagate/pallas_call | solution.py:310
  148.1 3.1 %collective-permute-start.7 = (f32[32,32,128]{2,1,0:T(8,128)}, f32[32,32,128]{2,1,0:T(8,128)}, u32[]{:S(2)}, u32[]{:S(2)}) collective-permute-start(f32[32,32,128]{2,1,0:T(8,128)} %get-tuple-element.21.refs_13_), channel_id=1, source_target_pairs={{0,8},{8,16},{16,24},{1,9},{9,17},{17,25},{2,10},{10,18},{18,26},{... | collective-permute-start | bytes 1572872 | tf_op jit(solution)/shard_map/ppermute | solution.py:439
  155.4 3.3 %propagate.9.refs_14_ = f32[32,32,128]{2,1,0:T(8,128)S(1)} custom-call(f32[288]{0:T(512)S(1)} %copy-done.6, f32[288]{0:T(512)S(1)} %copy-done.7, s32[2]{0:T(128)S(1)} %pad_add_fusion.place_ref, f32[3,32,128]{2,1,0:T(8,128)S(1)} %pad_maximum_fusion.mask_ref, f32[288,32,128]{2,1,0:T(8,128)} %bitcast.34, f32[288,32,128]{2,1,0:T(8,128)} %collective-permute-done.3.mate_hbm, ...), custom_call_target="tpu_custom_call" | custom-call | flops 5242880 | bytes 2621440 | tf_op jit(solution)/shard_map/propagate/pallas_call | solution.py:310
  158.8 7.3 %quadruplets.2 = (f32[544,32,128]{2,1,0:T(8,128)S(1)}, f32[288,32,128]{2,1,0:T(8,128)}) custom-call(f32[1152]{0:T(1024)S(1)} %copy-done.8, s32[2,4]{1,0:T(2,128)S(1)} %bitcast.21, s32[1]{0:T(128)} %bitcast.1.first_ref, f32[32,32,128]{2,1,0:T(8,128)S(1)} %get-tuple-element.23.refs_0_, f32[32,32,128]{2,1,0:T(8,128)S(1)} %get-tuple-element.24.refs_1_, ...), custom_call_target="tpu_custom_call" | custom-call | flops 13762560 | bytes 22020096 | tf_op jit(solution)/shard_map/quadruplets/pallas_call | solution.py:369
  166.2 3.6 %quadruplets.3 = (f32[544,32,128]{2,1,0:T(8,128)S(1)}, f32[288,32,128]{2,1,0:T(8,128)}) custom-call(f32[1152]{0:T(1024)S(1)} %copy-done.8, s32[2,4]{1,0:T(2,128)S(1)} %bitcast.22, s32[1]{0:T(128)} %bitcast.1.first_ref, f32[32,32,128]{2,1,0:T(8,128)} %collective-permute-done.7.refs_0_, ...), custom_call_target="tpu_custom_call", output_to_operand_aliasing={{0}: (5, {}), {1}: (6, {})} | custom-call | flops 3932160 | bytes 6291456 | tf_op jit(solution)/shard_map/quadruplets/pallas_call | solution.py:369
  (55 shorter events, 13.0 us)
Async XLA Ops:
  0.0 107.2 %collective-permute-start.3 = (f32[288,32,128]{2,1,0:T(8,128)}, f32[288,32,128]{2,1,0:T(8,128)}, u32[]{:S(2)}, u32[]{:S(2)}) collective-permute-start(f32[288,32,128]{2,1,0:T(8,128)} %bitcast.23), channel_id=1, source_target_pairs={{0,1},{1,0},{2,3},{3,2},{4,5},{5,4},{6,7},{7,6},{8,9},{9,8},{10,11... | collective-permute-start | bytes 14155784 | tf_op jit(solution)/shard_map/ppermute | solution.py:416
  2.0 10.1 %copy-start.6 = (f32[288]{0:T(512)S(1)}, f32[288]{0:T(512)}, u32[]{:S(2)}) copy-start(f32[288]{0:T(512)} %a_ref.19) | copy-start | bytes 3460
  2.0 8.6 %collective-permute-start = (f32[65,32,128]{2,1,0:T(8,128)S(1)}, f32[65,32,128]{2,1,0:T(8,128)S(1)}, u32[]{:S(2)}, u32[]{:S(2)}) collective-permute-start(f32[65,32,128]{2,1,0:T(8,128)S(1)} %load.2.own_ref), channel_id=1, source_target_pairs={{0,1},{1,0},{2,3},{3,2},{4,5},{5,4},{6,7},{7,6},{8,9},{9,8},{10,11... | collective-permute-start | bytes 3194888 | tf_op jit(solution)/shard_map/ppermute | solution.py:414
  6.4 48.1 %collective-permute-start.16 = (f32[64,32,128]{2,1,0:T(8,128)}, f32[64,32,128]{2,1,0:T(8,128)}, u32[]{:S(2)}, u32[]{:S(2)}) collective-permute-start(f32[64,32,128]{2,1,0:T(8,128)} %get-tuple-element.28), channel_id=1, source_target_pairs={{3,6},{4,1},{11,14},{12,9},{19,22},{20,17},{27,30},{28,25}} | collective-permute-start | bytes 3145736 | tf_op jit(solution)/shard_map/ppermute | solution.py:415
  8.2 50.9 %collective-permute-start.11 = (f32[64,32,128]{2,1,0:T(8,128)}, f32[64,32,128]{2,1,0:T(8,128)}, u32[]{:S(2)}, u32[]{:S(2)}) collective-permute-start(f32[64,32,128]{2,1,0:T(8,128)} %get-tuple-element.25), channel_id=1, source_target_pairs={{3,6},{4,1},{11,14},{12,9},{19,22},{20,17},{27,30},{28,25}} | collective-permute-start | bytes 3145736 | tf_op jit(solution)/shard_map/ppermute | solution.py:415
  9.8 55.5 %collective-permute-start.4 = (f32[64,32,128]{2,1,0:T(8,128)}, f32[64,32,128]{2,1,0:T(8,128)S(1)}, u32[]{:S(2)}, u32[]{:S(2)}) collective-permute-start(f32[64,32,128]{2,1,0:T(8,128)} %get-tuple-element.20), channel_id=1, source_target_pairs={{3,6},{4,1},{11,14},{12,9},{19,22},{20,17},{27,30},{28,25}} | collective-permute-start | bytes 3145736 | tf_op jit(solution)/shard_map/ppermute | solution.py:415
  10.6 2.4 %collective-permute-start.21 = (f32[32,32,128]{2,1,0:T(8,128)}, f32[32,32,128]{2,1,0:T(8,128)}, u32[]{:S(2)}, u32[]{:S(2)}) collective-permute-start(f32[32,32,128]{2,1,0:T(8,128)} %get-tuple-element.31), channel_id=1, source_target_pairs={{3,6},{4,1},{11,14},{12,9},{19,22},{20,17},{27,30},{28,25}} | collective-permute-start | bytes 1572872 | tf_op jit(solution)/shard_map/ppermute | solution.py:415
  12.9 61.4 %collective-permute-start.1 = (f32[66,32,128]{2,1,0:T(8,128)S(1)}, f32[66,32,128]{2,1,0:T(8,128)S(1)}, u32[]{:S(2)}, u32[]{:S(2)}) collective-permute-start(f32[66,32,128]{2,1,0:T(8,128)S(1)} %pack_first.1), channel_id=1, source_target_pairs={{1,2},{5,6},{2,1},{6,5},{9,10},{13,14},{10,9},{14,13},{17,18},{21,... | collective-permute-start | bytes 3244040 | tf_op jit(solution)/shard_map/ppermute | solution.py:417
  54.5 16.2 %collective-permute-start.22 = (f32[32,32,128]{2,1,0:T(8,128)S(1)}, f32[32,32,128]{2,1,0:T(8,128)S(1)}, u32[]{:S(2)}, u32[]{:S(2)}) collective-permute-start(f32[32,32,128]{2,1,0:T(8,128)S(1)} %pack_message.7), channel_id=1, source_target_pairs={{1,2},{5,6},{2,1},{6,5},{9,10},{13,14},{10,9},{14,13},{17,18},{21,... | collective-permute-start | bytes 1572872 | tf_op jit(solution)/shard_map/ppermute | solution.py:422
  59.0 22.9 %collective-permute-start.17 = (f32[64,32,128]{2,1,0:T(8,128)S(1)}, f32[64,32,128]{2,1,0:T(8,128)S(1)}, u32[]{:S(2)}, u32[]{:S(2)}) collective-permute-start(f32[64,32,128]{2,1,0:T(8,128)S(1)} %pack_message.6), channel_id=1, source_target_pairs={{1,2},{5,6},{2,1},{6,5},{9,10},{13,14},{10,9},{14,13},{17,18},{21,... | collective-permute-start | bytes 3145736 | tf_op jit(solution)/shard_map/ppermute | solution.py:422
  65.3 41.9 %copy-start.7 = (f32[288]{0:T(512)S(1)}, f32[288]{0:T(512)}, u32[]{:S(2)}) copy-start(f32[288]{0:T(512)} %b_ref.9) | copy-start | bytes 3460
  65.3 27.9 %collective-permute-start.12 = (f32[64,32,128]{2,1,0:T(8,128)S(1)}, f32[64,32,128]{2,1,0:T(8,128)S(1)}, u32[]{:S(2)}, u32[]{:S(2)}) collective-permute-start(f32[64,32,128]{2,1,0:T(8,128)S(1)} %pack_message.5), channel_id=1, source_target_pairs={{1,2},{5,6},{2,1},{6,5},{9,10},{13,14},{10,9},{14,13},{17,18},{21,... | collective-permute-start | bytes 3145736 | tf_op jit(solution)/shard_map/ppermute | solution.py:422
  70.7 41.4 %copy-start.2 = (f32[32,32,128]{2,1,0:T(8,128)}, f32[32,32,128]{2,1,0:T(8,128)S(1)}, u32[]{:S(2)}) copy-start(f32[32,32,128]{2,1,0:T(8,128)S(1)} %collective-permute-done.22.side_ref) | copy-start | bytes 1572868
  70.7 33.7 %collective-permute-start.5 = (f32[64,32,128]{2,1,0:T(8,128)S(1)}, f32[64,32,128]{2,1,0:T(8,128)S(1)}, u32[]{:S(2)}, u32[]{:S(2)}) collective-permute-start(f32[64,32,128]{2,1,0:T(8,128)S(1)} %pack_message.4), channel_id=1, source_target_pairs={{1,2},{5,6},{2,1},{6,5},{9,10},{13,14},{10,9},{14,13},{17,18},{21,... | collective-permute-start | bytes 3145736 | tf_op jit(solution)/shard_map/ppermute | solution.py:422
  74.4 31.4 %collective-permute-start.2 = (f32[66,32,128]{2,1,0:T(8,128)S(1)}, f32[66,32,128]{2,1,0:T(8,128)S(1)}, u32[]{:S(2)}, u32[]{:S(2)}) collective-permute-start(f32[66,32,128]{2,1,0:T(8,128)S(1)} %collective-permute-done.1.side_ref), channel_id=1, source_target_pairs={{1,4},{6,3},{9,12},{14,11},{17,20},{22,19},{25,28},{30,27}} | collective-permute-start | bytes 3244040 | tf_op jit(solution)/shard_map/ppermute | solution.py:418
  81.9 31.5 %collective-permute-start.18 = (f32[64,32,128]{2,1,0:T(8,128)S(1)}, f32[64,32,128]{2,1,0:T(8,128)S(1)}, u32[]{:S(2)}, u32[]{:S(2)}) collective-permute-start(f32[64,32,128]{2,1,0:T(8,128)S(1)} %collective-permute-done.17.side_ref), channel_id=1, source_target_pairs={{5,4},{2,3},{13,12},{10,11},{21,20},{18,19},{29,28},{26,27}} | collective-permute-start | bytes 3145736 | tf_op jit(solution)/shard_map/ppermute | solution.py:423
  93.2 30.3 %collective-permute-start.13 = (f32[64,32,128]{2,1,0:T(8,128)S(1)}, f32[64,32,128]{2,1,0:T(8,128)S(1)}, u32[]{:S(2)}, u32[]{:S(2)}) collective-permute-start(f32[64,32,128]{2,1,0:T(8,128)S(1)} %collective-permute-done.12.side_ref), channel_id=1, source_target_pairs={{5,4},{2,3},{13,12},{10,11},{21,20},{18,19},{29,28},{26,27}} | collective-permute-start | bytes 3145736 | tf_op jit(solution)/shard_map/ppermute | solution.py:423
  104.4 31.4 %collective-permute-start.6 = (f32[64,32,128]{2,1,0:T(8,128)S(1)}, f32[64,32,128]{2,1,0:T(8,128)S(1)}, u32[]{:S(2)}, u32[]{:S(2)}) collective-permute-start(f32[64,32,128]{2,1,0:T(8,128)S(1)} %collective-permute-done.5.side_ref), channel_id=1, source_target_pairs={{5,4},{2,3},{13,12},{10,11},{21,20},{18,19},{29,28},{26,27}} | collective-permute-start | bytes 3145736 | tf_op jit(solution)/shard_map/ppermute | solution.py:423
  105.8 24.6 %collective-permute-start.23 = (f32[32,32,128]{2,1,0:T(8,128)S(1)}, f32[32,32,128]{2,1,0:T(8,128)S(1)}, u32[]{:S(2)}, u32[]{:S(2)}) collective-permute-start(f32[32,32,128]{2,1,0:T(8,128)S(1)} %collective-permute-done.22.side_ref), channel_id=1, source_target_pairs={{5,4},{2,3},{13,12},{10,11},{21,20},{18,19},{29,28},{26,27}} | collective-permute-start | bytes 1572872 | tf_op jit(solution)/shard_map/ppermute | solution.py:423
  112.1 24.9 %collective-permute-start.10 = (f32[32,32,128]{2,1,0:T(8,128)S(1)}, f32[32,32,128]{2,1,0:T(8,128)S(1)}, u32[]{:S(2)}, u32[]{:S(2)}) collective-permute-start(f32[32,32,128]{2,1,0:T(8,128)S(1)} %get-tuple-element.23.refs_0_), channel_id=1, source_target_pairs={{8,0},{16,8},{24,16},{9,1},{17,9},{25,17},{10,2},{18,10},{26,18},{... | collective-permute-start | bytes 1572872 | tf_op jit(solution)/shard_map/ppermute | solution.py:439
  113.4 34.7 %collective-permute-start.9 = (f32[32,32,128]{2,1,0:T(8,128)S(1)}, f32[32,32,128]{2,1,0:T(8,128)S(1)}, u32[]{:S(2)}, u32[]{:S(2)}) collective-permute-start(f32[32,32,128]{2,1,0:T(8,128)S(1)} %get-tuple-element.24.refs_1_), channel_id=1, source_target_pairs={{0,8},{8,16},{16,24},{1,9},{9,17},{17,25},{2,10},{10,18},{18,26},{... | collective-permute-start | bytes 1572872 | tf_op jit(solution)/shard_map/ppermute | solution.py:439
  123.5 27.8 %collective-permute-start.20 = (f32[32,32,128]{2,1,0:T(8,128)S(1)}, f32[32,32,128]{2,1,0:T(8,128)S(1)}, u32[]{:S(2)}, u32[]{:S(2)}) collective-permute-start(f32[32,32,128]{2,1,0:T(8,128)S(1)} %get-tuple-element.29.refs_8_), channel_id=1, source_target_pairs={{8,0},{16,8},{24,16},{9,1},{17,9},{25,17},{10,2},{18,10},{26,18},{... | collective-permute-start | bytes 1572872 | tf_op jit(solution)/shard_map/ppermute | solution.py:439
  130.4 17.7 %copy-start.4 = (f32[32,32,128]{2,1,0:T(8,128)}, f32[32,32,128]{2,1,0:T(8,128)S(1)}, u32[]{:S(2)}) copy-start(f32[32,32,128]{2,1,0:T(8,128)S(1)} %collective-permute-done.23.hand_ref) | copy-start | bytes 1572868
  130.4 28.3 %collective-permute-start.19 = (f32[32,32,128]{2,1,0:T(8,128)S(1)}, f32[32,32,128]{2,1,0:T(8,128)}, u32[]{:S(2)}, u32[]{:S(2)}) collective-permute-start(f32[32,32,128]{2,1,0:T(8,128)S(1)} %get-tuple-element.30.refs_9_), channel_id=1, source_target_pairs={{0,8},{8,16},{16,24},{1,9},{9,17},{17,25},{2,10},{10,18},{18,26},{... | collective-permute-start | bytes 1572872 | tf_op jit(solution)/shard_map/ppermute | solution.py:439
  135.8 23.0 %collective-permute-start.15 = (f32[32,32,128]{2,1,0:T(8,128)}, f32[32,32,128]{2,1,0:T(8,128)}, u32[]{:S(2)}, u32[]{:S(2)}) collective-permute-start(f32[32,32,128]{2,1,0:T(8,128)} %get-tuple-element.26.refs_4_), channel_id=1, source_target_pairs={{8,0},{16,8},{24,16},{9,1},{17,9},{25,17},{10,2},{18,10},{26,18},{... | collective-permute-start | bytes 1572872 | tf_op jit(solution)/shard_map/ppermute | solution.py:439
  137.1 21.7 %collective-permute-start.14 = (f32[32,32,128]{2,1,0:T(8,128)}, f32[32,32,128]{2,1,0:T(8,128)}, u32[]{:S(2)}, u32[]{:S(2)}) collective-permute-start(f32[32,32,128]{2,1,0:T(8,128)} %get-tuple-element.27.refs_5_), channel_id=1, source_target_pairs={{0,8},{8,16},{16,24},{1,9},{9,17},{17,25},{2,10},{10,18},{18,26},{... | collective-permute-start | bytes 1572872 | tf_op jit(solution)/shard_map/ppermute | solution.py:439
  148.1 18.0 %collective-permute-start.7 = (f32[32,32,128]{2,1,0:T(8,128)}, f32[32,32,128]{2,1,0:T(8,128)}, u32[]{:S(2)}, u32[]{:S(2)}) collective-permute-start(f32[32,32,128]{2,1,0:T(8,128)} %get-tuple-element.21.refs_13_), channel_id=1, source_target_pairs={{0,8},{8,16},{16,24},{1,9},{9,17},{17,25},{2,10},{10,18},{18,26},{... | collective-permute-start | bytes 1572872 | tf_op jit(solution)/shard_map/ppermute | solution.py:439
  152.0 14.1 %collective-permute-start.8 = (f32[32,32,128]{2,1,0:T(8,128)}, f32[32,32,128]{2,1,0:T(8,128)}, u32[]{:S(2)}, u32[]{:S(2)}) collective-permute-start(f32[32,32,128]{2,1,0:T(8,128)} %get-tuple-element.22.refs_12_), channel_id=1, source_target_pairs={{8,0},{16,8},{24,16},{9,1},{17,9},{25,17},{10,2},{18,10},{26,18},{... | collective-permute-start | bytes 1572872 | tf_op jit(solution)/shard_map/ppermute | solution.py:439
  153.3 1.0 copy-start.3
  155.4 3.4 %copy-start.1 = (f32[32,32,128]{2,1,0:T(8,128)S(1)}, f32[32,32,128]{2,1,0:T(8,128)}, u32[]{:S(2)}) copy-start(f32[32,32,128]{2,1,0:T(8,128)} %copy-done) | copy-start | bytes 1572868
  155.4 3.4 %copy-start.8 = (f32[1152]{0:T(1024)S(1)}, f32[1152]{0:T(1024)}, u32[]{:S(2)}) copy-start(f32[1152]{0:T(1024)} %strength_ref.3) | copy-start | bytes 13828
  155.4 3.4 %copy-start.9 = (s32[4,2]{0,1:T(2,128)S(1)}, s32[4,2]{0,1:T(2,128)}, u32[]{:S(2)}) copy-start(s32[4,2]{0,1:T(2,128)} %param.11) | copy-start | bytes 100
  (2 other events, 1.8 us)

commit v3 on v2

--- a/solution.py
+++ b/solution.py
@@ -144,7 +144,7 @@
         for one in copies:
             one.start()
         if extra is not None:
-            out_refs[0][ends[0]] = refs[0][0]
+            out_refs[0][ends[0]] = refs[0][0].astype(jnp.float32)
         for one in copies:
             one.wait()
 
@@ -223,7 +223,7 @@
     )(along_lat, place, far_from_core(own), near_core(other))
 
 
-def propagate(own, mate, side, hand, along_lat, along_lon, place, masks, freqs):
+def propagate(own, mate, side, hand, along_lat, along_lon, place, masks, freqs, picked=False, skip=0):
     rows = own.shape[1]
     half = rows // PAIR
     size = len(freqs) * ND
@@ -236,7 +236,9 @@
         lane = lax.broadcasted_iota(jnp.int32, (half, LANES), 1)
         arrivals = [
             [
-                pltpu.make_async_copy(src.at[pl.ds(f * ND, ND)], dst.at[pl.ds(n * ND, ND)], sems.at[n, m])
+                pltpu.make_async_copy(
+                    src.at[pl.ds((n if picked else f) * ND, ND)], dst.at[pl.ds(n * ND, ND)], sems.at[n, m]
+                )
                 for m, (src, dst) in enumerate(((own_hbm, own_ref), (mate_hbm, mate_ref)))
             ]
             for n, f in enumerate(freqs)
@@ -278,8 +280,8 @@
 
                 fore_mask = row(mask_ref, 0, fore)
                 back_mask = row(mask_ref, 0, back)
-                x0 = jnp.where(near, row(mate_ref, j, fore), row(far_ref, j, fore))
-                x1 = jnp.where(near, row(mate_ref, j, back), row(far_ref, j, back))
+                x0 = jnp.where(near, row(mate_ref, j, fore), row(far_ref, skip * ND + j, fore))
+                x1 = jnp.where(near, row(mate_ref, j, back), row(far_ref, skip * ND + j, back))
                 x2 = row(own_ref, j, fore)
                 x3 = row(own_ref, j, back)
                 y1 = moved(x1, x0, row(mask_ref, jnp.where(near, 1, 2), back))
@@ -310,7 +312,8 @@
     return pl.pallas_call(
         kernel,
         out_shape=[jax.ShapeDtypeStruct((ND, rows, LANES), jnp.float32)] * len(freqs),
-        in_specs=[whole(pltpu.SMEM)] * 3 + [whole(pltpu.VMEM)] + [whole(pltpu.HBM)] * 2 + [whole(pltpu.VMEM)] * 2,
+        in_specs=[whole(pltpu.SMEM)] * 3 + [whole(pltpu.VMEM)] + [whole(pl.ANY if picked else pltpu.HBM), whole(pl.ANY)]
+        + [whole(pltpu.VMEM)] * 2,
         out_specs=[whole(pltpu.HBM)] * len(freqs),
         scratch_shapes=[vmem((size, rows, LANES))] * 3
         + [pltpu.SemaphoreType.DMA((len(freqs), 2)), pltpu.SemaphoreType.DMA((len(freqs),))],
@@ -319,7 +322,7 @@
         name="propagate",
     )(
         along_lat, along_lon, place, near_core(masks),
-        far_from_core(own), far_from_core(mate), near_core(side), near_core(hand),
+        own if picked else far_from_core(own), mate, near_core(side), near_core(hand),
     )
 
 
@@ -405,42 +408,47 @@
     z_down = [(i + 1, i) for i in range(comp_count - 1)]
 
     own = tiled(spectrum)
-    mask = tiled(sea_mask.astype(jnp.float32)[None])
-
-    pairs = [(c, local - 1 - c) for c in range(reach)]
+    mask = tiled(sea_mask[None])
+
+    chunks = [[c, local - 1 - c] for c in range(reach)]
     middle = list(range(reach, local - reach))
-    chunks = [list(pair) for pair in pairs] + ([middle] if middle else [])
-    (head,) = load(own, chunks[:1], mask)
+    lots = chunks[:-1] + [chunks[-1] + middle]
+    head, part = load(own, lots[:2], mask)
     mate_head = lax.ppermute(head, "lat", mates)
-    ahead = [None] + [lax.ppermute(part, "lat", aheads) for part in load(own, chunks[1:])]
+    ahead = [None, lax.ppermute(part, "lat", aheads)]
+    sides_in = [lax.ppermute(pack_first(head, mate_head, courant_lat, place, chunks[0]), "lat", sides)]
+    rest = load(own, lots[2:])
+    ahead += [lax.ppermute(part, "lat", aheads) for part in rest]
     mate = lax.ppermute(own, "lat", mates)
-    sides_in = [lax.ppermute(pack_first(head, mate_head, courant_lat, place, chunks[0]), "lat", sides)]
     hands_in = [lax.ppermute(sides_in[0], "lat", relays)]
-    for n, freqs in enumerate(chunks):
+    for n, freqs in enumerate(lots):
         if n:
             message = pack_message(own, ahead[n], courant_lat, place, freqs)
             sides_in.append(lax.ppermute(message, "lat", sides))
             hands_in.append(lax.ppermute(sides_in[n], "lat", hands))
     size = len(chunks[0]) * ND
     masks = jnp.concatenate([
-        mask, mate_head[size:], jnp.where(handed, hands_in[0][size + 1:], sides_in[0][size:size + 1])
+        head[size:], mate_head[size:], jnp.where(handed, hands_in[0][size + 1:], sides_in[0][size:size + 1])
     ])
     parts = []
     places = []
     last = []
     for n, freqs in enumerate(chunks):
-        made = propagate(
-            own, mate, sides_in[n], hands_in[n], courant_lat, courant_lon, place, masks, freqs
+        low, high = propagate(
+            own if n else head, mate if n else mate_head, sides_in[n], hands_in[n],
+            courant_lat, courant_lon, place, masks, freqs, picked=n == 0,
         )
-        parts += made
+        parts += [low, high]
         places += [reach + f for f in freqs]
-        if n < reach:
-            low, high = made
-            last = [lax.ppermute(high, "comp", z_up), lax.ppermute(low, "comp", z_down)]
-            last_places = [reach - 1 - n, reach + local + n]
-            if n < reach - 1:
-                parts += last
-                places += last_places
+        last = [lax.ppermute(high, "comp", z_up), lax.ppermute(low, "comp", z_down)]
+        last_places = [reach - 1 - n, reach + local + n]
+        if n < reach - 1:
+            parts += last
+            places += last_places
+    parts += propagate(
+        own, mate, sides_in[-1], hands_in[-1], courant_lat, courant_lon, place, masks, middle, skip=len(chunks[-1])
+    )
+    places += [reach + f for f in middle]
     shifts = quad_shift.T
     window, inner = quadruplets(
         None, parts, places, local, strength, shifts, first, list(range(1, local - 1)), None

time: 172 us -> 149 us (0.87)
  starting transfers between devices: 86.7 us -> 66 us
  waiting for transfers between devices: 28.2 us -> 25.6 us
    ppermute x1, starting transfers between devices: 39.3 us -> 1.92 us  [halo_plan(): lax.ppermute(pack_first(head, mate_head, courant_lat, place, chunks[0]),...]
    ppermute x4 -> x3, starting transfers between devices: 11.1 us -> 28 us  [halo_plan(): sides_in.append(lax.ppermute(message, 'lat', sides))]
    ppermute x4 -> x3, waiting for transfers between devices: 28.2 us -> 19 us  [halo_plan(): sides_in.append(lax.ppermute(message, 'lat', sides))]
    ppermute x1, waiting for transfers between devices: 0.01 us -> 6.59 us  [halo_plan(): lax.ppermute(pack_first(head, mate_head, courant_lat, place, chunks[0]),...]
    ppermute x1, starting transfers between devices: 0.57 us -> 2.94 us  [halo_plan(): mate_head = lax.ppermute(head, 'lat', mates)]
    pallas_call x4 -> x3, Pallas kernels: 9.29 us -> 7.23 us  [pack_message(): pl.pallas_call(kernel, out_shape=vmem(shape), in_specs=[whole(pltpu.SMEM)...]
    ppermute x4 -> x3, starting transfers between devices: 5.57 us -> 4.03 us  [the longest x2 2.4 us: halo_plan(): ahead += [lax.ppermute(part, 'lat', aheads) for part in rest]]
    ppermute x4 -> x3, starting transfers between devices: 5.36 us -> 4.08 us  [halo_plan(): hands_in.append(lax.ppermute(sides_in[n], 'lat', hands))]
  transfers between devices with their start and end apart: 24 -> 21, of which waited for: 4 -> 3; matrix products, arithmetic and copies ran while one was open for 0% -> 1% of each run, Pallas kernels for 28% -> 32%
where the time goes in v3:
time: 149 us; the launch traced here: 147 us
  starting transfers between devices  66 us (44%)
  Pallas kernels  51.1 us (34%)
  waiting for transfers between devices  25.6 us (17%)
  local copies, waits for them, and re-layouts  3.21 us (2%)
    ppermute x3, starting transfers between devices, halo_plan(): sides_in.append(lax.ppermute(message, 'lat', sides))  28 us
    pallas_call x5, Pallas kernels, propagate(): pl.pallas_call(kernel, out_shape=[jax.ShapeDtypeStruct((ND, rows, LANES),...  25.5 us
    ppermute x8, starting transfers between devices, halo_plan(): last = [lax.ppermute(high, 'comp', z_up), lax.ppermute(low, 'comp', z_down)]  24.3 us
    ppermute x3, waiting for transfers between devices, halo_plan(): sides_in.append(lax.ppermute(message, 'lat', sides))  19 us
    pallas_call x2, Pallas kernels, quadruplets(): pl.pallas_call(kernel, out_shape=[vmem(((local + 2 * reach) * ND, rows, L...  11.1 us
    pallas_call x3, Pallas kernels, pack_message(): pl.pallas_call(kernel, out_shape=vmem(shape), in_specs=[whole(pltpu.SMEM)...  7.23 us
    ppermute x1, waiting for transfers between devices, halo_plan(): lax.ppermute(pack_first(head, mate_head, courant_lat, place, chunks[0]),...  6.59 us
    pallas_call x2, Pallas kernels, load(): pl.pallas_call(kernel, out_shape=[vmem((size, rows, LANES)) for size in s...  5.8 us
  transfers between devices with their start and end apart: 21, of which 3 were waited for; matrix products, arithmetic and copies ran while one was open for 1% of the time, Pallas kernels for 32%

profile of v3, /device:TPU:2, one launch (start us, length us, event | category | flops | bytes accessed | tf_op | source)
XLA Modules:
  0.0 146.7 jit_solution(8600538503832266518)
XLA Ops:
  0.0 3.2 %load.3 = (f32[64,32,128]{2,1,0:T(8,128)}, f32[96,32,128]{2,1,0:T(8,128)}) custom-call(f32[288,32,128]{2,1,0:T(8,128)} %bitcast.23), custom_call_target="tpu_custom_call" | custom-call | bytes 5242880 | tf_op jit(solution)/shard_map/load/pallas_call | solution.py:151
  4.0 2.6 %load.2 = (f32[65,32,128]{2,1,0:T(8,128)S(1)}, f32[64,32,128]{2,1,0:T(8,128)}) custom-call(f32[288,32,128]{2,1,0:T(8,128)} %bitcast.24, s32[1,32,128]{2,1,0:T(8,128)S(1)} %bitcast.19), custom_call_target="tpu_custom_call" | custom-call | bytes 4194304 | tf_op jit(solution)/shard_map/load/pallas_call | solution.py:151
  6.6 2.9 %collective-permute-start = (f32[65,32,128]{2,1,0:T(8,128)S(1)}, f32[65,32,128]{2,1,0:T(8,128)}, u32[]{:S(2)}, u32[]{:S(2)}) collective-permute-start(f32[65,32,128]{2,1,0:T(8,128)S(1)} %get-tuple-element.20.own_ref.own_hbm), channel_id=1, source_target_pairs={{0,1},{1,0},{2,3},{3,2},{4,5},{5,4},{6,7},{7,6},{8,9},{9,8},{10,11... | collective-permute-start | bytes 3194888 | tf_op jit(solution)/shard_map/ppermute | solution.py:417
  9.6 1.6 %collective-permute-start.16 = (f32[64,32,128]{2,1,0:T(8,128)}, f32[64,32,128]{2,1,0:T(8,128)}, u32[]{:S(2)}, u32[]{:S(2)}) collective-permute-start(f32[64,32,128]{2,1,0:T(8,128)} %get-tuple-element.29), channel_id=1, source_target_pairs={{3,6},{4,1},{11,14},{12,9},{19,22},{20,17},{27,30},{28,25}} | collective-permute-start | bytes 3145736 | tf_op jit(solution)/shard_map/ppermute | solution.py:421
  11.2 1.6 %collective-permute-start.11 = (f32[64,32,128]{2,1,0:T(8,128)}, f32[64,32,128]{2,1,0:T(8,128)}, u32[]{:S(2)}, u32[]{:S(2)}) collective-permute-start(f32[64,32,128]{2,1,0:T(8,128)} %get-tuple-element.26), channel_id=1, source_target_pairs={{3,6},{4,1},{11,14},{12,9},{19,22},{20,17},{27,30},{28,25}} | collective-permute-start | bytes 3145736 | tf_op jit(solution)/shard_map/ppermute | solution.py:418
  12.9 2.1 %pack_message.3 = f32[96,32,128]{2,1,0:T(8,128)S(1)} custom-call(f32[288]{0:T(512)S(1)} %copy-done.14, s32[2]{0:T(128)S(1)} %pad_add_fusion.place_ref, f32[288,32,128]{2,1,0:T(8,128)} %bitcast.25, f32[96,32,128]{2,1,0:T(8,128)S(1)} %collective-permute-done.4.other_ref), custom_call_target="tpu_custom_call" | custom-call | bytes 4718592 | tf_op jit(solution)/shard_map/pack_message/pallas_call | solution.py:214
  15.0 13.6 %collective-permute-start.5 = (f32[96,32,128]{2,1,0:T(8,128)S(1)}, f32[96,32,128]{2,1,0:T(8,128)S(1)}, u32[]{:S(2)}, u32[]{:S(2)}) collective-permute-start(f32[96,32,128]{2,1,0:T(8,128)S(1)} %pack_message.3), channel_id=1, source_target_pairs={{1,2},{5,6},{2,1},{6,5},{9,10},{13,14},{10,9},{14,13},{17,18},{21,... | collective-permute-start | bytes 4718600 | tf_op jit(solution)/shard_map/ppermute | solution.py:427
  28.6 1.5 %pack_first.1 = f32[66,32,128]{2,1,0:T(8,128)S(1)} custom-call(f32[288]{0:T(512)S(1)} %copy-done.14, s32[2]{0:T(128)S(1)} %pad_add_fusion.place_ref, f32[65,32,128]{2,1,0:T(8,128)S(1)} %get-tuple-element.20.own_ref.own_hbm, f32[65,32,128]{2,1,0:T(8,128)} %collective-permute-done.mate_ref.mate_hbm), custom_call_target="tpu_custom_call" | custom-call | bytes 3145728 | tf_op jit(solution)/shard_map/pack_first/pallas_call | solution.py:180
  30.1 1.9 %collective-permute-start.1 = (f32[66,32,128]{2,1,0:T(8,128)S(1)}, f32[66,32,128]{2,1,0:T(8,128)S(1)}, u32[]{:S(2)}, u32[]{:S(2)}) collective-permute-start(f32[66,32,128]{2,1,0:T(8,128)S(1)} %pack_first.1), channel_id=1, source_target_pairs={{1,2},{5,6},{2,1},{6,5},{9,10},{13,14},{10,9},{14,13},{17,18},{21,... | collective-permute-start | bytes 3244040 | tf_op jit(solution)/shard_map/ppermute | solution.py:419
  32.1 2.6 %pack_message.5 = f32[64,32,128]{2,1,0:T(8,128)S(1)} custom-call(f32[288]{0:T(512)S(1)} %copy-done.14, s32[2]{0:T(128)S(1)} %pad_add_fusion.place_ref, f32[288,32,128]{2,1,0:T(8,128)} %bitcast.26, f32[64,32,128]{2,1,0:T(8,128)} %collective-permute-done.16.other_ref), custom_call_target="tpu_custom_call" | custom-call | bytes 3145728 | tf_op jit(solution)/shard_map/pack_message/pallas_call | solution.py:214
  34.7 5.9 %collective-permute-start.17 = (f32[64,32,128]{2,1,0:T(8,128)S(1)}, f32[64,32,128]{2,1,0:T(8,128)S(1)}, u32[]{:S(2)}, u32[]{:S(2)}) collective-permute-start(f32[64,32,128]{2,1,0:T(8,128)S(1)} %pack_message.5), channel_id=1, source_target_pairs={{1,2},{5,6},{2,1},{6,5},{9,10},{13,14},{10,9},{14,13},{17,18},{21,... | collective-permute-start | bytes 3145736 | tf_op jit(solution)/shard_map/ppermute | solution.py:427
  40.6 2.6 %pack_message.4 = f32[64,32,128]{2,1,0:T(8,128)S(1)} custom-call(f32[288]{0:T(512)S(1)} %copy-done.14, s32[2]{0:T(128)S(1)} %pad_add_fusion.place_ref, f32[288,32,128]{2,1,0:T(8,128)} %bitcast.27, f32[64,32,128]{2,1,0:T(8,128)} %collective-permute-done.11.other_ref), custom_call_target="tpu_custom_call" | custom-call | bytes 3145728 | tf_op jit(solution)/shard_map/pack_message/pallas_call | solution.py:214
  43.2 8.5 %collective-permute-start.12 = (f32[64,32,128]{2,1,0:T(8,128)S(1)}, f32[64,32,128]{2,1,0:T(8,128)S(1)}, u32[]{:S(2)}, u32[]{:S(2)}) collective-permute-start(f32[64,32,128]{2,1,0:T(8,128)S(1)} %pack_message.4), channel_id=1, source_target_pairs={{1,2},{5,6},{2,1},{6,5},{9,10},{13,14},{10,9},{14,13},{17,18},{21,... | collective-permute-start | bytes 3145736 | tf_op jit(solution)/shard_map/ppermute | solution.py:427
  51.7 6.6 %collective-permute-done.1.side_ref = f32[66,32,128]{2,1,0:T(8,128)S(1)} collective-permute-done((f32[66,32,128]{2,1,0:T(8,128)S(1)}, f32[66,32,128]{2,1,0:T(8,128)S(1)}, u32[]{:S(2)}, u32[]{:S(2)}) %collective-permute-start.1) | collective-permute-done | bytes 1081376 | tf_op jit(solution)/shard_map/ppermute | solution.py:419
  59.0 1.4 collective-permute-start.6
  60.4 9.1 %collective-permute-done.17.side_ref = f32[64,32,128]{2,1,0:T(8,128)S(1)} collective-permute-done((f32[64,32,128]{2,1,0:T(8,128)S(1)}, f32[64,32,128]{2,1,0:T(8,128)S(1)}, u32[]{:S(2)}, u32[]{:S(2)}) %collective-permute-start.17) | collective-permute-done | bytes 1048608 | tf_op jit(solution)/shard_map/ppermute | solution.py:427
  69.5 1.3 collective-permute-start.18
  70.8 9.9 %collective-permute-done.12.side_ref = f32[64,32,128]{2,1,0:T(8,128)S(1)} collective-permute-done((f32[64,32,128]{2,1,0:T(8,128)S(1)}, f32[64,32,128]{2,1,0:T(8,128)S(1)}, u32[]{:S(2)}, u32[]{:S(2)}) %collective-permute-start.12) | collective-permute-done | bytes 1048608 | tf_op jit(solution)/shard_map/ppermute | solution.py:427
  80.7 1.3 collective-permute-start.13
  82.9 4.8 %propagate.6 = (f32[32,32,128]{2,1,0:T(8,128)S(1)}, f32[32,32,128]{2,1,0:T(8,128)S(1)}) custom-call(f32[288]{0:T(512)S(1)} %copy-done.14, f32[288]{0:T(512)S(1)} %copy-done.15, s32[2]{0:T(128)S(1)} %pad_add_fusion.place_ref, f32[3,32,128]{2,1,0:T(8,128)S(1)} %pad_maximum_fusion.mask_ref, f32[65,32,128]{2,1,0:T(8,128)S(1)} %copy-done.1, ...), custom_call_target="tpu_custom_call" | custom-call | flops 10485760 | bytes 5242880 | tf_op jit(solution)/shard_map/propagate/pallas_call | solution.py:312
  87.7 1.3 collective-permute-start.10
  89.0 5.4 %collective-permute-start.9 = (f32[32,32,128]{2,1,0:T(8,128)S(1)}, f32[32,32,128]{2,1,0:T(8,128)S(1)}, u32[]{:S(2)}, u32[]{:S(2)}) collective-permute-start(f32[32,32,128]{2,1,0:T(8,128)S(1)} %get-tuple-element.25.refs_1_), channel_id=1, source_target_pairs={{0,8},{8,16},{16,24},{1,9},{9,17},{17,25},{2,10},{10,18},{18,26},{... | collective-permute-start | bytes 1572872 | tf_op jit(solution)/shard_map/ppermute | solution.py:443
  94.4 5.7 %propagate.8 = (f32[32,32,128]{2,1,0:T(8,128)S(1)}, f32[32,32,128]{2,1,0:T(8,128)}) custom-call(f32[288]{0:T(512)S(1)} %copy-done.14, f32[288]{0:T(512)S(1)} %copy-done.15, s32[2]{0:T(128)S(1)} %pad_add_fusion.place_ref, f32[3,32,128]{2,1,0:T(8,128)S(1)} %pad_maximum_fusion.mask_ref, f32[288,32,128]{2,1,0:T(8,128)} %bitcast.28, ...), custom_call_target="tpu_custom_call" | custom-call | flops 10485760 | bytes 5242880 | tf_op jit(solution)/shard_map/propagate/pallas_call | solution.py:312
  100.1 1.3 collective-permute-start.20
  101.5 5.3 %collective-permute-start.19 = (f32[32,32,128]{2,1,0:T(8,128)}, f32[32,32,128]{2,1,0:T(8,128)}, u32[]{:S(2)}, u32[]{:S(2)}) collective-permute-start(f32[32,32,128]{2,1,0:T(8,128)} %get-tuple-element.31.refs_9_), channel_id=1, source_target_pairs={{0,8},{8,16},{16,24},{1,9},{9,17},{17,25},{2,10},{10,18},{18,26},{... | collective-permute-start | bytes 1572872 | tf_op jit(solution)/shard_map/ppermute | solution.py:443
  106.8 5.6 %propagate.7 = (f32[32,32,128]{2,1,0:T(8,128)}, f32[32,32,128]{2,1,0:T(8,128)}) custom-call(f32[288]{0:T(512)S(1)} %copy-done.14, f32[288]{0:T(512)S(1)} %copy-done.15, s32[2]{0:T(128)S(1)} %pad_add_fusion.place_ref, f32[3,32,128]{2,1,0:T(8,128)S(1)} %pad_maximum_fusion.mask_ref, f32[288,32,128]{2,1,0:T(8,128)} %bitcast.29, ...), custom_call_target="tpu_custom_call" | custom-call | flops 10485760 | bytes 5242880 | tf_op jit(solution)/shard_map/propagate/pallas_call | solution.py:312
  114.6 5.4 %collective-permute-start.14 = (f32[32,32,128]{2,1,0:T(8,128)}, f32[32,32,128]{2,1,0:T(8,128)}, u32[]{:S(2)}, u32[]{:S(2)}) collective-permute-start(f32[32,32,128]{2,1,0:T(8,128)} %get-tuple-element.28.refs_5_), channel_id=1, source_target_pairs={{0,8},{8,16},{16,24},{1,9},{9,17},{17,25},{2,10},{10,18},{18,26},{... | collective-permute-start | bytes 1572872 | tf_op jit(solution)/shard_map/ppermute | solution.py:443
  120.0 5.7 %propagate.5 = (f32[32,32,128]{2,1,0:T(8,128)}, f32[32,32,128]{2,1,0:T(8,128)}) custom-call(f32[288]{0:T(512)S(1)} %copy-done.14, f32[288]{0:T(512)S(1)} %copy-done.15, s32[2]{0:T(128)S(1)} %pad_add_fusion.place_ref, f32[3,32,128]{2,1,0:T(8,128)S(1)} %pad_maximum_fusion.mask_ref, f32[288,32,128]{2,1,0:T(8,128)} %bitcast.30, ...), custom_call_target="tpu_custom_call" | custom-call | flops 10485760 | bytes 5242880 | tf_op jit(solution)/shard_map/propagate/pallas_call | solution.py:312
  126.5 3.1 %collective-permute-start.7 = (f32[32,32,128]{2,1,0:T(8,128)}, f32[32,32,128]{2,1,0:T(8,128)}, u32[]{:S(2)}, u32[]{:S(2)}) collective-permute-start(f32[32,32,128]{2,1,0:T(8,128)} %get-tuple-element.22.refs_13_), channel_id=1, source_target_pairs={{0,8},{8,16},{16,24},{1,9},{9,17},{17,25},{2,10},{10,18},{18,26},{... | collective-permute-start | bytes 1572872 | tf_op jit(solution)/shard_map/ppermute | solution.py:443
  131.8 3.6 %propagate.9.refs_14_ = f32[32,32,128]{2,1,0:T(8,128)S(1)} custom-call(f32[288]{0:T(512)S(1)} %copy-done.14, f32[288]{0:T(512)S(1)} %copy-done.15, s32[2]{0:T(128)S(1)} %pad_add_fusion.place_ref, f32[3,32,128]{2,1,0:T(8,128)S(1)} %pad_maximum_fusion.mask_ref, f32[288,32,128]{2,1,0:T(8,128)} %bitcast.31, f32[288,32,128]{2,1,0:T(8,128)} %collective-permute-done.3.mate_hbm, ...), custom_call_target="tpu_custom_call" | custom-call | flops 5242880 | bytes 2621440 | tf_op jit(solution)/shard_map/propagate/pallas_call | solution.py:312
  135.5 7.5 %quadruplets.2 = (f32[544,32,128]{2,1,0:T(8,128)S(1)}, f32[288,32,128]{2,1,0:T(8,128)}) custom-call(f32[1152]{0:T(1024)S(1)} %copy-done.16, s32[2,4]{1,0:T(2,128)S(1)} %bitcast.20, s32[1]{0:T(128)} %bitcast.1.first_ref, f32[32,32,128]{2,1,0:T(8,128)S(1)} %copy-done.3, f32[32,32,128]{2,1,0:T(8,128)S(1)} %copy-done.5, f32[32,32,128]{2,1,0:T(8,128)S(1)} %copy-done.9, ...), custom_call_target="tpu_custom_call" | custom-call | flops 13762560 | bytes 22020096 | tf_op jit(solution)/shard_map/quadruplets/pallas_call | solution.py:372
  143.0 3.6 %quadruplets.3 = (f32[544,32,128]{2,1,0:T(8,128)S(1)}, f32[288,32,128]{2,1,0:T(8,128)}) custom-call(f32[1152]{0:T(1024)S(1)} %copy-done.16, s32[2,4]{1,0:T(2,128)S(1)} %bitcast.21, s32[1]{0:T(128)} %bitcast.1.first_ref, f32[32,32,128]{2,1,0:T(8,128)} %collective-permute-done.7.refs_0_, ...), custom_call_target="tpu_custom_call", output_to_operand_aliasing={{0}: (5, {}), {1}: (6, {})} | custom-call | flops 3932160 | bytes 6291456 | tf_op jit(solution)/shard_map/quadruplets/pallas_call | solution.py:372
  (66 shorter events, 7.4 us)
Async XLA Ops:
  0.0 4.0 %copy-start.17 = (s32[2,2048]{1,0:T(2,128)S(1)}, s32[2,2048]{1,0:T(2,128)}, u32[]{:S(2)}) copy-start(s32[2,2048]{1,0:T(2,128)} %param.9) | copy-start | bytes 49156
  0.0 94.4 %collective-permute-start.3 = (f32[288,32,128]{2,1,0:T(8,128)}, f32[288,32,128]{2,1,0:T(8,128)}, u32[]{:S(2)}, u32[]{:S(2)}) collective-permute-start(f32[288,32,128]{2,1,0:T(8,128)} %bitcast.22), channel_id=1, source_target_pairs={{0,1},{1,0},{2,3},{3,2},{4,5},{5,4},{6,7},{7,6},{8,9},{9,8},{10,11... | collective-permute-start | bytes 14155784 | tf_op jit(solution)/shard_map/ppermute | solution.py:422
  3.2 9.7 %collective-permute-start.4 = (f32[96,32,128]{2,1,0:T(8,128)}, f32[96,32,128]{2,1,0:T(8,128)S(1)}, u32[]{:S(2)}, u32[]{:S(2)}) collective-permute-start(f32[96,32,128]{2,1,0:T(8,128)} %get-tuple-element.21), channel_id=1, source_target_pairs={{3,6},{4,1},{11,14},{12,9},{19,22},{20,17},{27,30},{28,25}} | collective-permute-start | bytes 4718600 | tf_op jit(solution)/shard_map/ppermute | solution.py:421
  4.0 8.9 %copy-start.14 = (f32[288]{0:T(512)S(1)}, f32[288]{0:T(512)}, u32[]{:S(2)}) copy-start(f32[288]{0:T(512)} %a_ref.17) | copy-start | bytes 3460
  6.6 22.0 %copy-start = (f32[65,32,128]{2,1,0:T(8,128)}, f32[65,32,128]{2,1,0:T(8,128)S(1)}, u32[]{:S(2)}) copy-start(f32[65,32,128]{2,1,0:T(8,128)S(1)} %get-tuple-element.20.own_ref.own_hbm) | copy-start | bytes 3194884
  6.6 22.0 %collective-permute-start = (f32[65,32,128]{2,1,0:T(8,128)S(1)}, f32[65,32,128]{2,1,0:T(8,128)}, u32[]{:S(2)}, u32[]{:S(2)}) collective-permute-start(f32[65,32,128]{2,1,0:T(8,128)S(1)} %get-tuple-element.20.own_ref.own_hbm), channel_id=1, source_target_pairs={{0,1},{1,0},{2,3},{3,2},{4,5},{5,4},{6,7},{7,6},{8,9},{9,8},{10,11... | collective-permute-start | bytes 3194888 | tf_op jit(solution)/shard_map/ppermute | solution.py:417
  9.6 22.5 %collective-permute-start.16 = (f32[64,32,128]{2,1,0:T(8,128)}, f32[64,32,128]{2,1,0:T(8,128)}, u32[]{:S(2)}, u32[]{:S(2)}) collective-permute-start(f32[64,32,128]{2,1,0:T(8,128)} %get-tuple-element.29), channel_id=1, source_target_pairs={{3,6},{4,1},{11,14},{12,9},{19,22},{20,17},{27,30},{28,25}} | collective-permute-start | bytes 3145736 | tf_op jit(solution)/shard_map/ppermute | solution.py:421
  11.2 29.4 %collective-permute-start.11 = (f32[64,32,128]{2,1,0:T(8,128)}, f32[64,32,128]{2,1,0:T(8,128)}, u32[]{:S(2)}, u32[]{:S(2)}) collective-permute-start(f32[64,32,128]{2,1,0:T(8,128)} %get-tuple-element.26), channel_id=1, source_target_pairs={{3,6},{4,1},{11,14},{12,9},{19,22},{20,17},{27,30},{28,25}} | collective-permute-start | bytes 3145736 | tf_op jit(solution)/shard_map/ppermute | solution.py:418
  15.0 44.0 %collective-permute-start.5 = (f32[96,32,128]{2,1,0:T(8,128)S(1)}, f32[96,32,128]{2,1,0:T(8,128)S(1)}, u32[]{:S(2)}, u32[]{:S(2)}) collective-permute-start(f32[96,32,128]{2,1,0:T(8,128)S(1)} %pack_message.3), channel_id=1, source_target_pairs={{1,2},{5,6},{2,1},{6,5},{9,10},{13,14},{10,9},{14,13},{17,18},{21,... | collective-permute-start | bytes 4718600 | tf_op jit(solution)/shard_map/ppermute | solution.py:427
  30.1 28.1 %collective-permute-start.1 = (f32[66,32,128]{2,1,0:T(8,128)S(1)}, f32[66,32,128]{2,1,0:T(8,128)S(1)}, u32[]{:S(2)}, u32[]{:S(2)}) collective-permute-start(f32[66,32,128]{2,1,0:T(8,128)S(1)} %pack_first.1), channel_id=1, source_target_pairs={{1,2},{5,6},{2,1},{6,5},{9,10},{13,14},{10,9},{14,13},{17,18},{21,... | collective-permute-start | bytes 3244040 | tf_op jit(solution)/shard_map/ppermute | solution.py:419
  34.6 47.4 %copy-start.1 = (f32[65,32,128]{2,1,0:T(8,128)S(1)}, f32[65,32,128]{2,1,0:T(8,128)}, u32[]{:S(2)}) copy-start(f32[65,32,128]{2,1,0:T(8,128)} %copy-done) | copy-start | bytes 3194884
  34.7 48.2 %copy-start.15 = (f32[288]{0:T(512)S(1)}, f32[288]{0:T(512)}, u32[]{:S(2)}) copy-start(f32[288]{0:T(512)} %b_ref.9) | copy-start | bytes 3460
  34.7 34.8 %collective-permute-start.17 = (f32[64,32,128]{2,1,0:T(8,128)S(1)}, f32[64,32,128]{2,1,0:T(8,128)S(1)}, u32[]{:S(2)}, u32[]{:S(2)}) collective-permute-start(f32[64,32,128]{2,1,0:T(8,128)S(1)} %pack_message.5), channel_id=1, source_target_pairs={{1,2},{5,6},{2,1},{6,5},{9,10},{13,14},{10,9},{14,13},{17,18},{21,... | collective-permute-start | bytes 3145736 | tf_op jit(solution)/shard_map/ppermute | solution.py:427
  43.2 37.5 %collective-permute-start.12 = (f32[64,32,128]{2,1,0:T(8,128)S(1)}, f32[64,32,128]{2,1,0:T(8,128)S(1)}, u32[]{:S(2)}, u32[]{:S(2)}) collective-permute-start(f32[64,32,128]{2,1,0:T(8,128)S(1)} %pack_message.4), channel_id=1, source_target_pairs={{1,2},{5,6},{2,1},{6,5},{9,10},{13,14},{10,9},{14,13},{17,18},{21,... | collective-permute-start | bytes 3145736 | tf_op jit(solution)/shard_map/ppermute | solution.py:427
  58.3 24.6 %collective-permute-start.2 = (f32[66,32,128]{2,1,0:T(8,128)S(1)}, f32[66,32,128]{2,1,0:T(8,128)S(1)}, u32[]{:S(2)}, u32[]{:S(2)}) collective-permute-start(f32[66,32,128]{2,1,0:T(8,128)S(1)} %collective-permute-done.1.side_ref), channel_id=1, source_target_pairs={{1,4},{6,3},{9,12},{14,11},{17,20},{22,19},{25,28},{30,27}} | collective-permute-start | bytes 3244040 | tf_op jit(solution)/shard_map/ppermute | solution.py:423
  59.0 55.6 %collective-permute-start.6 = (f32[96,32,128]{2,1,0:T(8,128)S(1)}, f32[96,32,128]{2,1,0:T(8,128)S(1)}, u32[]{:S(2)}, u32[]{:S(2)}) collective-permute-start(f32[96,32,128]{2,1,0:T(8,128)S(1)} %collective-permute-done.5.side_ref), channel_id=1, source_target_pairs={{5,4},{2,3},{13,12},{10,11},{21,20},{18,19},{29,28},{26,27}} | collective-permute-start | bytes 4718600 | tf_op jit(solution)/shard_map/ppermute | solution.py:428
  69.5 19.5 %collective-permute-start.18 = (f32[64,32,128]{2,1,0:T(8,128)S(1)}, f32[64,32,128]{2,1,0:T(8,128)S(1)}, u32[]{:S(2)}, u32[]{:S(2)}) collective-permute-start(f32[64,32,128]{2,1,0:T(8,128)S(1)} %collective-permute-done.17.side_ref), channel_id=1, source_target_pairs={{5,4},{2,3},{13,12},{10,11},{21,20},{18,19},{29,28},{26,27}} | collective-permute-start | bytes 3145736 | tf_op jit(solution)/shard_map/ppermute | solution.py:428
  80.7 20.7 %collective-permute-start.13 = (f32[64,32,128]{2,1,0:T(8,128)S(1)}, f32[64,32,128]{2,1,0:T(8,128)S(1)}, u32[]{:S(2)}, u32[]{:S(2)}) collective-permute-start(f32[64,32,128]{2,1,0:T(8,128)S(1)} %collective-permute-done.12.side_ref), channel_id=1, source_target_pairs={{5,4},{2,3},{13,12},{10,11},{21,20},{18,19},{29,28},{26,27}} | collective-permute-start | bytes 3145736 | tf_op jit(solution)/shard_map/ppermute | solution.py:428
  87.7 12.4 %copy-start.2 = (f32[32,32,128]{2,1,0:T(8,128)}, f32[32,32,128]{2,1,0:T(8,128)S(1)}, u32[]{:S(2)}) copy-start(f32[32,32,128]{2,1,0:T(8,128)S(1)} %get-tuple-element.24.refs_0_) | copy-start | bytes 1572868
  87.7 12.4 %copy-start.4 = (f32[32,32,128]{2,1,0:T(8,128)}, f32[32,32,128]{2,1,0:T(8,128)S(1)}, u32[]{:S(2)}) copy-start(f32[32,32,128]{2,1,0:T(8,128)S(1)} %get-tuple-element.25.refs_1_) | copy-start | bytes 1572868
  87.7 24.8 %collective-permute-start.10 = (f32[32,32,128]{2,1,0:T(8,128)S(1)}, f32[32,32,128]{2,1,0:T(8,128)S(1)}, u32[]{:S(2)}, u32[]{:S(2)}) collective-permute-start(f32[32,32,128]{2,1,0:T(8,128)S(1)} %get-tuple-element.24.refs_0_), channel_id=1, source_target_pairs={{8,0},{16,8},{24,16},{9,1},{17,9},{25,17},{10,2},{18,10},{26,18},{... | collective-permute-start | bytes 1572872 | tf_op jit(solution)/shard_map/ppermute | solution.py:443
  89.0 36.7 %collective-permute-start.9 = (f32[32,32,128]{2,1,0:T(8,128)S(1)}, f32[32,32,128]{2,1,0:T(8,128)S(1)}, u32[]{:S(2)}, u32[]{:S(2)}) collective-permute-start(f32[32,32,128]{2,1,0:T(8,128)S(1)} %get-tuple-element.25.refs_1_), channel_id=1, source_target_pairs={{0,8},{8,16},{16,24},{1,9},{9,17},{17,25},{2,10},{10,18},{18,26},{... | collective-permute-start | bytes 1572872 | tf_op jit(solution)/shard_map/ppermute | solution.py:443
  100.1 12.3 %copy-start.10 = (f32[32,32,128]{2,1,0:T(8,128)}, f32[32,32,128]{2,1,0:T(8,128)S(1)}, u32[]{:S(2)}) copy-start(f32[32,32,128]{2,1,0:T(8,128)S(1)} %get-tuple-element.30.refs_8_) | copy-start | bytes 1572868
  100.1 29.4 %collective-permute-start.20 = (f32[32,32,128]{2,1,0:T(8,128)S(1)}, f32[32,32,128]{2,1,0:T(8,128)S(1)}, u32[]{:S(2)}, u32[]{:S(2)}) collective-permute-start(f32[32,32,128]{2,1,0:T(8,128)S(1)} %get-tuple-element.30.refs_8_), channel_id=1, source_target_pairs={{8,0},{16,8},{24,16},{9,1},{17,9},{25,17},{10,2},{18,10},{26,18},{... | collective-permute-start | bytes 1572872 | tf_op jit(solution)/shard_map/ppermute | solution.py:443
  101.5 34.0 %collective-permute-start.19 = (f32[32,32,128]{2,1,0:T(8,128)}, f32[32,32,128]{2,1,0:T(8,128)}, u32[]{:S(2)}, u32[]{:S(2)}) collective-permute-start(f32[32,32,128]{2,1,0:T(8,128)} %get-tuple-element.31.refs_9_), channel_id=1, source_target_pairs={{0,8},{8,16},{16,24},{1,9},{9,17},{17,25},{2,10},{10,18},{18,26},{... | collective-permute-start | bytes 1572872 | tf_op jit(solution)/shard_map/ppermute | solution.py:443
  113.3 22.1 %collective-permute-start.15 = (f32[32,32,128]{2,1,0:T(8,128)}, f32[32,32,128]{2,1,0:T(8,128)}, u32[]{:S(2)}, u32[]{:S(2)}) collective-permute-start(f32[32,32,128]{2,1,0:T(8,128)} %get-tuple-element.27.refs_4_), channel_id=1, source_target_pairs={{8,0},{16,8},{24,16},{9,1},{17,9},{25,17},{10,2},{18,10},{26,18},{... | collective-permute-start | bytes 1572872 | tf_op jit(solution)/shard_map/ppermute | solution.py:443
  114.6 20.9 %collective-permute-start.14 = (f32[32,32,128]{2,1,0:T(8,128)}, f32[32,32,128]{2,1,0:T(8,128)}, u32[]{:S(2)}, u32[]{:S(2)}) collective-permute-start(f32[32,32,128]{2,1,0:T(8,128)} %get-tuple-element.28.refs_5_), channel_id=1, source_target_pairs={{0,8},{8,16},{16,24},{1,9},{9,17},{17,25},{2,10},{10,18},{18,26},{... | collective-permute-start | bytes 1572872 | tf_op jit(solution)/shard_map/ppermute | solution.py:443
  126.5 16.5 %collective-permute-start.7 = (f32[32,32,128]{2,1,0:T(8,128)}, f32[32,32,128]{2,1,0:T(8,128)}, u32[]{:S(2)}, u32[]{:S(2)}) collective-permute-start(f32[32,32,128]{2,1,0:T(8,128)} %get-tuple-element.22.refs_13_), channel_id=1, source_target_pairs={{0,8},{8,16},{16,24},{1,9},{9,17},{17,25},{2,10},{10,18},{18,26},{... | collective-permute-start | bytes 1572872 | tf_op jit(solution)/shard_map/ppermute | solution.py:443
  130.4 12.6 %collective-permute-start.8 = (f32[32,32,128]{2,1,0:T(8,128)}, f32[32,32,128]{2,1,0:T(8,128)}, u32[]{:S(2)}, u32[]{:S(2)}) collective-permute-start(f32[32,32,128]{2,1,0:T(8,128)} %get-tuple-element.23.refs_12_), channel_id=1, source_target_pairs={{8,0},{16,8},{24,16},{9,1},{17,9},{25,17},{10,2},{18,10},{26,18},{... | collective-permute-start | bytes 1572872 | tf_op jit(solution)/shard_map/ppermute | solution.py:443
  131.7 3.8 %copy-start.3 = (f32[32,32,128]{2,1,0:T(8,128)S(1)}, f32[32,32,128]{2,1,0:T(8,128)}, u32[]{:S(2)}) copy-start(f32[32,32,128]{2,1,0:T(8,128)} %copy-done.2) | copy-start | bytes 1572868
  131.7 3.8 %copy-start.5 = (f32[32,32,128]{2,1,0:T(8,128)S(1)}, f32[32,32,128]{2,1,0:T(8,128)}, u32[]{:S(2)}) copy-start(f32[32,32,128]{2,1,0:T(8,128)} %copy-done.4) | copy-start | bytes 1572868
  131.7 3.8 %copy-start.7 = (f32[32,32,128]{2,1,0:T(8,128)S(1)}, f32[32,32,128]{2,1,0:T(8,128)}, u32[]{:S(2)}) copy-start(f32[32,32,128]{2,1,0:T(8,128)} %copy-done.6) | copy-start | bytes 1572868
  (8 other events, 21.3 us)

commit v4 on v3

--- a/solution.py
+++ b/solution.py
@@ -132,6 +132,7 @@
     operands = [own]
     if extra is not None:
         sizes[0] += 1
+        sizes.append(1)
         operands.append(extra)
 
     def kernel(own_ref, *refs):
@@ -144,7 +145,9 @@
         for one in copies:
             one.start()
         if extra is not None:
-            out_refs[0][ends[0]] = refs[0][0].astype(jnp.float32)
+            maskf = refs[0][0].astype(jnp.float32)
+            out_refs[0][ends[0]] = maskf
+            out_refs[-1][0] = maskf
         for one in copies:
             one.wait()
 
@@ -152,40 +155,12 @@
         kernel,
         out_shape=[vmem((size, rows, LANES)) for size in sizes],
         in_specs=[whole(pltpu.HBM)] + [whole(pltpu.VMEM)] * (len(operands) - 1),
-        out_specs=[whole(pltpu.VMEM)] * len(chunks),
+        out_specs=[whole(pltpu.VMEM)] * len(sizes),
         scratch_shapes=[pltpu.SemaphoreType.DMA((len(spots),))],
         compiler_params=limits(8),
         cost_estimate=cost(0, 2 * len(spots) * ND * rows * LANES * 4),
         name="load",
     )(far_from_core(own), *operands[1:])
-
-
-def pack_first(own, mate, along_lat, place, freqs):
-    rows = own.shape[1]
-    size = len(freqs) * ND
-
-    def kernel(a_ref, place_ref, own_ref, mate_ref, out_ref):
-        odd = place_ref[0] > 0
-        for n, f in enumerate(freqs):
-            def one(i, carry):
-                j = n * ND + i
-                from_own = (a_ref[f * ND + i] > 0) == odd
-                out_ref[j] = jnp.where(from_own, own_ref[j], mate_ref[j])
-                return carry
-
-            lax.fori_loop(0, ND, one, 0, unroll=8)
-        out_ref[size] = own_ref[size]
-        out_ref[size + 1] = mate_ref[size]
-
-    return pl.pallas_call(
-        kernel,
-        out_shape=vmem((size + 2, rows, LANES)),
-        in_specs=[whole(pltpu.SMEM)] * 2 + [whole(pltpu.VMEM)] * 2,
-        out_specs=whole(pltpu.VMEM),
-        compiler_params=limits(8),
-        cost_estimate=cost(0, 3 * size * rows * LANES * 4),
-        name="pack_first",
-    )(along_lat, place, near_core(own), near_core(mate))
 
 
 def pack_message(own, other, along_lat, place, freqs):
@@ -223,7 +198,7 @@
     )(along_lat, place, far_from_core(own), near_core(other))
 
 
-def propagate(own, mate, side, hand, along_lat, along_lon, place, masks, freqs, picked=False, skip=0):
+def propagate(own, mate, side, hand, along_lat, along_lon, place, masks, freqs, skip=0):
     rows = own.shape[1]
     half = rows // PAIR
     size = len(freqs) * ND
@@ -237,7 +212,7 @@
         arrivals = [
             [
                 pltpu.make_async_copy(
-                    src.at[pl.ds((n if picked else f) * ND, ND)], dst.at[pl.ds(n * ND, ND)], sems.at[n, m]
+                    src.at[pl.ds(f * ND, ND)], dst.at[pl.ds(n * ND, ND)], sems.at[n, m]
                 )
                 for m, (src, dst) in enumerate(((own_hbm, own_ref), (mate_hbm, mate_ref)))
             ]
@@ -312,7 +287,7 @@
     return pl.pallas_call(
         kernel,
         out_shape=[jax.ShapeDtypeStruct((ND, rows, LANES), jnp.float32)] * len(freqs),
-        in_specs=[whole(pltpu.SMEM)] * 3 + [whole(pltpu.VMEM)] + [whole(pl.ANY if picked else pltpu.HBM), whole(pl.ANY)]
+        in_specs=[whole(pltpu.SMEM)] * 3 + [whole(pltpu.VMEM)] + [whole(pltpu.HBM), whole(pl.ANY)]
         + [whole(pltpu.VMEM)] * 2,
         out_specs=[whole(pltpu.HBM)] * len(freqs),
         scratch_shapes=[vmem((size, rows, LANES))] * 3
@@ -322,7 +297,7 @@
         name="propagate",
     )(
         along_lat, along_lon, place, near_core(masks),
-        own if picked else far_from_core(own), mate, near_core(side), near_core(hand),
+        far_from_core(own), mate, near_core(side), near_core(hand),
     )
 
 
@@ -399,7 +374,7 @@
     mates = [(i, i ^ 1) for i in range(lat_count)]
     corners = range(3, lat_count - 1, 4)
     sides = [(i, i + 1) for i in range(1, lat_count, 4)] + [(i + 1, i) for i in range(1, lat_count, 4)]
-    relays = [(i - 2, i + 1) for i in corners] + [(i + 3, i) for i in corners]
+    diagonals = [(i, i + 1) for i in corners] + [(i + 1, i) for i in corners]
     aheads = [(i, i + 3) for i in corners] + [(i + 1, i - 2) for i in corners]
     hands = [(i + 2, i + 1) for i in corners] + [(i - 1, i) for i in corners]
     handed = (at % 4 == 0) | (at % 4 == 3)
@@ -413,30 +388,28 @@
     chunks = [[c, local - 1 - c] for c in range(reach)]
     middle = list(range(reach, local - reach))
     lots = chunks[:-1] + [chunks[-1] + middle]
-    head, part = load(own, lots[:2], mask)
-    mate_head = lax.ppermute(head, "lat", mates)
+    head, part, maskf = load(own, lots[:2], mask)
+    hands_in = [lax.ppermute(head, "lat", diagonals)]
+    sides_in = [lax.ppermute(head, "lat", sides)]
     ahead = [None, lax.ppermute(part, "lat", aheads)]
-    sides_in = [lax.ppermute(pack_first(head, mate_head, courant_lat, place, chunks[0]), "lat", sides)]
     rest = load(own, lots[2:])
     ahead += [lax.ppermute(part, "lat", aheads) for part in rest]
+    mate_mask = lax.ppermute(maskf, "lat", mates)
     mate = lax.ppermute(own, "lat", mates)
-    hands_in = [lax.ppermute(sides_in[0], "lat", relays)]
     for n, freqs in enumerate(lots):
         if n:
             message = pack_message(own, ahead[n], courant_lat, place, freqs)
             sides_in.append(lax.ppermute(message, "lat", sides))
             hands_in.append(lax.ppermute(sides_in[n], "lat", hands))
     size = len(chunks[0]) * ND
-    masks = jnp.concatenate([
-        head[size:], mate_head[size:], jnp.where(handed, hands_in[0][size + 1:], sides_in[0][size:size + 1])
-    ])
+    masks = jnp.concatenate([maskf, mate_mask, jnp.where(handed, hands_in[0][size:], sides_in[0][size:])])
     parts = []
     places = []
     last = []
     for n, freqs in enumerate(chunks):
         low, high = propagate(
-            own if n else head, mate if n else mate_head, sides_in[n], hands_in[n],
-            courant_lat, courant_lon, place, masks, freqs, picked=n == 0,
+            own, far_from_core(mate) if n else mate, sides_in[n], hands_in[n],
+            courant_lat, courant_lon, place, masks, freqs,
         )
         parts += [low, high]
         places += [reach + f for f in freqs]
@@ -446,7 +419,8 @@
             parts += last
             places += last_places
     parts += propagate(
-        own, mate, sides_in[-1], hands_in[-1], courant_lat, courant_lon, place, masks, middle, skip=len(chunks[-1])
+        own, far_from_core(mate), sides_in[-1], hands_in[-1],
+        courant_lat, courant_lon, place, masks, middle, skip=len(chunks[-1]),
     )
     places += [reach + f for f in middle]
     shifts = quad_shift.T

time: 149 us -> 162 us (1.087)
  waiting for transfers between devices: 25.6 us -> 41.5 us
  Pallas kernels: 51.1 us -> 49 us
    ppermute x3, waiting for transfers between devices: 6.6 us -> 15.2 us  [the longest x1 13.1 us: halo_plan(): sides_in = [lax.ppermute(head, 'lat', sides)]]
    ppermute x3, waiting for transfers between devices: 19 us -> 24.4 us  [halo_plan(): sides_in.append(lax.ppermute(message, 'lat', sides))]
    ppermute x3, starting transfers between devices: 28 us -> 32.2 us  [halo_plan(): sides_in.append(lax.ppermute(message, 'lat', sides))]
    ppermute x3, starting transfers between devices: 5.58 us -> 2.71 us  [the longest x1 1.92 us: halo_plan(): sides_in = [lax.ppermute(head, 'lat', sides)]]
    ppermute x8, waiting for transfers between devices: 0.02 us -> 1.94 us  [halo_plan(): last = [lax.ppermute(high, 'comp', z_up), lax.ppermute(low, 'comp', z_down)]]
  transfers between devices with their start and end apart: 21 -> 21, of which waited for: 3 -> 5; matrix products, arithmetic and copies ran while one was open for 1% -> 0% of each run, Pallas kernels for 32% -> 28%
where the time goes in v4:
time: 162 us; the launch traced here: 160 us
  starting transfers between devices  66.5 us (41%)
  Pallas kernels  49 us (30%)
  waiting for transfers between devices  41.5 us (26%)
  local copies, waits for them, and re-layouts  2.7 us (2%)
    ppermute x3, starting transfers between devices, halo_plan(): sides_in.append(lax.ppermute(message, 'lat', sides))  32.2 us
    pallas_call x5, Pallas kernels, propagate(): pl.pallas_call(kernel, out_shape=[jax.ShapeDtypeStruct((ND, rows, LANES),...  25.6 us
    ppermute x3, waiting for transfers between devices, halo_plan(): sides_in.append(lax.ppermute(message, 'lat', sides))  24.4 us
    ppermute x8, starting transfers between devices, halo_plan(): last = [lax.ppermute(high, 'comp', z_up), lax.ppermute(low, 'comp', z_down)]  24.3 us
    ppermute x1, waiting for transfers between devices, halo_plan(): sides_in = [lax.ppermute(head, 'lat', sides)]  13.1 us
    pallas_call x2, Pallas kernels, quadruplets(): pl.pallas_call(kernel, out_shape=[vmem(((local + 2 * reach) * ND, rows, L...  11.1 us
    pallas_call x3, Pallas kernels, pack_message(): pl.pallas_call(kernel, out_shape=vmem(shape), in_specs=[whole(pltpu.SMEM)...  6.55 us
    pallas_call x2, Pallas kernels, load(): pl.pallas_call(kernel, out_shape=[vmem((size, rows, LANES)) for size in s...  5.77 us
  transfers between devices with their start and end apart: 21, of which 5 were waited for; matrix products, arithmetic and copies ran while one was open for 0% of the time, Pallas kernels for 28%

profile of v4, /device:TPU:2, one launch (start us, length us, event | category | flops | bytes accessed | tf_op | source)
XLA Modules:
  0.0 160.4 jit_solution(13327308045109330932)
XLA Ops:
  0.0 3.2 %load.3 = (f32[64,32,128]{2,1,0:T(8,128)}, f32[96,32,128]{2,1,0:T(8,128)}) custom-call(f32[288,32,128]{2,1,0:T(8,128)} %bitcast.23), custom_call_target="tpu_custom_call" | custom-call | bytes 5242880 | tf_op jit(solution)/shard_map/load/pallas_call | solution.py:154
  4.0 1.7 %collective-permute-start.16 = (f32[64,32,128]{2,1,0:T(8,128)}, f32[64,32,128]{2,1,0:T(8,128)}, u32[]{:S(2)}, u32[]{:S(2)}) collective-permute-start(f32[64,32,128]{2,1,0:T(8,128)} %get-tuple-element.31), channel_id=1, source_target_pairs={{3,6},{4,1},{11,14},{12,9},{19,22},{20,17},{27,30},{28,25}} | collective-permute-start | bytes 3145736 | tf_op jit(solution)/shard_map/ppermute | solution.py:396
  5.7 2.6 %load.2 = (f32[65,32,128]{2,1,0:T(8,128)S(1)}, f32[64,32,128]{2,1,0:T(8,128)}, f32[1,32,128]{2,1,0:T(8,128)S(1)}) custom-call(f32[288,32,128]{2,1,0:T(8,128)} %bitcast.24, s32[1,32,128]{2,1,0:T(8,128)S(1)} %bitcast.19), custom_call_target="tpu_custom_call" | custom-call | bytes 4194304 | tf_op jit(solution)/shard_map/load/pallas_call | solution.py:154
  10.1 2.1 %pack_message.3 = f32[96,32,128]{2,1,0:T(8,128)S(1)} custom-call(f32[288]{0:T(512)S(1)} %copy-done.12, s32[2]{0:T(128)S(1)} %pad_add_fusion.place_ref, f32[288,32,128]{2,1,0:T(8,128)} %bitcast.25, f32[96,32,128]{2,1,0:T(8,128)S(1)} %collective-permute-done.4.other_ref), custom_call_target="tpu_custom_call" | custom-call | bytes 4718592 | tf_op jit(solution)/shard_map/pack_message/pallas_call | solution.py:189
  12.2 16.4 %collective-permute-start.5 = (f32[96,32,128]{2,1,0:T(8,128)S(1)}, f32[96,32,128]{2,1,0:T(8,128)S(1)}, u32[]{:S(2)}, u32[]{:S(2)}) collective-permute-start(f32[96,32,128]{2,1,0:T(8,128)S(1)} %pack_message.3), channel_id=1, source_target_pairs={{1,2},{5,6},{2,1},{6,5},{9,10},{13,14},{10,9},{14,13},{17,18},{21,... | collective-permute-start | bytes 4718600 | tf_op jit(solution)/shard_map/ppermute | solution.py:402
  28.6 1.9 %collective-permute-start.2 = (f32[65,32,128]{2,1,0:T(8,128)S(1)}, f32[65,32,128]{2,1,0:T(8,128)S(1)}, u32[]{:S(2)}, u32[]{:S(2)}) collective-permute-start(f32[65,32,128]{2,1,0:T(8,128)S(1)} %copy-done.18), channel_id=1, source_target_pairs={{1,2},{5,6},{2,1},{6,5},{9,10},{13,14},{10,9},{14,13},{17,18},{21,... | collective-permute-start | bytes 3194888 | tf_op jit(solution)/shard_map/ppermute | solution.py:393
  30.5 2.6 %pack_message.5 = f32[64,32,128]{2,1,0:T(8,128)S(1)} custom-call(f32[288]{0:T(512)S(1)} %copy-done.12, s32[2]{0:T(128)S(1)} %pad_add_fusion.place_ref, f32[288,32,128]{2,1,0:T(8,128)} %bitcast.26, f32[64,32,128]{2,1,0:T(8,128)} %collective-permute-done.16.other_ref), custom_call_target="tpu_custom_call" | custom-call | bytes 3145728 | tf_op jit(solution)/shard_map/pack_message/pallas_call | solution.py:189
  33.1 7.3 %collective-permute-start.17 = (f32[64,32,128]{2,1,0:T(8,128)S(1)}, f32[64,32,128]{2,1,0:T(8,128)S(1)}, u32[]{:S(2)}, u32[]{:S(2)}) collective-permute-start(f32[64,32,128]{2,1,0:T(8,128)S(1)} %pack_message.5), channel_id=1, source_target_pairs={{1,2},{5,6},{2,1},{6,5},{9,10},{13,14},{10,9},{14,13},{17,18},{21,... | collective-permute-start | bytes 3145736 | tf_op jit(solution)/shard_map/ppermute | solution.py:402
  40.4 1.9 %pack_message.4 = f32[64,32,128]{2,1,0:T(8,128)S(1)} custom-call(f32[288]{0:T(512)S(1)} %copy-done.12, s32[2]{0:T(128)S(1)} %pad_add_fusion.place_ref, f32[288,32,128]{2,1,0:T(8,128)} %bitcast.27, f32[64,32,128]{2,1,0:T(8,128)S(1)} %collective-permute-done.11.other_ref), custom_call_target="tpu_custom_call" | custom-call | bytes 3145728 | tf_op jit(solution)/shard_map/pack_message/pallas_call | solution.py:189
  42.4 8.5 %collective-permute-start.12 = (f32[64,32,128]{2,1,0:T(8,128)S(1)}, f32[64,32,128]{2,1,0:T(8,128)S(1)}, u32[]{:S(2)}, u32[]{:S(2)}) collective-permute-start(f32[64,32,128]{2,1,0:T(8,128)S(1)} %pack_message.4), channel_id=1, source_target_pairs={{1,2},{5,6},{2,1},{6,5},{9,10},{13,14},{10,9},{14,13},{17,18},{21,... | collective-permute-start | bytes 3145736 | tf_op jit(solution)/shard_map/ppermute | solution.py:402
  50.9 13.1 %collective-permute-done.2.side_ref = f32[65,32,128]{2,1,0:T(8,128)S(1)} collective-permute-done((f32[65,32,128]{2,1,0:T(8,128)S(1)}, f32[65,32,128]{2,1,0:T(8,128)S(1)}, u32[]{:S(2)}, u32[]{:S(2)}) %collective-permute-start.2) | collective-permute-done | bytes 1064992 | tf_op jit(solution)/shard_map/ppermute | solution.py:393
  64.7 1.4 collective-permute-start.6
  66.1 14.5 %collective-permute-done.17.side_ref = f32[64,32,128]{2,1,0:T(8,128)S(1)} collective-permute-done((f32[64,32,128]{2,1,0:T(8,128)S(1)}, f32[64,32,128]{2,1,0:T(8,128)S(1)}, u32[]{:S(2)}, u32[]{:S(2)}) %collective-permute-start.17) | collective-permute-done | bytes 1048608 | tf_op jit(solution)/shard_map/ppermute | solution.py:402
  80.6 1.3 collective-permute-start.18
  81.9 9.9 %collective-permute-done.12.side_ref = f32[64,32,128]{2,1,0:T(8,128)S(1)} collective-permute-done((f32[64,32,128]{2,1,0:T(8,128)S(1)}, f32[64,32,128]{2,1,0:T(8,128)S(1)}, u32[]{:S(2)}, u32[]{:S(2)}) %collective-permute-start.12) | collective-permute-done | bytes 1048608 | tf_op jit(solution)/shard_map/ppermute | solution.py:402
  91.8 1.3 collective-permute-start.13
  93.2 2.1 %collective-permute-done = f32[1,32,128]{2,1,0:T(8,128)S(1)} collective-permute-done((f32[1,32,128]{2,1,0:T(8,128)S(1)}, f32[1,32,128]{2,1,0:T(8,128)S(1)}, u32[]{:S(2)}, u32[]{:S(2)}) %collective-permute-start) | collective-permute-done | bytes 16416 | tf_op jit(solution)/shard_map/ppermute | solution.py:397
  95.4 4.9 %propagate.6 = (f32[32,32,128]{2,1,0:T(8,128)S(1)}, f32[32,32,128]{2,1,0:T(8,128)S(1)}) custom-call(f32[288]{0:T(512)S(1)} %copy-done.12, f32[288]{0:T(512)S(1)} %copy-done.13, s32[2]{0:T(128)S(1)} %pad_add_fusion.place_ref, f32[3,32,128]{2,1,0:T(8,128)S(1)} %pad_maximum_fusion.mask_ref, f32[288,32,128]{2,1,0:T(8,128)} %bitcast.28, ...), custom_call_target="tpu_custom_call" | custom-call | flops 10485760 | bytes 5242880 | tf_op jit(solution)/shard_map/propagate/pallas_call | solution.py:287
  100.3 1.3 collective-permute-start.10
  101.6 5.4 %collective-permute-start.9 = (f32[32,32,128]{2,1,0:T(8,128)S(1)}, f32[32,32,128]{2,1,0:T(8,128)S(1)}, u32[]{:S(2)}, u32[]{:S(2)}) collective-permute-start(f32[32,32,128]{2,1,0:T(8,128)S(1)} %get-tuple-element.27.refs_1_), channel_id=1, source_target_pairs={{0,8},{8,16},{16,24},{1,9},{9,17},{17,25},{2,10},{10,18},{18,26},{... | collective-permute-start | bytes 1572872 | tf_op jit(solution)/shard_map/ppermute | solution.py:416
  107.0 5.7 %propagate.8 = (f32[32,32,128]{2,1,0:T(8,128)S(1)}, f32[32,32,128]{2,1,0:T(8,128)}) custom-call(f32[288]{0:T(512)S(1)} %copy-done.12, f32[288]{0:T(512)S(1)} %copy-done.13, s32[2]{0:T(128)S(1)} %pad_add_fusion.place_ref, f32[3,32,128]{2,1,0:T(8,128)S(1)} %pad_maximum_fusion.mask_ref, f32[288,32,128]{2,1,0:T(8,128)} %bitcast.29, ...), custom_call_target="tpu_custom_call" | custom-call | flops 10485760 | bytes 5242880 | tf_op jit(solution)/shard_map/propagate/pallas_call | solution.py:287
  112.8 1.3 collective-permute-start.20
  114.1 5.4 %collective-permute-start.19 = (f32[32,32,128]{2,1,0:T(8,128)}, f32[32,32,128]{2,1,0:T(8,128)}, u32[]{:S(2)}, u32[]{:S(2)}) collective-permute-start(f32[32,32,128]{2,1,0:T(8,128)} %get-tuple-element.33.refs_9_), channel_id=1, source_target_pairs={{0,8},{8,16},{16,24},{1,9},{9,17},{17,25},{2,10},{10,18},{18,26},{... | collective-permute-start | bytes 1572872 | tf_op jit(solution)/shard_map/ppermute | solution.py:416
  119.4 5.6 %propagate.7 = (f32[32,32,128]{2,1,0:T(8,128)}, f32[32,32,128]{2,1,0:T(8,128)}) custom-call(f32[288]{0:T(512)S(1)} %copy-done.12, f32[288]{0:T(512)S(1)} %copy-done.13, s32[2]{0:T(128)S(1)} %pad_add_fusion.place_ref, f32[3,32,128]{2,1,0:T(8,128)S(1)} %pad_maximum_fusion.mask_ref, f32[288,32,128]{2,1,0:T(8,128)} %bitcast.30, ...), custom_call_target="tpu_custom_call" | custom-call | flops 10485760 | bytes 5242880 | tf_op jit(solution)/shard_map/propagate/pallas_call | solution.py:287
  125.1 1.3 collective-permute-start.15
  126.4 5.4 %collective-permute-start.14 = (f32[32,32,128]{2,1,0:T(8,128)}, f32[32,32,128]{2,1,0:T(8,128)}, u32[]{:S(2)}, u32[]{:S(2)}) collective-permute-start(f32[32,32,128]{2,1,0:T(8,128)} %get-tuple-element.30.refs_5_), channel_id=1, source_target_pairs={{0,8},{8,16},{16,24},{1,9},{9,17},{17,25},{2,10},{10,18},{18,26},{... | collective-permute-start | bytes 1572872 | tf_op jit(solution)/shard_map/ppermute | solution.py:416
  131.8 5.7 %propagate.5 = (f32[32,32,128]{2,1,0:T(8,128)}, f32[32,32,128]{2,1,0:T(8,128)}) custom-call(f32[288]{0:T(512)S(1)} %copy-done.12, f32[288]{0:T(512)S(1)} %copy-done.13, s32[2]{0:T(128)S(1)} %pad_add_fusion.place_ref, f32[3,32,128]{2,1,0:T(8,128)S(1)} %pad_maximum_fusion.mask_ref, f32[288,32,128]{2,1,0:T(8,128)} %bitcast.31, ...), custom_call_target="tpu_custom_call" | custom-call | flops 10485760 | bytes 5242880 | tf_op jit(solution)/shard_map/propagate/pallas_call | solution.py:287
  138.3 3.1 %collective-permute-start.7 = (f32[32,32,128]{2,1,0:T(8,128)}, f32[32,32,128]{2,1,0:T(8,128)}, u32[]{:S(2)}, u32[]{:S(2)}) collective-permute-start(f32[32,32,128]{2,1,0:T(8,128)} %get-tuple-element.24.refs_13_), channel_id=1, source_target_pairs={{0,8},{8,16},{16,24},{1,9},{9,17},{17,25},{2,10},{10,18},{18,26},{... | collective-permute-start | bytes 1572872 | tf_op jit(solution)/shard_map/ppermute | solution.py:416
  143.6 3.6 %propagate.9.refs_14_ = f32[32,32,128]{2,1,0:T(8,128)S(1)} custom-call(f32[288]{0:T(512)S(1)} %copy-done.12, f32[288]{0:T(512)S(1)} %copy-done.13, s32[2]{0:T(128)S(1)} %pad_add_fusion.place_ref, f32[3,32,128]{2,1,0:T(8,128)S(1)} %pad_maximum_fusion.mask_ref, f32[288,32,128]{2,1,0:T(8,128)} %bitcast.32, f32[288,32,128]{2,1,0:T(8,128)} %collective-permute-done.3.mate_hbm, ...), custom_call_target="tpu_custom_call" | custom-call | flops 5242880 | bytes 2621440 | tf_op jit(solution)/shard_map/propagate/pallas_call | solution.py:287
  147.4 7.5 %quadruplets.2 = (f32[544,32,128]{2,1,0:T(8,128)S(1)}, f32[288,32,128]{2,1,0:T(8,128)}) custom-call(f32[1152]{0:T(1024)S(1)} %copy-done.14, s32[2,4]{1,0:T(2,128)S(1)} %bitcast.20, s32[1]{0:T(128)} %bitcast.1.first_ref, f32[32,32,128]{2,1,0:T(8,128)S(1)} %copy-done.1, f32[32,32,128]{2,1,0:T(8,128)S(1)} %copy-done.3, f32[32,32,128]{2,1,0:T(8,128)S(1)} %copy-done.7, ...), custom_call_target="tpu_custom_call" | custom-call | flops 13762560 | bytes 22020096 | tf_op jit(solution)/shard_map/quadruplets/pallas_call | solution.py:347
  154.9 1.9 %collective-permute-done.8.refs_1_ = f32[32,32,128]{2,1,0:T(8,128)} collective-permute-done((f32[32,32,128]{2,1,0:T(8,128)}, f32[32,32,128]{2,1,0:T(8,128)}, u32[]{:S(2)}, u32[]{:S(2)}) %collective-permute-start.8) | collective-permute-done | bytes 524320 | tf_op jit(solution)/shard_map/ppermute | solution.py:416
  156.8 3.6 %quadruplets.3 = (f32[544,32,128]{2,1,0:T(8,128)S(1)}, f32[288,32,128]{2,1,0:T(8,128)}) custom-call(f32[1152]{0:T(1024)S(1)} %copy-done.14, s32[2,4]{1,0:T(2,128)S(1)} %bitcast.21, s32[1]{0:T(128)} %bitcast.1.first_ref, f32[32,32,128]{2,1,0:T(8,128)} %collective-permute-done.7.refs_0_, ...), custom_call_target="tpu_custom_call", output_to_operand_aliasing={{0}: (5, {}), {1}: (6, {})} | custom-call | flops 3932160 | bytes 6291456 | tf_op jit(solution)/shard_map/quadruplets/pallas_call | solution.py:347
  (63 shorter events, 6.4 us)
Async XLA Ops:
  0.0 5.7 %copy-start.15 = (s32[2,2048]{1,0:T(2,128)S(1)}, s32[2,2048]{1,0:T(2,128)}, u32[]{:S(2)}) copy-start(s32[2,2048]{1,0:T(2,128)} %param.9) | copy-start | bytes 49156
  0.0 95.4 %collective-permute-start.3 = (f32[288,32,128]{2,1,0:T(8,128)}, f32[288,32,128]{2,1,0:T(8,128)}, u32[]{:S(2)}, u32[]{:S(2)}) collective-permute-start(f32[288,32,128]{2,1,0:T(8,128)} %bitcast.22), channel_id=1, source_target_pairs={{0,1},{1,0},{2,3},{3,2},{4,5},{5,4},{6,7},{7,6},{8,9},{9,8},{10,11... | collective-permute-start | bytes 14155784 | tf_op jit(solution)/shard_map/ppermute | solution.py:398
  3.2 6.9 %collective-permute-start.4 = (f32[96,32,128]{2,1,0:T(8,128)}, f32[96,32,128]{2,1,0:T(8,128)S(1)}, u32[]{:S(2)}, u32[]{:S(2)}) collective-permute-start(f32[96,32,128]{2,1,0:T(8,128)} %get-tuple-element.23), channel_id=1, source_target_pairs={{3,6},{4,1},{11,14},{12,9},{19,22},{20,17},{27,30},{28,25}} | collective-permute-start | bytes 4718600 | tf_op jit(solution)/shard_map/ppermute | solution.py:396
  4.0 26.5 %collective-permute-start.16 = (f32[64,32,128]{2,1,0:T(8,128)}, f32[64,32,128]{2,1,0:T(8,128)}, u32[]{:S(2)}, u32[]{:S(2)}) collective-permute-start(f32[64,32,128]{2,1,0:T(8,128)} %get-tuple-element.31), channel_id=1, source_target_pairs={{3,6},{4,1},{11,14},{12,9},{19,22},{20,17},{27,30},{28,25}} | collective-permute-start | bytes 3145736 | tf_op jit(solution)/shard_map/ppermute | solution.py:396
  5.7 4.4 %copy-start.12 = (f32[288]{0:T(512)S(1)}, f32[288]{0:T(512)}, u32[]{:S(2)}) copy-start(f32[288]{0:T(512)} %a_ref.15) | copy-start | bytes 3460
  9.3 31.1 %collective-permute-start.11 = (f32[64,32,128]{2,1,0:T(8,128)}, f32[64,32,128]{2,1,0:T(8,128)S(1)}, u32[]{:S(2)}, u32[]{:S(2)}) collective-permute-start(f32[64,32,128]{2,1,0:T(8,128)} %get-tuple-element.28), channel_id=1, source_target_pairs={{3,6},{4,1},{11,14},{12,9},{19,22},{20,17},{27,30},{28,25}} | collective-permute-start | bytes 3145736 | tf_op jit(solution)/shard_map/ppermute | solution.py:394
  10.1 18.4 %copy-start.18 = (f32[65,32,128]{2,1,0:T(8,128)S(1)}, f32[65,32,128]{2,1,0:T(8,128)}, u32[]{:S(2)}) copy-start(f32[65,32,128]{2,1,0:T(8,128)} %copy-done.17) | copy-start | bytes 3194884
  12.2 52.5 %collective-permute-start.5 = (f32[96,32,128]{2,1,0:T(8,128)S(1)}, f32[96,32,128]{2,1,0:T(8,128)S(1)}, u32[]{:S(2)}, u32[]{:S(2)}) collective-permute-start(f32[96,32,128]{2,1,0:T(8,128)S(1)} %pack_message.3), channel_id=1, source_target_pairs={{1,2},{5,6},{2,1},{6,5},{9,10},{13,14},{10,9},{14,13},{17,18},{21,... | collective-permute-start | bytes 4718600 | tf_op jit(solution)/shard_map/ppermute | solution.py:402
  28.6 35.4 %collective-permute-start.2 = (f32[65,32,128]{2,1,0:T(8,128)S(1)}, f32[65,32,128]{2,1,0:T(8,128)S(1)}, u32[]{:S(2)}, u32[]{:S(2)}) collective-permute-start(f32[65,32,128]{2,1,0:T(8,128)S(1)} %copy-done.18), channel_id=1, source_target_pairs={{1,2},{5,6},{2,1},{6,5},{9,10},{13,14},{10,9},{14,13},{17,18},{21,... | collective-permute-start | bytes 3194888 | tf_op jit(solution)/shard_map/ppermute | solution.py:393
  33.1 62.3 %copy-start.13 = (f32[288]{0:T(512)S(1)}, f32[288]{0:T(512)}, u32[]{:S(2)}) copy-start(f32[288]{0:T(512)} %b_ref.9) | copy-start | bytes 3460
  33.1 47.4 %collective-permute-start.17 = (f32[64,32,128]{2,1,0:T(8,128)S(1)}, f32[64,32,128]{2,1,0:T(8,128)S(1)}, u32[]{:S(2)}, u32[]{:S(2)}) collective-permute-start(f32[64,32,128]{2,1,0:T(8,128)S(1)} %pack_message.5), channel_id=1, source_target_pairs={{1,2},{5,6},{2,1},{6,5},{9,10},{13,14},{10,9},{14,13},{17,18},{21,... | collective-permute-start | bytes 3145736 | tf_op jit(solution)/shard_map/ppermute | solution.py:402
  42.4 49.4 %collective-permute-start.12 = (f32[64,32,128]{2,1,0:T(8,128)S(1)}, f32[64,32,128]{2,1,0:T(8,128)S(1)}, u32[]{:S(2)}, u32[]{:S(2)}) collective-permute-start(f32[64,32,128]{2,1,0:T(8,128)S(1)} %pack_message.4), channel_id=1, source_target_pairs={{1,2},{5,6},{2,1},{6,5},{9,10},{13,14},{10,9},{14,13},{17,18},{21,... | collective-permute-start | bytes 3145736 | tf_op jit(solution)/shard_map/ppermute | solution.py:402
  64.0 29.2 %collective-permute-start.1 = (f32[65,32,128]{2,1,0:T(8,128)S(1)}, f32[65,32,128]{2,1,0:T(8,128)S(1)}, u32[]{:S(2)}, u32[]{:S(2)}) collective-permute-start(f32[65,32,128]{2,1,0:T(8,128)S(1)} %copy-done.18), channel_id=1, source_target_pairs={{3,4},{4,3},{11,12},{12,11},{19,20},{20,19},{27,28},{28,27}} | collective-permute-start | bytes 3194888 | tf_op jit(solution)/shard_map/ppermute | solution.py:392
  64.7 60.4 %collective-permute-start.6 = (f32[96,32,128]{2,1,0:T(8,128)S(1)}, f32[96,32,128]{2,1,0:T(8,128)S(1)}, u32[]{:S(2)}, u32[]{:S(2)}) collective-permute-start(f32[96,32,128]{2,1,0:T(8,128)S(1)} %collective-permute-done.5.side_ref), channel_id=1, source_target_pairs={{5,4},{2,3},{13,12},{10,11},{21,20},{18,19},{29,28},{26,27}} | collective-permute-start | bytes 4718600 | tf_op jit(solution)/shard_map/ppermute | solution.py:403
  80.6 26.5 %collective-permute-start.18 = (f32[64,32,128]{2,1,0:T(8,128)S(1)}, f32[64,32,128]{2,1,0:T(8,128)S(1)}, u32[]{:S(2)}, u32[]{:S(2)}) collective-permute-start(f32[64,32,128]{2,1,0:T(8,128)S(1)} %collective-permute-done.17.side_ref), channel_id=1, source_target_pairs={{5,4},{2,3},{13,12},{10,11},{21,20},{18,19},{29,28},{26,27}} | collective-permute-start | bytes 3145736 | tf_op jit(solution)/shard_map/ppermute | solution.py:403
  91.8 22.3 %collective-permute-start.13 = (f32[64,32,128]{2,1,0:T(8,128)S(1)}, f32[64,32,128]{2,1,0:T(8,128)S(1)}, u32[]{:S(2)}, u32[]{:S(2)}) collective-permute-start(f32[64,32,128]{2,1,0:T(8,128)S(1)} %collective-permute-done.12.side_ref), channel_id=1, source_target_pairs={{5,4},{2,3},{13,12},{10,11},{21,20},{18,19},{29,28},{26,27}} | collective-permute-start | bytes 3145736 | tf_op jit(solution)/shard_map/ppermute | solution.py:403
  93.2 2.2 %collective-permute-start = (f32[1,32,128]{2,1,0:T(8,128)S(1)}, f32[1,32,128]{2,1,0:T(8,128)S(1)}, u32[]{:S(2)}, u32[]{:S(2)}) collective-permute-start(f32[1,32,128]{2,1,0:T(8,128)S(1)} %get-tuple-element.21), channel_id=1, source_target_pairs={{0,1},{1,0},{2,3},{3,2},{4,5},{5,4},{6,7},{7,6},{8,9},{9,8},{10,11... | collective-permute-start | bytes 49160 | tf_op jit(solution)/shard_map/ppermute | solution.py:397
  100.3 12.4 %copy-start = (f32[32,32,128]{2,1,0:T(8,128)}, f32[32,32,128]{2,1,0:T(8,128)S(1)}, u32[]{:S(2)}) copy-start(f32[32,32,128]{2,1,0:T(8,128)S(1)} %get-tuple-element.26.refs_0_) | copy-start | bytes 1572868
  100.3 12.4 %copy-start.2 = (f32[32,32,128]{2,1,0:T(8,128)}, f32[32,32,128]{2,1,0:T(8,128)S(1)}, u32[]{:S(2)}) copy-start(f32[32,32,128]{2,1,0:T(8,128)S(1)} %get-tuple-element.27.refs_1_) | copy-start | bytes 1572868
  100.3 26.1 %collective-permute-start.10 = (f32[32,32,128]{2,1,0:T(8,128)S(1)}, f32[32,32,128]{2,1,0:T(8,128)S(1)}, u32[]{:S(2)}, u32[]{:S(2)}) collective-permute-start(f32[32,32,128]{2,1,0:T(8,128)S(1)} %get-tuple-element.26.refs_0_), channel_id=1, source_target_pairs={{8,0},{16,8},{24,16},{9,1},{17,9},{25,17},{10,2},{18,10},{26,18},{... | collective-permute-start | bytes 1572872 | tf_op jit(solution)/shard_map/ppermute | solution.py:416
  101.6 35.9 %collective-permute-start.9 = (f32[32,32,128]{2,1,0:T(8,128)S(1)}, f32[32,32,128]{2,1,0:T(8,128)S(1)}, u32[]{:S(2)}, u32[]{:S(2)}) collective-permute-start(f32[32,32,128]{2,1,0:T(8,128)S(1)} %get-tuple-element.27.refs_1_), channel_id=1, source_target_pairs={{0,8},{8,16},{16,24},{1,9},{9,17},{17,25},{2,10},{10,18},{18,26},{... | collective-permute-start | bytes 1572872 | tf_op jit(solution)/shard_map/ppermute | solution.py:416
  112.8 12.3 %copy-start.8 = (f32[32,32,128]{2,1,0:T(8,128)}, f32[32,32,128]{2,1,0:T(8,128)S(1)}, u32[]{:S(2)}) copy-start(f32[32,32,128]{2,1,0:T(8,128)S(1)} %get-tuple-element.32.refs_8_) | copy-start | bytes 1572868
  112.8 28.6 %collective-permute-start.20 = (f32[32,32,128]{2,1,0:T(8,128)S(1)}, f32[32,32,128]{2,1,0:T(8,128)S(1)}, u32[]{:S(2)}, u32[]{:S(2)}) collective-permute-start(f32[32,32,128]{2,1,0:T(8,128)S(1)} %get-tuple-element.32.refs_8_), channel_id=1, source_target_pairs={{8,0},{16,8},{24,16},{9,1},{17,9},{25,17},{10,2},{18,10},{26,18},{... | collective-permute-start | bytes 1572872 | tf_op jit(solution)/shard_map/ppermute | solution.py:416
  114.1 33.2 %collective-permute-start.19 = (f32[32,32,128]{2,1,0:T(8,128)}, f32[32,32,128]{2,1,0:T(8,128)}, u32[]{:S(2)}, u32[]{:S(2)}) collective-permute-start(f32[32,32,128]{2,1,0:T(8,128)} %get-tuple-element.33.refs_9_), channel_id=1, source_target_pairs={{0,8},{8,16},{16,24},{1,9},{9,17},{17,25},{2,10},{10,18},{18,26},{... | collective-permute-start | bytes 1572872 | tf_op jit(solution)/shard_map/ppermute | solution.py:416
  125.1 22.2 %collective-permute-start.15 = (f32[32,32,128]{2,1,0:T(8,128)}, f32[32,32,128]{2,1,0:T(8,128)}, u32[]{:S(2)}, u32[]{:S(2)}) collective-permute-start(f32[32,32,128]{2,1,0:T(8,128)} %get-tuple-element.29.refs_4_), channel_id=1, source_target_pairs={{8,0},{16,8},{24,16},{9,1},{17,9},{25,17},{10,2},{18,10},{26,18},{... | collective-permute-start | bytes 1572872 | tf_op jit(solution)/shard_map/ppermute | solution.py:416
  126.4 11.1 %copy-start.4 = (f32[32,32,128]{2,1,0:T(8,128)}, f32[32,32,128]{2,1,0:T(8,128)S(1)}, u32[]{:S(2)}) copy-start(f32[32,32,128]{2,1,0:T(8,128)S(1)} %collective-permute-done.10.refs_3_) | copy-start | bytes 1572868
  126.4 20.9 %collective-permute-start.14 = (f32[32,32,128]{2,1,0:T(8,128)}, f32[32,32,128]{2,1,0:T(8,128)}, u32[]{:S(2)}, u32[]{:S(2)}) collective-permute-start(f32[32,32,128]{2,1,0:T(8,128)} %get-tuple-element.30.refs_5_), channel_id=1, source_target_pairs={{0,8},{8,16},{16,24},{1,9},{9,17},{17,25},{2,10},{10,18},{18,26},{... | collective-permute-start | bytes 1572872 | tf_op jit(solution)/shard_map/ppermute | solution.py:416
  138.3 16.5 %collective-permute-start.7 = (f32[32,32,128]{2,1,0:T(8,128)}, f32[32,32,128]{2,1,0:T(8,128)}, u32[]{:S(2)}, u32[]{:S(2)}) collective-permute-start(f32[32,32,128]{2,1,0:T(8,128)} %get-tuple-element.24.refs_13_), channel_id=1, source_target_pairs={{0,8},{8,16},{16,24},{1,9},{9,17},{17,25},{2,10},{10,18},{18,26},{... | collective-permute-start | bytes 1572872 | tf_op jit(solution)/shard_map/ppermute | solution.py:416
  142.2 14.5 %collective-permute-start.8 = (f32[32,32,128]{2,1,0:T(8,128)}, f32[32,32,128]{2,1,0:T(8,128)}, u32[]{:S(2)}, u32[]{:S(2)}) collective-permute-start(f32[32,32,128]{2,1,0:T(8,128)} %get-tuple-element.25.refs_12_), channel_id=1, source_target_pairs={{8,0},{16,8},{24,16},{9,1},{17,9},{25,17},{10,2},{18,10},{26,18},{... | collective-permute-start | bytes 1572872 | tf_op jit(solution)/shard_map/ppermute | solution.py:416
  143.5 3.8 %copy-start.1 = (f32[32,32,128]{2,1,0:T(8,128)S(1)}, f32[32,32,128]{2,1,0:T(8,128)}, u32[]{:S(2)}) copy-start(f32[32,32,128]{2,1,0:T(8,128)} %copy-done) | copy-start | bytes 1572868
  143.5 3.8 %copy-start.3 = (f32[32,32,128]{2,1,0:T(8,128)S(1)}, f32[32,32,128]{2,1,0:T(8,128)}, u32[]{:S(2)}) copy-start(f32[32,32,128]{2,1,0:T(8,128)} %copy-done.2) | copy-start | bytes 1572868
  143.6 3.8 %copy-start.5 = (f32[32,32,128]{2,1,0:T(8,128)S(1)}, f32[32,32,128]{2,1,0:T(8,128)}, u32[]{:S(2)}) copy-start(f32[32,32,128]{2,1,0:T(8,128)} %copy-done.4) | copy-start | bytes 1572868
  (8 other events, 21.5 us)

commit v5 on v4

--- a/solution.py
+++ b/solution.py
@@ -84,6 +84,8 @@
 
 LANES = 128
 PAIR = 2
+GROUP = 4
+CUTS = (0, 3, 8, 13, 16)
 
 
 def vmem(shape):
@@ -124,10 +126,21 @@
     return cells.reshape(comp_dev, lat_dev, blocks * LANES)
 
 
+def total(spans):
+    return sum(length for _, length in spans)
+
+
+def laid(spans):
+    at = 0
+    for start, length in spans:
+        yield at, start, length
+        at += length
+
+
 def load(own, chunks, extra=None):
-    spots = [(c, n, f) for c, freqs in enumerate(chunks) for n, f in enumerate(freqs)]
+    spots = [(c, at, start, length) for c, spans in enumerate(chunks) for at, start, length in laid(spans)]
     rows = own.shape[1]
-    ends = [len(freqs) * ND for freqs in chunks]
+    ends = [total(spans) for spans in chunks]
     sizes = list(ends)
     operands = [own]
     if extra is not None:
@@ -139,8 +152,8 @@
         sems = refs[-1]
         out_refs = refs[len(operands) - 1:-1]
         copies = [
-            pltpu.make_async_copy(own_ref.at[pl.ds(f * ND, ND)], out_refs[c].at[pl.ds(n * ND, ND)], sems.at[m])
-            for m, (c, n, f) in enumerate(spots)
+            pltpu.make_async_copy(own_ref.at[pl.ds(start, length)], out_refs[c].at[pl.ds(at, length)], sems.at[m])
+            for m, (c, at, start, length) in enumerate(spots)
         ]
         for one in copies:
             one.start()
@@ -158,78 +171,80 @@
         out_specs=[whole(pltpu.VMEM)] * len(sizes),
         scratch_shapes=[pltpu.SemaphoreType.DMA((len(spots),))],
         compiler_params=limits(8),
-        cost_estimate=cost(0, 2 * len(spots) * ND * rows * LANES * 4),
+        cost_estimate=cost(0, 2 * sum(ends) * rows * LANES * 4),
         name="load",
     )(far_from_core(own), *operands[1:])
 
 
-def pack_message(own, other, along_lat, place, freqs):
+def pack_message(own, other, along_lat, place, spans):
     rows = own.shape[1]
 
     def kernel(a_ref, place_ref, own_ref, other_ref, out_ref, held_ref, sems):
         odd = place_ref[0] > 0
         copies = [
-            pltpu.make_async_copy(own_ref.at[pl.ds(f * ND, ND)], held_ref.at[pl.ds(n * ND, ND)], sems.at[n])
-            for n, f in enumerate(freqs)
+            pltpu.make_async_copy(own_ref.at[pl.ds(start, length)], held_ref.at[pl.ds(at, length)], sems.at[n])
+            for n, (at, start, length) in enumerate(laid(spans))
         ]
         for one in copies:
             one.start()
-        for n, f in enumerate(freqs):
+        for n, (at, start, length) in enumerate(laid(spans)):
             copies[n].wait()
 
             def one(i, carry):
-                j = n * ND + i
-                from_own = (a_ref[f * ND + i] > 0) == odd
-                out_ref[j] = jnp.where(from_own, held_ref[j], other_ref[j])
+                from_own = (a_ref[start + i] > 0) == odd
+                out_ref[at + i] = jnp.where(from_own, held_ref[at + i], other_ref[at + i])
                 return carry
 
-            lax.fori_loop(0, ND, one, 0, unroll=8)
-
-    shape = (len(freqs) * ND, rows, LANES)
+            lax.fori_loop(0, length, one, 0, unroll=8)
+
+    shape = (total(spans), rows, LANES)
     return pl.pallas_call(
         kernel,
         out_shape=vmem(shape),
         in_specs=[whole(pltpu.SMEM)] * 2 + [whole(pltpu.HBM), whole(pltpu.VMEM)],
         out_specs=whole(pltpu.VMEM),
-        scratch_shapes=[vmem(shape), pltpu.SemaphoreType.DMA((len(freqs),))],
+        scratch_shapes=[vmem(shape), pltpu.SemaphoreType.DMA((len(spans),))],
         compiler_params=limits(8),
-        cost_estimate=cost(0, 3 * len(freqs) * ND * rows * LANES * 4),
+        cost_estimate=cost(0, 3 * total(spans) * rows * LANES * 4),
         name="pack_message",
     )(along_lat, place, far_from_core(own), near_core(other))
 
 
-def propagate(own, mate, side, hand, along_lat, along_lon, place, masks, freqs, skip=0):
+def propagate(own, mate, side, hand, along_lat, along_lon, place, masks, spans, skip=0):
     rows = own.shape[1]
     half = rows // PAIR
-    size = len(freqs) * ND
+    size = total(spans)
+    count = len(spans)
 
     def kernel(a_ref, b_ref, place_ref, mask_ref, own_hbm, mate_hbm, side_ref, hand_ref, *refs):
-        out_refs = refs[:len(freqs)]
-        own_ref, mate_ref, done_ref, sems, out_sems = refs[len(freqs):]
+        out_refs = refs[:count]
+        own_ref, mate_ref, done_ref, sems, out_sems = refs[count:]
         odd = place_ref[0] > 0
         handed = place_ref[1] > 0
         lane = lax.broadcasted_iota(jnp.int32, (half, LANES), 1)
+        sub = lax.broadcasted_iota(jnp.int32, (8, LANES), 0)
         arrivals = [
             [
-                pltpu.make_async_copy(
-                    src.at[pl.ds(f * ND, ND)], dst.at[pl.ds(n * ND, ND)], sems.at[n, m]
-                )
+                pltpu.make_async_copy(src.at[pl.ds(start, length)], dst.at[pl.ds(at, length)], sems.at[n, m])
                 for m, (src, dst) in enumerate(((own_hbm, own_ref), (mate_hbm, mate_ref)))
             ]
-            for n, f in enumerate(freqs)
+            for n, (at, start, length) in enumerate(laid(spans))
         ]
         for pair in arrivals:
             for one in pair:
                 one.start()
         leaving = [
-            pltpu.make_async_copy(done_ref.at[pl.ds(n * ND, ND)], out_refs[n], out_sems.at[n])
-            for n in range(len(freqs))
+            pltpu.make_async_copy(done_ref.at[pl.ds(at, length)], out_refs[n], out_sems.at[n])
+            for n, (at, start, length) in enumerate(laid(spans))
         ]
 
-        def run(far_ref, n, f):
-            def one(i, carry):
-                k = f * ND + i
-                j = n * ND + i
+        def run(far_ref, at, start, length):
+            def row(ref, spot, which):
+                return ref[spot, pl.ds(which, half, stride=PAIR), :]
+
+            def prepare(i):
+                k = start + i
+                j = at + i
                 a = a_ref[k]
                 b = b_ref[k]
                 south = a > 0
@@ -237,48 +252,66 @@
                 west = b > 0
                 fore = jnp.where(south, 0, 1)
                 back = 1 - fore
-                turn = jnp.where(west, 1, LANES - 1)
-                edge = lane == jnp.where(west, 0, LANES - 1)
-                a = jnp.abs(a)
-                b = jnp.abs(b)
-
-                def row(ref, at, which):
-                    return ref[at, pl.ds(which, half, stride=PAIR), :]
-
-                def beside(x):
-                    turned = pltpu.roll(x, turn, 1)
-                    over = jnp.where(west, pltpu.roll(turned, 1, 0), pltpu.roll(turned, half - 1, 0))
-                    return jnp.where(edge, over, turned)
-
-                def moved(x, before, mask):
-                    return (x - a * (x - before) - b * (x - beside(x))) * mask
-
-                fore_mask = row(mask_ref, 0, fore)
-                back_mask = row(mask_ref, 0, back)
-                x0 = jnp.where(near, row(mate_ref, j, fore), row(far_ref, skip * ND + j, fore))
-                x1 = jnp.where(near, row(mate_ref, j, back), row(far_ref, skip * ND + j, back))
-                x2 = row(own_ref, j, fore)
-                x3 = row(own_ref, j, back)
-                y1 = moved(x1, x0, row(mask_ref, jnp.where(near, 1, 2), back))
-                y2 = moved(x2, x1, fore_mask)
-                y3 = moved(x3, x2, back_mask)
-                done_ref[j, pl.ds(fore, half, stride=PAIR), :] = moved(y2, y1, fore_mask)
-                done_ref[j, pl.ds(back, half, stride=PAIR), :] = moved(y3, y2, back_mask)
+                far = skip + j
+                return dict(
+                    j=j,
+                    a=jnp.abs(a),
+                    b=jnp.abs(b),
+                    west=west,
+                    fore=fore,
+                    back=back,
+                    turn=jnp.where(west, 1, LANES - 1),
+                    step=jnp.where(west, 1, 7),
+                    first=sub == jnp.where(west, 0, 7),
+                    edge=lane == jnp.where(west, 0, LANES - 1),
+                    fore_mask=row(mask_ref, 0, fore),
+                    back_mask=row(mask_ref, 0, back),
+                    halo_mask=row(mask_ref, jnp.where(near, 1, 2), back),
+                    x=[
+                        jnp.where(near, row(mate_ref, j, fore), row(far_ref, far, fore)),
+                        jnp.where(near, row(mate_ref, j, back), row(far_ref, far, back)),
+                        row(own_ref, j, fore),
+                        row(own_ref, j, back),
+                    ],
+                )
+
+            def beside(c, x):
+                turned = pltpu.roll(x, c["turn"], 1)
+                rolled = [pltpu.roll(turned[8 * t:8 * t + 8], c["step"], 0) for t in range(half // 8)]
+                over = [
+                    jnp.where(c["first"], jnp.where(c["west"], rolled[t - 1], rolled[(t + 1) % len(rolled)]), rolled[t])
+                    for t in range(len(rolled))
+                ]
+                return jnp.where(c["edge"], jnp.concatenate(over, 0), turned)
+
+            def moved(c, x, before, mask):
+                return (x - c["a"] * (x - before) - c["b"] * (x - beside(c, x))) * mask
+
+            def some(group, carry):
+                comps = [prepare(group * GROUP + u) for u in range(GROUP)]
+                y1 = [moved(c, c["x"][1], c["x"][0], c["halo_mask"]) for c in comps]
+                y2 = [moved(c, c["x"][2], c["x"][1], c["fore_mask"]) for c in comps]
+                y3 = [moved(c, c["x"][3], c["x"][2], c["back_mask"]) for c in comps]
+                z2 = [moved(c, v, u, c["fore_mask"]) for c, v, u in zip(comps, y2, y1)]
+                z3 = [moved(c, v, u, c["back_mask"]) for c, v, u in zip(comps, y3, y2)]
+                for c, v, u in zip(comps, z2, z3):
+                    done_ref[c["j"], pl.ds(c["fore"], half, stride=PAIR), :] = v
+                    done_ref[c["j"], pl.ds(c["back"], half, stride=PAIR), :] = u
                 return carry
 
-            lax.fori_loop(0, ND, one, 0, unroll=4)
-
-        for n, f in enumerate(freqs):
+            lax.fori_loop(0, length // GROUP, some, 0)
+
+        for n, span in enumerate(laid(spans)):
             for one in arrivals[n]:
                 one.wait()
 
             @pl.when(handed)
             def _():
-                run(hand_ref, n, f)
+                run(hand_ref, *span)
 
             @pl.when(jnp.logical_not(handed))
             def _():
-                run(side_ref, n, f)
+                run(side_ref, *span)
 
             leaving[n].start()
         for one in leaving:
@@ -286,12 +319,12 @@
 
     return pl.pallas_call(
         kernel,
-        out_shape=[jax.ShapeDtypeStruct((ND, rows, LANES), jnp.float32)] * len(freqs),
+        out_shape=[jax.ShapeDtypeStruct((length, rows, LANES), jnp.float32) for _, length in spans],
         in_specs=[whole(pltpu.SMEM)] * 3 + [whole(pltpu.VMEM)] + [whole(pltpu.HBM), whole(pl.ANY)]
         + [whole(pltpu.VMEM)] * 2,
-        out_specs=[whole(pltpu.HBM)] * len(freqs),
+        out_specs=[whole(pltpu.HBM)] * count,
         scratch_shapes=[vmem((size, rows, LANES))] * 3
-        + [pltpu.SemaphoreType.DMA((len(freqs), 2)), pltpu.SemaphoreType.DMA((len(freqs),))],
+        + [pltpu.SemaphoreType.DMA((count, 2)), pltpu.SemaphoreType.DMA((count,))],
         compiler_params=limits(8),
         cost_estimate=cost(40 * size * rows * LANES, 5 * size * rows * LANES * 4),
         name="propagate",
@@ -309,7 +342,7 @@
         part_refs = refs[:count]
         held_ref, out_ref, done, sems, part_sems = refs[-5:]
         arrivals = [
-            pltpu.make_async_copy(part_refs[n], held_ref.at[pl.ds(place * ND, ND)], part_sems.at[n])
+            pltpu.make_async_copy(part_refs[n], held_ref.at[pl.ds(place, parts[n].shape[0])], part_sems.at[n])
             for n, place in enumerate(places)
         ]
         for one in arrivals:
@@ -317,19 +350,26 @@
         for one in arrivals:
             one.wait()
         base = first_ref[0]
+        turns = [shift_ref[1, q] for q in range(NQ)]
         copies = []
         for n, f in enumerate(freqs):
-            def one(d, carry):
-                energy = held_ref[(f + reach) * ND + d]
-                total = jnp.zeros_like(energy)
-                for q in range(NQ):
-                    turned = lax.rem(d + shift_ref[1, q] + ND, ND)
-                    partner = held_ref[(f + reach + shift_ref[0, q]) * ND + turned]
-                    total = total + partner * (partner - energy)
-                done[n * ND + d] = energy + strength_ref[base + f * ND + d] * energy * total
+            bases = [(f + reach + shift_ref[0, q]) * ND for q in range(NQ)]
+
+            def some(group, carry):
+                made = []
+                for u in range(GROUP):
+                    d = group * GROUP + u
+                    energy = held_ref[(f + reach) * ND + d]
+                    summed = jnp.zeros_like(energy)
+                    for q in range(NQ):
+                        partner = held_ref[bases[q] + jnp.bitwise_and(d + turns[q], ND - 1)]
+                        summed = summed + partner * (partner - energy)
+                    made.append(energy + strength_ref[base + f * ND + d] * energy * summed)
+                for u, one in enumerate(made):
+                    done[n * ND + group * GROUP + u] = one
                 return carry
 
-            lax.fori_loop(0, ND, one, 0, unroll=4)
+            lax.fori_loop(0, ND // GROUP, some, 0)
             copies.append(
                 pltpu.make_async_copy(done.at[pl.ds(n * ND, ND)], out_ref.at[pl.ds(f * ND, ND)], sems.at[n])
             )
@@ -385,8 +425,10 @@
     own = tiled(spectrum)
     mask = tiled(sea_mask[None])
 
-    chunks = [[c, local - 1 - c] for c in range(reach)]
-    middle = list(range(reach, local - reach))
+    edge = reach * ND
+    cuts = [edge * cut // 16 for cut in CUTS]
+    chunks = [[(low, high - low), (comp_dev - high, high - low)] for low, high in zip(cuts, cuts[1:])]
+    middle = [(edge, comp_dev - 2 * edge)]
     lots = chunks[:-1] + [chunks[-1] + middle]
     head, part, maskf = load(own, lots[:2], mask)
     hands_in = [lax.ppermute(head, "lat", diagonals)]
@@ -396,33 +438,33 @@
     ahead += [lax.ppermute(part, "lat", aheads) for part in rest]
     mate_mask = lax.ppermute(maskf, "lat", mates)
     mate = lax.ppermute(own, "lat", mates)
-    for n, freqs in enumerate(lots):
+    for n, spans in enumerate(lots):
         if n:
-            message = pack_message(own, ahead[n], courant_lat, place, freqs)
+            message = pack_message(own, ahead[n], courant_lat, place, spans)
             sides_in.append(lax.ppermute(message, "lat", sides))
             hands_in.append(lax.ppermute(sides_in[n], "lat", hands))
-    size = len(chunks[0]) * ND
+    size = total(chunks[0])
     masks = jnp.concatenate([maskf, mate_mask, jnp.where(handed, hands_in[0][size:], sides_in[0][size:])])
     parts = []
     places = []
     last = []
-    for n, freqs in enumerate(chunks):
+    for n, spans in enumerate(chunks):
         low, high = propagate(
             own, far_from_core(mate) if n else mate, sides_in[n], hands_in[n],
-            courant_lat, courant_lon, place, masks, freqs,
+            courant_lat, courant_lon, place, masks, spans,
         )
         parts += [low, high]
-        places += [reach + f for f in freqs]
+        places += [edge + start for start, _ in spans]
         last = [lax.ppermute(high, "comp", z_up), lax.ppermute(low, "comp", z_down)]
-        last_places = [reach - 1 - n, reach + local + n]
-        if n < reach - 1:
+        last_places = [edge + spans[1][0] - comp_dev, edge + comp_dev + spans[0][0]]
+        if n < len(chunks) - 1:
             parts += last
             places += last_places
     parts += propagate(
         own, far_from_core(mate), sides_in[-1], hands_in[-1],
-        courant_lat, courant_lon, place, masks, middle, skip=len(chunks[-1]),
+        courant_lat, courant_lon, place, masks, middle, skip=total(chunks[-1]),
     )
-    places += [reach + f for f in middle]
+    places += [edge + start for start, _ in middle]
     shifts = quad_shift.T
     window, inner = quadruplets(
         None, parts, places, local, strength, shifts, first, list(range(1, local - 1)), None

time: 162 us -> 164 us (1.012)
  starting transfers between devices: 66.5 us -> 71.1 us
  waiting for transfers between devices: 41.5 us -> 39.2 us
    ppermute x3, waiting for transfers between devices: 24.4 us -> 0.01 us  [halo_plan(): sides_in.append(lax.ppermute(message, 'lat', sides))]
    ppermute x1, waiting for transfers between devices: 13.1 us -> 29.9 us  [halo_plan(): sides_in = [lax.ppermute(head, 'lat', sides)]]
    ppermute x3, starting transfers between devices: 32.2 us -> 36.7 us  [halo_plan(): sides_in.append(lax.ppermute(message, 'lat', sides))]
    ppermute x8, waiting for transfers between devices: 1.94 us -> 6.37 us  [halo_plan(): last = [lax.ppermute(high, 'comp', z_up), lax.ppermute(low, 'comp', z_down)]]
  transfers between devices with their start and end apart: 21 -> 21, of which waited for: 5 -> 4; matrix products, arithmetic and copies ran while one was open for 0% -> 0% of each run, Pallas kernels for 28% -> 28%
where the time goes in v5:
time: 164 us; the launch traced here: 162 us
  starting transfers between devices  71.1 us (43%)
  Pallas kernels  48.4 us (30%)
  waiting for transfers between devices  39.2 us (24%)
  local copies, waits for them, and re-layouts  2.54 us (2%)
    ppermute x3, starting transfers between devices, halo_plan(): sides_in.append(lax.ppermute(message, 'lat', sides))  36.7 us
    ppermute x1, waiting for transfers between devices, halo_plan(): sides_in = [lax.ppermute(head, 'lat', sides)]  29.9 us
    pallas_call x5, Pallas kernels, propagate(): pl.pallas_call(kernel, out_shape=[jax.ShapeDtypeStruct((length, rows, LAN...  25.5 us
    ppermute x8, starting transfers between devices, halo_plan(): last = [lax.ppermute(high, 'comp', z_up), lax.ppermute(low, 'comp', z_down)]  24.3 us
    pallas_call x2, Pallas kernels, quadruplets(): pl.pallas_call(kernel, out_shape=[vmem(((local + 2 * reach) * ND, rows, L...  10.3 us
    pallas_call x3, Pallas kernels, pack_message(): pl.pallas_call(kernel, out_shape=vmem(shape), in_specs=[whole(pltpu.SMEM)...  6.8 us
    ppermute x8, waiting for transfers between devices, halo_plan(): last = [lax.ppermute(high, 'comp', z_up), lax.ppermute(low, 'comp', z_down)]  6.37 us
    pallas_call x2, Pallas kernels, load(): pl.pallas_call(kernel, out_shape=[vmem((size, rows, LANES)) for size in s...  5.85 us
  transfers between devices with their start and end apart: 21, of which 4 were waited for; matrix products, arithmetic and copies ran while one was open for 0% of the time, Pallas kernels for 28%

profile of v5, /device:TPU:2, one launch (start us, length us, event | category | flops | bytes accessed | tf_op | source)
XLA Modules:
  0.0 162.0 jit_solution(8724651623389238487)
XLA Ops:
  0.0 3.2 %load.3 = (f32[80,32,128]{2,1,0:T(8,128)}, f32[80,32,128]{2,1,0:T(8,128)}) custom-call(f32[288,32,128]{2,1,0:T(8,128)} %bitcast.23), custom_call_target="tpu_custom_call" | custom-call | bytes 5242880 | tf_op jit(solution)/shard_map/load/pallas_call | solution.py:167
  3.2 1.8 %collective-permute-start.16 = (f32[80,32,128]{2,1,0:T(8,128)}, f32[80,32,128]{2,1,0:T(8,128)}, u32[]{:S(2)}, u32[]{:S(2)}) collective-permute-start(f32[80,32,128]{2,1,0:T(8,128)} %get-tuple-element.31), channel_id=1, source_target_pairs={{3,6},{4,1},{11,14},{12,9},{19,22},{20,17},{27,30},{28,25}} | collective-permute-start | bytes 3932168 | tf_op jit(solution)/shard_map/ppermute | solution.py:438
  5.1 2.6 %load.2 = (f32[49,32,128]{2,1,0:T(8,128)S(1)}, f32[80,32,128]{2,1,0:T(8,128)}, f32[1,32,128]{2,1,0:T(8,128)S(1)}) custom-call(f32[288,32,128]{2,1,0:T(8,128)} %bitcast.24, s32[1,32,128]{2,1,0:T(8,128)S(1)} %bitcast.19), custom_call_target="tpu_custom_call" | custom-call | bytes 4194304 | tf_op jit(solution)/shard_map/load/pallas_call | solution.py:167
  7.7 0.9 copy-done.15
  10.2 2.8 %pack_message.5 = f32[80,32,128]{2,1,0:T(8,128)S(1)} custom-call(f32[288]{0:T(512)S(1)} %copy-done.10, s32[2]{0:T(128)S(1)} %pad_add_fusion.place_ref, f32[288,32,128]{2,1,0:T(8,128)} %bitcast.25, f32[80,32,128]{2,1,0:T(8,128)} %collective-permute-done.16.other_ref), custom_call_target="tpu_custom_call" | custom-call | bytes 3932160 | tf_op jit(solution)/shard_map/pack_message/pallas_call | solution.py:201
  13.0 13.6 %collective-permute-start.17 = (f32[80,32,128]{2,1,0:T(8,128)S(1)}, f32[80,32,128]{2,1,0:T(8,128)S(1)}, u32[]{:S(2)}, u32[]{:S(2)}) collective-permute-start(f32[80,32,128]{2,1,0:T(8,128)S(1)} %pack_message.5), channel_id=1, source_target_pairs={{1,2},{5,6},{2,1},{6,5},{9,10},{13,14},{10,9},{14,13},{17,18},{21,... | collective-permute-start | bytes 3932168 | tf_op jit(solution)/shard_map/ppermute | solution.py:444
  26.6 2.0 %pack_message.4 = f32[80,32,128]{2,1,0:T(8,128)S(1)} custom-call(f32[288]{0:T(512)S(1)} %copy-done.10, s32[2]{0:T(128)S(1)} %pad_add_fusion.place_ref, f32[288,32,128]{2,1,0:T(8,128)} %bitcast.26, f32[80,32,128]{2,1,0:T(8,128)S(1)} %collective-permute-done.11.other_ref), custom_call_target="tpu_custom_call" | custom-call | bytes 3932160 | tf_op jit(solution)/shard_map/pack_message/pallas_call | solution.py:201
  28.7 11.3 %collective-permute-start.12 = (f32[80,32,128]{2,1,0:T(8,128)S(1)}, f32[80,32,128]{2,1,0:T(8,128)S(1)}, u32[]{:S(2)}, u32[]{:S(2)}) collective-permute-start(f32[80,32,128]{2,1,0:T(8,128)S(1)} %pack_message.4), channel_id=1, source_target_pairs={{1,2},{5,6},{2,1},{6,5},{9,10},{13,14},{10,9},{14,13},{17,18},{21,... | collective-permute-start | bytes 3932168 | tf_op jit(solution)/shard_map/ppermute | solution.py:444
  39.9 2.0 %pack_message.3 = f32[80,32,128]{2,1,0:T(8,128)S(1)} custom-call(f32[288]{0:T(512)S(1)} %copy-done.10, s32[2]{0:T(128)S(1)} %pad_add_fusion.place_ref, f32[288,32,128]{2,1,0:T(8,128)} %bitcast.27, f32[80,32,128]{2,1,0:T(8,128)S(1)} %collective-permute-done.4.other_ref), custom_call_target="tpu_custom_call" | custom-call | bytes 3932160 | tf_op jit(solution)/shard_map/pack_message/pallas_call | solution.py:201
  41.9 11.8 %collective-permute-start.5 = (f32[80,32,128]{2,1,0:T(8,128)S(1)}, f32[80,32,128]{2,1,0:T(8,128)S(1)}, u32[]{:S(2)}, u32[]{:S(2)}) collective-permute-start(f32[80,32,128]{2,1,0:T(8,128)S(1)} %pack_message.3), channel_id=1, source_target_pairs={{1,2},{5,6},{2,1},{6,5},{9,10},{13,14},{10,9},{14,13},{17,18},{21,... | collective-permute-start | bytes 3932168 | tf_op jit(solution)/shard_map/ppermute | solution.py:444
  53.8 1.9 %collective-permute-start.2 = (f32[49,32,128]{2,1,0:T(8,128)S(1)}, f32[49,32,128]{2,1,0:T(8,128)S(1)}, u32[]{:S(2)}, u32[]{:S(2)}) collective-permute-start(f32[49,32,128]{2,1,0:T(8,128)S(1)} %copy-done.16), channel_id=1, source_target_pairs={{1,2},{5,6},{2,1},{6,5},{9,10},{13,14},{10,9},{14,13},{17,18},{21,... | collective-permute-start | bytes 2408456 | tf_op jit(solution)/shard_map/ppermute | solution.py:435
  55.7 1.4 collective-permute-start.18
  57.1 29.9 %collective-permute-done.2.side_ref = f32[49,32,128]{2,1,0:T(8,128)S(1)} collective-permute-done((f32[49,32,128]{2,1,0:T(8,128)S(1)}, f32[49,32,128]{2,1,0:T(8,128)S(1)}, u32[]{:S(2)}, u32[]{:S(2)}) %collective-permute-start.2) | collective-permute-done | bytes 802848 | tf_op jit(solution)/shard_map/ppermute | solution.py:435
  87.7 1.4 collective-permute-start.13
  89.1 1.4 collective-permute-start.6
  90.6 3.0 %collective-permute-done = f32[1,32,128]{2,1,0:T(8,128)S(1)} collective-permute-done((f32[1,32,128]{2,1,0:T(8,128)S(1)}, f32[1,32,128]{2,1,0:T(8,128)S(1)}, u32[]{:S(2)}, u32[]{:S(2)}) %collective-permute-start) | collective-permute-done | bytes 16416 | tf_op jit(solution)/shard_map/ppermute | solution.py:439
  93.6 4.4 %propagate.6 = (f32[24,32,128]{2,1,0:T(8,128)S(1)}, f32[24,32,128]{2,1,0:T(8,128)S(1)}) custom-call(f32[288]{0:T(512)S(1)} %copy-done.10, f32[288]{0:T(512)S(1)} %copy-done.11, s32[2]{0:T(128)S(1)} %pad_add_fusion.place_ref, f32[3,32,128]{2,1,0:T(8,128)S(1)} %pad_maximum_fusion.mask_ref, f32[288,32,128]{2,1,0:T(8,128)} %bitcast.28, ...), custom_call_target="tpu_custom_call" | custom-call | flops 7864320 | bytes 3932160 | tf_op jit(solution)/shard_map/propagate/pallas_call | solution.py:320
  98.0 1.3 collective-permute-start.10
  99.3 6.6 %propagate.8 = (f32[40,32,128]{2,1,0:T(8,128)S(1)}, f32[40,32,128]{2,1,0:T(8,128)}) custom-call(f32[288]{0:T(512)S(1)} %copy-done.10, f32[288]{0:T(512)S(1)} %copy-done.11, s32[2]{0:T(128)S(1)} %pad_add_fusion.place_ref, f32[3,32,128]{2,1,0:T(8,128)S(1)} %pad_maximum_fusion.mask_ref, f32[288,32,128]{2,1,0:T(8,128)} %bitcast.29, ...), custom_call_target="tpu_custom_call" | custom-call | flops 13107200 | bytes 6553600 | tf_op jit(solution)/shard_map/propagate/pallas_call | solution.py:320
  105.9 1.3 collective-permute-start.20
  107.2 6.0 %collective-permute-start.9 = (f32[24,32,128]{2,1,0:T(8,128)S(1)}, f32[24,32,128]{2,1,0:T(8,128)S(1)}, u32[]{:S(2)}, u32[]{:S(2)}) collective-permute-start(f32[24,32,128]{2,1,0:T(8,128)S(1)} %get-tuple-element.27.refs_1_), channel_id=1, source_target_pairs={{0,8},{8,16},{16,24},{1,9},{9,17},{17,25},{2,10},{10,18},{18,26},{... | collective-permute-start | bytes 1179656 | tf_op jit(solution)/shard_map/ppermute | solution.py:458
  113.2 4.8 %collective-permute-start.19 = (f32[40,32,128]{2,1,0:T(8,128)}, f32[40,32,128]{2,1,0:T(8,128)}, u32[]{:S(2)}, u32[]{:S(2)}) collective-permute-start(f32[40,32,128]{2,1,0:T(8,128)} %get-tuple-element.33.refs_9_), channel_id=1, source_target_pairs={{0,8},{8,16},{16,24},{1,9},{9,17},{17,25},{2,10},{10,18},{18,26},{... | collective-permute-start | bytes 1966088 | tf_op jit(solution)/shard_map/ppermute | solution.py:458
  118.1 6.4 %propagate.7 = (f32[40,32,128]{2,1,0:T(8,128)}, f32[40,32,128]{2,1,0:T(8,128)}) custom-call(f32[288]{0:T(512)S(1)} %copy-done.10, f32[288]{0:T(512)S(1)} %copy-done.11, s32[2]{0:T(128)S(1)} %pad_add_fusion.place_ref, f32[3,32,128]{2,1,0:T(8,128)S(1)} %pad_maximum_fusion.mask_ref, f32[288,32,128]{2,1,0:T(8,128)} %bitcast.30, ...), custom_call_target="tpu_custom_call" | custom-call | flops 13107200 | bytes 6553600 | tf_op jit(solution)/shard_map/propagate/pallas_call | solution.py:320
  124.5 1.3 collective-permute-start.15
  125.8 5.5 %collective-permute-start.14 = (f32[40,32,128]{2,1,0:T(8,128)}, f32[40,32,128]{2,1,0:T(8,128)}, u32[]{:S(2)}, u32[]{:S(2)}) collective-permute-start(f32[40,32,128]{2,1,0:T(8,128)} %get-tuple-element.30.refs_5_), channel_id=1, source_target_pairs={{0,8},{8,16},{16,24},{1,9},{9,17},{17,25},{2,10},{10,18},{18,26},{... | collective-permute-start | bytes 1966088 | tf_op jit(solution)/shard_map/ppermute | solution.py:458
  131.3 4.7 %propagate.5 = (f32[24,32,128]{2,1,0:T(8,128)}, f32[24,32,128]{2,1,0:T(8,128)}) custom-call(f32[288]{0:T(512)S(1)} %copy-done.10, f32[288]{0:T(512)S(1)} %copy-done.11, s32[2]{0:T(128)S(1)} %pad_add_fusion.place_ref, f32[3,32,128]{2,1,0:T(8,128)S(1)} %pad_maximum_fusion.mask_ref, f32[288,32,128]{2,1,0:T(8,128)} %bitcast.31, ...), custom_call_target="tpu_custom_call" | custom-call | flops 7864320 | bytes 3932160 | tf_op jit(solution)/shard_map/propagate/pallas_call | solution.py:320
  136.8 2.9 %collective-permute-start.7 = (f32[24,32,128]{2,1,0:T(8,128)}, f32[24,32,128]{2,1,0:T(8,128)}, u32[]{:S(2)}, u32[]{:S(2)}) collective-permute-start(f32[24,32,128]{2,1,0:T(8,128)} %get-tuple-element.24.refs_13_), channel_id=1, source_target_pairs={{0,8},{8,16},{16,24},{1,9},{9,17},{17,25},{2,10},{10,18},{18,26},{... | collective-permute-start | bytes 1179656 | tf_op jit(solution)/shard_map/ppermute | solution.py:458
  140.5 1.3 collective-permute-start.8
  141.9 3.3 %propagate.9.refs_14_ = f32[32,32,128]{2,1,0:T(8,128)S(1)} custom-call(f32[288]{0:T(512)S(1)} %copy-done.10, f32[288]{0:T(512)S(1)} %copy-done.11, s32[2]{0:T(128)S(1)} %pad_add_fusion.place_ref, f32[3,32,128]{2,1,0:T(8,128)S(1)} %pad_maximum_fusion.mask_ref, f32[288,32,128]{2,1,0:T(8,128)} %bitcast.32, f32[288,32,128]{2,1,0:T(8,128)} %collective-permute-done.3.mate_hbm, ...), custom_call_target="tpu_custom_call" | custom-call | flops 5242880 | bytes 2621440 | tf_op jit(solution)/shard_map/propagate/pallas_call | solution.py:320
  145.2 5.7 %collective-permute-done.14.refs_6_ = f32[40,32,128]{2,1,0:T(8,128)} collective-permute-done((f32[40,32,128]{2,1,0:T(8,128)}, f32[40,32,128]{2,1,0:T(8,128)}, u32[]{:S(2)}, u32[]{:S(2)}) %collective-permute-start.14) | collective-permute-done | bytes 655392 | tf_op jit(solution)/shard_map/ppermute | solution.py:458
  150.9 7.1 %quadruplets.2 = (f32[544,32,128]{2,1,0:T(8,128)S(1)}, f32[288,32,128]{2,1,0:T(8,128)}) custom-call(f32[1152]{0:T(1024)S(1)} %copy-done.12, s32[2,4]{1,0:T(2,128)S(1)} %bitcast.20, s32[1]{0:T(128)} %bitcast.1.first_ref, f32[24,32,128]{2,1,0:T(8,128)S(1)} %copy-done.3, f32[24,32,128]{2,1,0:T(8,128)S(1)} %copy-done.5, f32[24,32,128]{2,1,0:T(8,128)S(1)} %copy-done.9, ...), custom_call_target="tpu_custom_call" | custom-call | flops 13762560 | bytes 22020096 | tf_op jit(solution)/shard_map/quadruplets/pallas_call | solution.py:387
  158.8 3.2 %quadruplets.3 = (f32[544,32,128]{2,1,0:T(8,128)S(1)}, f32[288,32,128]{2,1,0:T(8,128)}) custom-call(f32[1152]{0:T(1024)S(1)} %copy-done.12, s32[2,4]{1,0:T(2,128)S(1)} %bitcast.21, s32[1]{0:T(128)} %bitcast.1.first_ref, f32[24,32,128]{2,1,0:T(8,128)} %collective-permute-done.7.refs_0_, ...), custom_call_target="tpu_custom_call", output_to_operand_aliasing={{0}: (5, {}), {1}: (6, {})} | custom-call | flops 3932160 | bytes 6291456 | tf_op jit(solution)/shard_map/quadruplets/pallas_call | solution.py:387
  (59 shorter events, 4.7 us)
Async XLA Ops:
  0.0 93.6 %collective-permute-start.3 = (f32[288,32,128]{2,1,0:T(8,128)}, f32[288,32,128]{2,1,0:T(8,128)}, u32[]{:S(2)}, u32[]{:S(2)}) collective-permute-start(f32[288,32,128]{2,1,0:T(8,128)} %bitcast.22), channel_id=1, source_target_pairs={{0,1},{1,0},{2,3},{3,2},{4,5},{5,4},{6,7},{7,6},{8,9},{9,8},{10,11... | collective-permute-start | bytes 14155784 | tf_op jit(solution)/shard_map/ppermute | solution.py:440
  3.2 6.9 %collective-permute-start.16 = (f32[80,32,128]{2,1,0:T(8,128)}, f32[80,32,128]{2,1,0:T(8,128)}, u32[]{:S(2)}, u32[]{:S(2)}) collective-permute-start(f32[80,32,128]{2,1,0:T(8,128)} %get-tuple-element.31), channel_id=1, source_target_pairs={{3,6},{4,1},{11,14},{12,9},{19,22},{20,17},{27,30},{28,25}} | collective-permute-start | bytes 3932168 | tf_op jit(solution)/shard_map/ppermute | solution.py:438
  8.6 18.0 %collective-permute-start.11 = (f32[80,32,128]{2,1,0:T(8,128)}, f32[80,32,128]{2,1,0:T(8,128)S(1)}, u32[]{:S(2)}, u32[]{:S(2)}) collective-permute-start(f32[80,32,128]{2,1,0:T(8,128)} %get-tuple-element.28), channel_id=1, source_target_pairs={{3,6},{4,1},{11,14},{12,9},{19,22},{20,17},{27,30},{28,25}} | collective-permute-start | bytes 3932168 | tf_op jit(solution)/shard_map/ppermute | solution.py:436
  9.3 30.6 %collective-permute-start.4 = (f32[80,32,128]{2,1,0:T(8,128)}, f32[80,32,128]{2,1,0:T(8,128)S(1)}, u32[]{:S(2)}, u32[]{:S(2)}) collective-permute-start(f32[80,32,128]{2,1,0:T(8,128)} %get-tuple-element.23), channel_id=1, source_target_pairs={{3,6},{4,1},{11,14},{12,9},{19,22},{20,17},{27,30},{28,25}} | collective-permute-start | bytes 3932168 | tf_op jit(solution)/shard_map/ppermute | solution.py:438
  13.0 42.8 %collective-permute-start.17 = (f32[80,32,128]{2,1,0:T(8,128)S(1)}, f32[80,32,128]{2,1,0:T(8,128)S(1)}, u32[]{:S(2)}, u32[]{:S(2)}) collective-permute-start(f32[80,32,128]{2,1,0:T(8,128)S(1)} %pack_message.5), channel_id=1, source_target_pairs={{1,2},{5,6},{2,1},{6,5},{9,10},{13,14},{10,9},{14,13},{17,18},{21,... | collective-permute-start | bytes 3932168 | tf_op jit(solution)/shard_map/ppermute | solution.py:444
  28.6 25.1 %copy-start.16 = (f32[49,32,128]{2,1,0:T(8,128)S(1)}, f32[49,32,128]{2,1,0:T(8,128)}, u32[]{:S(2)}) copy-start(f32[49,32,128]{2,1,0:T(8,128)} %copy-done.15) | copy-start | bytes 2408452
  28.7 64.9 %copy-start.11 = (f32[288]{0:T(512)S(1)}, f32[288]{0:T(512)}, u32[]{:S(2)}) copy-start(f32[288]{0:T(512)} %b_ref.9) | copy-start | bytes 3460
  28.7 59.0 %collective-permute-start.12 = (f32[80,32,128]{2,1,0:T(8,128)S(1)}, f32[80,32,128]{2,1,0:T(8,128)S(1)}, u32[]{:S(2)}, u32[]{:S(2)}) collective-permute-start(f32[80,32,128]{2,1,0:T(8,128)S(1)} %pack_message.4), channel_id=1, source_target_pairs={{1,2},{5,6},{2,1},{6,5},{9,10},{13,14},{10,9},{14,13},{17,18},{21,... | collective-permute-start | bytes 3932168 | tf_op jit(solution)/shard_map/ppermute | solution.py:444
  41.9 47.2 %collective-permute-start.5 = (f32[80,32,128]{2,1,0:T(8,128)S(1)}, f32[80,32,128]{2,1,0:T(8,128)S(1)}, u32[]{:S(2)}, u32[]{:S(2)}) collective-permute-start(f32[80,32,128]{2,1,0:T(8,128)S(1)} %pack_message.3), channel_id=1, source_target_pairs={{1,2},{5,6},{2,1},{6,5},{9,10},{13,14},{10,9},{14,13},{17,18},{21,... | collective-permute-start | bytes 3932168 | tf_op jit(solution)/shard_map/ppermute | solution.py:444
  53.8 33.2 %collective-permute-start.2 = (f32[49,32,128]{2,1,0:T(8,128)S(1)}, f32[49,32,128]{2,1,0:T(8,128)S(1)}, u32[]{:S(2)}, u32[]{:S(2)}) collective-permute-start(f32[49,32,128]{2,1,0:T(8,128)S(1)} %copy-done.16), channel_id=1, source_target_pairs={{1,2},{5,6},{2,1},{6,5},{9,10},{13,14},{10,9},{14,13},{17,18},{21,... | collective-permute-start | bytes 2408456 | tf_op jit(solution)/shard_map/ppermute | solution.py:435
  55.7 43.5 %collective-permute-start.18 = (f32[80,32,128]{2,1,0:T(8,128)S(1)}, f32[80,32,128]{2,1,0:T(8,128)S(1)}, u32[]{:S(2)}, u32[]{:S(2)}) collective-permute-start(f32[80,32,128]{2,1,0:T(8,128)S(1)} %collective-permute-done.17.side_ref), channel_id=1, source_target_pairs={{5,4},{2,3},{13,12},{10,11},{21,20},{18,19},{29,28},{26,27}} | collective-permute-start | bytes 3932168 | tf_op jit(solution)/shard_map/ppermute | solution.py:445
  87.0 3.5 %collective-permute-start.1 = (f32[49,32,128]{2,1,0:T(8,128)S(1)}, f32[49,32,128]{2,1,0:T(8,128)S(1)}, u32[]{:S(2)}, u32[]{:S(2)}) collective-permute-start(f32[49,32,128]{2,1,0:T(8,128)S(1)} %copy-done.16), channel_id=1, source_target_pairs={{3,4},{4,3},{11,12},{12,11},{19,20},{20,19},{27,28},{28,27}} | collective-permute-start | bytes 2408456 | tf_op jit(solution)/shard_map/ppermute | solution.py:434
  87.7 25.5 %collective-permute-start.13 = (f32[80,32,128]{2,1,0:T(8,128)S(1)}, f32[80,32,128]{2,1,0:T(8,128)S(1)}, u32[]{:S(2)}, u32[]{:S(2)}) collective-permute-start(f32[80,32,128]{2,1,0:T(8,128)S(1)} %collective-permute-done.12.side_ref), channel_id=1, source_target_pairs={{5,4},{2,3},{13,12},{10,11},{21,20},{18,19},{29,28},{26,27}} | collective-permute-start | bytes 3932168 | tf_op jit(solution)/shard_map/ppermute | solution.py:445
  89.1 35.4 %collective-permute-start.6 = (f32[80,32,128]{2,1,0:T(8,128)S(1)}, f32[80,32,128]{2,1,0:T(8,128)S(1)}, u32[]{:S(2)}, u32[]{:S(2)}) collective-permute-start(f32[80,32,128]{2,1,0:T(8,128)S(1)} %collective-permute-done.5.side_ref), channel_id=1, source_target_pairs={{5,4},{2,3},{13,12},{10,11},{21,20},{18,19},{29,28},{26,27}} | collective-permute-start | bytes 3932168 | tf_op jit(solution)/shard_map/ppermute | solution.py:445
  90.5 3.1 %collective-permute-start = (f32[1,32,128]{2,1,0:T(8,128)S(1)}, f32[1,32,128]{2,1,0:T(8,128)S(1)}, u32[]{:S(2)}, u32[]{:S(2)}) collective-permute-start(f32[1,32,128]{2,1,0:T(8,128)S(1)} %get-tuple-element.21), channel_id=1, source_target_pairs={{0,1},{1,0},{2,3},{3,2},{4,5},{5,4},{6,7},{7,6},{8,9},{9,8},{10,11... | collective-permute-start | bytes 49160 | tf_op jit(solution)/shard_map/ppermute | solution.py:439
  98.0 9.3 %copy-start.4 = (f32[24,32,128]{2,1,0:T(8,128)}, f32[24,32,128]{2,1,0:T(8,128)S(1)}, u32[]{:S(2)}) copy-start(f32[24,32,128]{2,1,0:T(8,128)S(1)} %get-tuple-element.27.refs_1_) | copy-start | bytes 1179652
  98.0 27.8 %collective-permute-start.10 = (f32[24,32,128]{2,1,0:T(8,128)S(1)}, f32[24,32,128]{2,1,0:T(8,128)S(1)}, u32[]{:S(2)}, u32[]{:S(2)}) collective-permute-start(f32[24,32,128]{2,1,0:T(8,128)S(1)} %get-tuple-element.26.refs_0_), channel_id=1, source_target_pairs={{8,0},{16,8},{24,16},{9,1},{17,9},{25,17},{10,2},{18,10},{26,18},{... | collective-permute-start | bytes 1179656 | tf_op jit(solution)/shard_map/ppermute | solution.py:458
  105.9 33.7 %collective-permute-start.20 = (f32[40,32,128]{2,1,0:T(8,128)S(1)}, f32[40,32,128]{2,1,0:T(8,128)S(1)}, u32[]{:S(2)}, u32[]{:S(2)}) collective-permute-start(f32[40,32,128]{2,1,0:T(8,128)S(1)} %get-tuple-element.32.refs_8_), channel_id=1, source_target_pairs={{8,0},{16,8},{24,16},{9,1},{17,9},{25,17},{10,2},{18,10},{26,18},{... | collective-permute-start | bytes 1966088 | tf_op jit(solution)/shard_map/ppermute | solution.py:458
  107.2 28.8 %collective-permute-start.9 = (f32[24,32,128]{2,1,0:T(8,128)S(1)}, f32[24,32,128]{2,1,0:T(8,128)S(1)}, u32[]{:S(2)}, u32[]{:S(2)}) collective-permute-start(f32[24,32,128]{2,1,0:T(8,128)S(1)} %get-tuple-element.27.refs_1_), channel_id=1, source_target_pairs={{0,8},{8,16},{16,24},{1,9},{9,17},{17,25},{2,10},{10,18},{18,26},{... | collective-permute-start | bytes 1179656 | tf_op jit(solution)/shard_map/ppermute | solution.py:458
  113.2 32.0 %collective-permute-start.19 = (f32[40,32,128]{2,1,0:T(8,128)}, f32[40,32,128]{2,1,0:T(8,128)}, u32[]{:S(2)}, u32[]{:S(2)}) collective-permute-start(f32[40,32,128]{2,1,0:T(8,128)} %get-tuple-element.33.refs_9_), channel_id=1, source_target_pairs={{0,8},{8,16},{16,24},{1,9},{9,17},{17,25},{2,10},{10,18},{18,26},{... | collective-permute-start | bytes 1966088 | tf_op jit(solution)/shard_map/ppermute | solution.py:458
  124.5 20.7 %collective-permute-start.15 = (f32[40,32,128]{2,1,0:T(8,128)}, f32[40,32,128]{2,1,0:T(8,128)}, u32[]{:S(2)}, u32[]{:S(2)}) collective-permute-start(f32[40,32,128]{2,1,0:T(8,128)} %get-tuple-element.29.refs_4_), channel_id=1, source_target_pairs={{8,0},{16,8},{24,16},{9,1},{17,9},{25,17},{10,2},{18,10},{26,18},{... | collective-permute-start | bytes 1966088 | tf_op jit(solution)/shard_map/ppermute | solution.py:458
  125.8 10.2 %copy-start.6 = (f32[24,32,128]{2,1,0:T(8,128)}, f32[24,32,128]{2,1,0:T(8,128)S(1)}, u32[]{:S(2)}) copy-start(f32[24,32,128]{2,1,0:T(8,128)S(1)} %collective-permute-done.10.refs_3_) | copy-start | bytes 1179652
  125.8 25.1 %collective-permute-start.14 = (f32[40,32,128]{2,1,0:T(8,128)}, f32[40,32,128]{2,1,0:T(8,128)}, u32[]{:S(2)}, u32[]{:S(2)}) collective-permute-start(f32[40,32,128]{2,1,0:T(8,128)} %get-tuple-element.30.refs_5_), channel_id=1, source_target_pairs={{0,8},{8,16},{16,24},{1,9},{9,17},{17,25},{2,10},{10,18},{18,26},{... | collective-permute-start | bytes 1966088 | tf_op jit(solution)/shard_map/ppermute | solution.py:458
  136.8 22.0 %collective-permute-start.7 = (f32[24,32,128]{2,1,0:T(8,128)}, f32[24,32,128]{2,1,0:T(8,128)}, u32[]{:S(2)}, u32[]{:S(2)}) collective-permute-start(f32[24,32,128]{2,1,0:T(8,128)} %get-tuple-element.24.refs_13_), channel_id=1, source_target_pairs={{0,8},{8,16},{16,24},{1,9},{9,17},{17,25},{2,10},{10,18},{18,26},{... | collective-permute-start | bytes 1179656 | tf_op jit(solution)/shard_map/ppermute | solution.py:458
  140.5 18.3 %collective-permute-start.8 = (f32[24,32,128]{2,1,0:T(8,128)}, f32[24,32,128]{2,1,0:T(8,128)}, u32[]{:S(2)}, u32[]{:S(2)}) collective-permute-start(f32[24,32,128]{2,1,0:T(8,128)} %get-tuple-element.25.refs_12_), channel_id=1, source_target_pairs={{8,0},{16,8},{24,16},{9,1},{17,9},{25,17},{10,2},{18,10},{26,18},{... | collective-permute-start | bytes 1179656 | tf_op jit(solution)/shard_map/ppermute | solution.py:458
  141.8 9.1 %copy-start.1 = (f32[40,32,128]{2,1,0:T(8,128)S(1)}, f32[40,32,128]{2,1,0:T(8,128)}, u32[]{:S(2)}) copy-start(f32[40,32,128]{2,1,0:T(8,128)} %copy-done) | copy-start | bytes 1966084
  141.8 9.1 %copy-start.3 = (f32[24,32,128]{2,1,0:T(8,128)S(1)}, f32[24,32,128]{2,1,0:T(8,128)}, u32[]{:S(2)}) copy-start(f32[24,32,128]{2,1,0:T(8,128)} %copy-done.2) | copy-start | bytes 1179652
  141.8 9.1 %copy-start.5 = (f32[24,32,128]{2,1,0:T(8,128)S(1)}, f32[24,32,128]{2,1,0:T(8,128)}, u32[]{:S(2)}) copy-start(f32[24,32,128]{2,1,0:T(8,128)} %copy-done.4) | copy-start | bytes 1179652
  141.8 9.1 %copy-start.7 = (f32[24,32,128]{2,1,0:T(8,128)S(1)}, f32[24,32,128]{2,1,0:T(8,128)}, u32[]{:S(2)}) copy-start(f32[24,32,128]{2,1,0:T(8,128)} %copy-done.6) | copy-start | bytes 1179652
  141.8 9.1 %copy-start.9 = (f32[24,32,128]{2,1,0:T(8,128)S(1)}, f32[24,32,128]{2,1,0:T(8,128)}, u32[]{:S(2)}) copy-start(f32[24,32,128]{2,1,0:T(8,128)} %copy-done.8) | copy-start | bytes 1179652
  141.8 9.1 %copy-start.12 = (f32[1152]{0:T(1024)S(1)}, f32[1152]{0:T(1024)}, u32[]{:S(2)}) copy-start(f32[1152]{0:T(1024)} %strength_ref.3) | copy-start | bytes 13828
  141.9 9.1 %copy-start.14 = (s32[4,2]{0,1:T(2,128)S(1)}, s32[4,2]{0,1:T(2,128)}, u32[]{:S(2)}) copy-start(s32[4,2]{0,1:T(2,128)} %param.11) | copy-start | bytes 100
  (6 other events, 20.6 us)

commit v6 on v5

--- a/solution.py
+++ b/solution.py
@@ -174,6 +174,33 @@
         cost_estimate=cost(0, 2 * sum(ends) * rows * LANES * 4),
         name="load",
     )(far_from_core(own), *operands[1:])
+
+
+def pack_first(own, mate, along_lat, place, spans):
+    rows = own.shape[1]
+    size = total(spans)
+
+    def kernel(a_ref, place_ref, own_ref, mate_ref, out_ref):
+        odd = place_ref[0] > 0
+        for at, start, length in laid(spans):
+            def one(i, carry):
+                from_own = (a_ref[start + i] > 0) == odd
+                out_ref[at + i] = jnp.where(from_own, own_ref[at + i], mate_ref[at + i])
+                return carry
+
+            lax.fori_loop(0, length, one, 0, unroll=8)
+        out_ref[size] = own_ref[size]
+        out_ref[size + 1] = mate_ref[size]
+
+    return pl.pallas_call(
+        kernel,
+        out_shape=vmem((size + 2, rows, LANES)),
+        in_specs=[whole(pltpu.SMEM)] * 2 + [whole(pltpu.VMEM)] * 2,
+        out_specs=whole(pltpu.VMEM),
+        compiler_params=limits(8),
+        cost_estimate=cost(0, 3 * size * rows * LANES * 4),
+        name="pack_first",
+    )(along_lat, place, near_core(own), near_core(mate))
 
 
 def pack_message(own, other, along_lat, place, spans):
@@ -414,7 +441,7 @@
     mates = [(i, i ^ 1) for i in range(lat_count)]
     corners = range(3, lat_count - 1, 4)
     sides = [(i, i + 1) for i in range(1, lat_count, 4)] + [(i + 1, i) for i in range(1, lat_count, 4)]
-    diagonals = [(i, i + 1) for i in corners] + [(i + 1, i) for i in corners]
+    relays = [(i - 2, i + 1) for i in corners] + [(i + 3, i) for i in corners]
     aheads = [(i, i + 3) for i in corners] + [(i + 1, i - 2) for i in corners]
     hands = [(i + 2, i + 1) for i in corners] + [(i - 1, i) for i in corners]
     handed = (at % 4 == 0) | (at % 4 == 3)
@@ -431,12 +458,12 @@
     middle = [(edge, comp_dev - 2 * edge)]
     lots = chunks[:-1] + [chunks[-1] + middle]
     head, part, maskf = load(own, lots[:2], mask)
-    hands_in = [lax.ppermute(head, "lat", diagonals)]
-    sides_in = [lax.ppermute(head, "lat", sides)]
+    mate_head = lax.ppermute(head, "lat", mates)
     ahead = [None, lax.ppermute(part, "lat", aheads)]
+    sides_in = [lax.ppermute(pack_first(head, mate_head, courant_lat, place, chunks[0]), "lat", sides)]
+    hands_in = [lax.ppermute(sides_in[0], "lat", relays)]
     rest = load(own, lots[2:])
     ahead += [lax.ppermute(part, "lat", aheads) for part in rest]
-    mate_mask = lax.ppermute(maskf, "lat", mates)
     mate = lax.ppermute(own, "lat", mates)
     for n, spans in enumerate(lots):
         if n:
@@ -444,7 +471,8 @@
             sides_in.append(lax.ppermute(message, "lat", sides))
             hands_in.append(lax.ppermute(sides_in[n], "lat", hands))
     size = total(chunks[0])
-    masks = jnp.concatenate([maskf, mate_mask, jnp.where(handed, hands_in[0][size:], sides_in[0][size:])])
+    far_mask = jnp.where(handed, hands_in[0][size + 1:], sides_in[0][size:size + 1])
+    masks = jnp.concatenate([maskf, mate_head[size:], far_mask])
     parts = []
     places = []
     last = []

time: 164 us -> 157 us (0.957)
  the two profiles are of different devices: /device:TPU:2 before, /device:TPU:27 now
where the time goes in v6:
time: 157 us; the launch traced here: 156 us
  waiting for transfers between devices  67.4 us (43%)
  Pallas kernels  50.1 us (32%)
  starting transfers between devices  36.3 us (23%)
  local copies, waits for them, and re-layouts  1.62 us (1%)
    ppermute x1, waiting for transfers between devices, halo_plan(): hands_in = [lax.ppermute(sides_in[0], 'lat', relays)]  34.2 us
    pallas_call x5, Pallas kernels, propagate(): pl.pallas_call(kernel, out_shape=[jax.ShapeDtypeStruct((length, rows, LAN...  25.5 us
    ppermute x8, starting transfers between devices, halo_plan(): last = [lax.ppermute(high, 'comp', z_up), lax.ppermute(low, 'comp', z_down)]  20.5 us
    ppermute x2, waiting for transfers between devices, halo_plan(): ahead += [lax.ppermute(part, 'lat', aheads) for part in rest]  19.1 us
    ppermute x1, waiting for transfers between devices, halo_plan(): ahead = [None, lax.ppermute(part, 'lat', aheads)]  10.5 us
    pallas_call x2, Pallas kernels, quadruplets(): pl.pallas_call(kernel, out_shape=[vmem(((local + 2 * reach) * ND, rows, L...  10.3 us
    pallas_call x3, Pallas kernels, pack_message(): pl.pallas_call(kernel, out_shape=vmem(shape), in_specs=[whole(pltpu.SMEM)...  6.8 us
    pallas_call x2, Pallas kernels, load(): pl.pallas_call(kernel, out_shape=[vmem((size, rows, LANES)) for size in s...  6.09 us
  transfers between devices with their start and end apart: 21, of which 5 were waited for; matrix products, arithmetic and copies ran while one was open for 0% of the time, Pallas kernels for 30%

profile of v6, /device:TPU:27, one launch (start us, length us, event | category | flops | bytes accessed | tf_op | source)
XLA Modules:
  0.0 156.0 jit_solution(16988805798576185709)
XLA Ops:
  0.7 3.2 %load.3 = (f32[80,32,128]{2,1,0:T(8,128)}, f32[80,32,128]{2,1,0:T(8,128)}) custom-call(f32[288,32,128]{2,1,0:T(8,128)} %bitcast.23), custom_call_target="tpu_custom_call" | custom-call | bytes 5242880 | tf_op jit(solution)/shard_map/load/pallas_call | solution.py:167
  3.9 4.2 %collective-permute-start.16 = (f32[80,32,128]{2,1,0:T(8,128)}, f32[80,32,128]{2,1,0:T(8,128)}, u32[]{:S(2)}, u32[]{:S(2)}) collective-permute-start(f32[80,32,128]{2,1,0:T(8,128)} %get-tuple-element.31), channel_id=1, source_target_pairs={{3,6},{4,1},{11,14},{12,9},{19,22},{20,17},{27,30},{28,25}} | collective-permute-start | bytes 3932168 | tf_op jit(solution)/shard_map/ppermute | solution.py:466
  8.1 2.9 %load.2 = (f32[49,32,128]{2,1,0:T(8,128)}, f32[80,32,128]{2,1,0:T(8,128)}, f32[1,32,128]{2,1,0:T(8,128)S(1)}) custom-call(f32[288,32,128]{2,1,0:T(8,128)} %bitcast.24, s32[1,32,128]{2,1,0:T(8,128)S(1)} %bitcast.19), custom_call_target="tpu_custom_call" | custom-call | bytes 4194304 | tf_op jit(solution)/shard_map/load/pallas_call | solution.py:167
  11.0 1.4 collective-permute-start.11
  12.4 1.4 collective-permute-start.4
  13.9 7.9 %collective-permute-done.16.other_ref = f32[80,32,128]{2,1,0:T(8,128)} collective-permute-done((f32[80,32,128]{2,1,0:T(8,128)}, f32[80,32,128]{2,1,0:T(8,128)}, u32[]{:S(2)}, u32[]{:S(2)}) %collective-permute-start.16) | collective-permute-done | bytes 1310752 | tf_op jit(solution)/shard_map/ppermute | solution.py:466
  21.8 2.8 %pack_message.5 = f32[80,32,128]{2,1,0:T(8,128)S(1)} custom-call(f32[288]{0:T(512)S(1)} %copy-done.10, s32[2]{0:T(128)S(1)} %pad_add_fusion.place_ref, f32[288,32,128]{2,1,0:T(8,128)} %bitcast.25, f32[80,32,128]{2,1,0:T(8,128)} %collective-permute-done.16.other_ref), custom_call_target="tpu_custom_call" | custom-call | bytes 3932160 | tf_op jit(solution)/shard_map/pack_message/pallas_call | solution.py:228
  25.3 10.5 %collective-permute-done.11.other_ref = f32[80,32,128]{2,1,0:T(8,128)S(1)} collective-permute-done((f32[80,32,128]{2,1,0:T(8,128)}, f32[80,32,128]{2,1,0:T(8,128)S(1)}, u32[]{:S(2)}, u32[]{:S(2)}) %collective-permute-start.11) | collective-permute-done | bytes 1310752 | tf_op jit(solution)/shard_map/ppermute | solution.py:462
  35.8 2.0 %pack_message.4 = f32[80,32,128]{2,1,0:T(8,128)S(1)} custom-call(f32[288]{0:T(512)S(1)} %copy-done.10, s32[2]{0:T(128)S(1)} %pad_add_fusion.place_ref, f32[288,32,128]{2,1,0:T(8,128)} %bitcast.26, f32[80,32,128]{2,1,0:T(8,128)S(1)} %collective-permute-done.11.other_ref), custom_call_target="tpu_custom_call" | custom-call | bytes 3932160 | tf_op jit(solution)/shard_map/pack_message/pallas_call | solution.py:228
  38.6 11.3 %collective-permute-done.4.other_ref = f32[80,32,128]{2,1,0:T(8,128)S(1)} collective-permute-done((f32[80,32,128]{2,1,0:T(8,128)}, f32[80,32,128]{2,1,0:T(8,128)S(1)}, u32[]{:S(2)}, u32[]{:S(2)}) %collective-permute-start.4) | collective-permute-done | bytes 1310752 | tf_op jit(solution)/shard_map/ppermute | solution.py:466
  49.9 2.0 %pack_message.3 = f32[80,32,128]{2,1,0:T(8,128)S(1)} custom-call(f32[288]{0:T(512)S(1)} %copy-done.10, s32[2]{0:T(128)S(1)} %pad_add_fusion.place_ref, f32[288,32,128]{2,1,0:T(8,128)} %bitcast.27, f32[80,32,128]{2,1,0:T(8,128)S(1)} %collective-permute-done.4.other_ref), custom_call_target="tpu_custom_call" | custom-call | bytes 3932160 | tf_op jit(solution)/shard_map/pack_message/pallas_call | solution.py:228
  52.7 1.4 pack_first.1
  54.7 1.3 collective-permute-start.18
  56.1 1.3 collective-permute-start.2
  57.4 1.3 collective-permute-start.13
  58.7 1.3 collective-permute-start.6
  60.0 34.2 %collective-permute-done.2.hand_ref = f32[50,32,128]{2,1,0:T(8,128)S(1)} collective-permute-done((f32[50,32,128]{2,1,0:T(8,128)S(1)}, f32[50,32,128]{2,1,0:T(8,128)S(1)}, u32[]{:S(2)}, u32[]{:S(2)}) %collective-permute-start.2) | collective-permute-done | bytes 819232 | tf_op jit(solution)/shard_map/ppermute | solution.py:464
  94.2 4.4 %propagate.6 = (f32[24,32,128]{2,1,0:T(8,128)S(1)}, f32[24,32,128]{2,1,0:T(8,128)S(1)}) custom-call(f32[288]{0:T(512)S(1)} %copy-done.10, f32[288]{0:T(512)S(1)} %copy-done.11, s32[2]{0:T(128)S(1)} %pad_add_fusion.place_ref, f32[3,32,128]{2,1,0:T(8,128)S(1)} %pad_maximum_fusion.mask_ref, f32[288,32,128]{2,1,0:T(8,128)} %bitcast.28, ...), custom_call_target="tpu_custom_call" | custom-call | flops 7864320 | bytes 3932160 | tf_op jit(solution)/shard_map/propagate/pallas_call | solution.py:347
  98.6 2.4 %collective-permute-start.10 = (f32[24,32,128]{2,1,0:T(8,128)S(1)}, f32[24,32,128]{2,1,0:T(8,128)S(1)}, u32[]{:S(2)}, u32[]{:S(2)}) collective-permute-start(f32[24,32,128]{2,1,0:T(8,128)S(1)} %get-tuple-element.26.refs_0_), channel_id=1, source_target_pairs={{8,0},{16,8},{24,16},{9,1},{17,9},{25,17},{10,2},{18,10},{26,18},{... | collective-permute-start | bytes 1179656 | tf_op jit(solution)/shard_map/ppermute | solution.py:486
  101.0 6.7 %propagate.8 = (f32[40,32,128]{2,1,0:T(8,128)S(1)}, f32[40,32,128]{2,1,0:T(8,128)}) custom-call(f32[288]{0:T(512)S(1)} %copy-done.10, f32[288]{0:T(512)S(1)} %copy-done.11, s32[2]{0:T(128)S(1)} %pad_add_fusion.place_ref, f32[3,32,128]{2,1,0:T(8,128)S(1)} %pad_maximum_fusion.mask_ref, f32[288,32,128]{2,1,0:T(8,128)} %bitcast.29, ...), custom_call_target="tpu_custom_call" | custom-call | flops 13107200 | bytes 6553600 | tf_op jit(solution)/shard_map/propagate/pallas_call | solution.py:347
  107.7 2.1 %collective-permute-start.20 = (f32[40,32,128]{2,1,0:T(8,128)S(1)}, f32[40,32,128]{2,1,0:T(8,128)S(1)}, u32[]{:S(2)}, u32[]{:S(2)}) collective-permute-start(f32[40,32,128]{2,1,0:T(8,128)S(1)} %get-tuple-element.32.refs_8_), channel_id=1, source_target_pairs={{8,0},{16,8},{24,16},{9,1},{17,9},{25,17},{10,2},{18,10},{26,18},{... | collective-permute-start | bytes 1966088 | tf_op jit(solution)/shard_map/ppermute | solution.py:486
  109.8 1.3 collective-permute-start.9
  111.1 1.3 collective-permute-start.19
  112.4 6.4 %propagate.7 = (f32[40,32,128]{2,1,0:T(8,128)}, f32[40,32,128]{2,1,0:T(8,128)}) custom-call(f32[288]{0:T(512)S(1)} %copy-done.10, f32[288]{0:T(512)S(1)} %copy-done.11, s32[2]{0:T(128)S(1)} %pad_add_fusion.place_ref, f32[3,32,128]{2,1,0:T(8,128)S(1)} %pad_maximum_fusion.mask_ref, f32[288,32,128]{2,1,0:T(8,128)} %bitcast.30, ...), custom_call_target="tpu_custom_call" | custom-call | flops 13107200 | bytes 6553600 | tf_op jit(solution)/shard_map/propagate/pallas_call | solution.py:347
  118.8 5.5 %collective-permute-start.15 = (f32[40,32,128]{2,1,0:T(8,128)}, f32[40,32,128]{2,1,0:T(8,128)}, u32[]{:S(2)}, u32[]{:S(2)}) collective-permute-start(f32[40,32,128]{2,1,0:T(8,128)} %get-tuple-element.29.refs_4_), channel_id=1, source_target_pairs={{8,0},{16,8},{24,16},{9,1},{17,9},{25,17},{10,2},{18,10},{26,18},{... | collective-permute-start | bytes 1966088 | tf_op jit(solution)/shard_map/ppermute | solution.py:486
  124.3 1.3 collective-permute-start.14
  125.6 4.7 %propagate.5 = (f32[24,32,128]{2,1,0:T(8,128)}, f32[24,32,128]{2,1,0:T(8,128)}) custom-call(f32[288]{0:T(512)S(1)} %copy-done.10, f32[288]{0:T(512)S(1)} %copy-done.11, s32[2]{0:T(128)S(1)} %pad_add_fusion.place_ref, f32[3,32,128]{2,1,0:T(8,128)S(1)} %pad_maximum_fusion.mask_ref, f32[288,32,128]{2,1,0:T(8,128)} %bitcast.31, ...), custom_call_target="tpu_custom_call" | custom-call | flops 7864320 | bytes 3932160 | tf_op jit(solution)/shard_map/propagate/pallas_call | solution.py:347
  133.2 5.4 %collective-permute-start.8 = (f32[24,32,128]{2,1,0:T(8,128)}, f32[24,32,128]{2,1,0:T(8,128)}, u32[]{:S(2)}, u32[]{:S(2)}) collective-permute-start(f32[24,32,128]{2,1,0:T(8,128)} %get-tuple-element.25.refs_12_), channel_id=1, source_target_pairs={{8,0},{16,8},{24,16},{9,1},{17,9},{25,17},{10,2},{18,10},{26,18},{... | collective-permute-start | bytes 1179656 | tf_op jit(solution)/shard_map/ppermute | solution.py:486
  138.6 3.4 %propagate.9.refs_14_ = f32[32,32,128]{2,1,0:T(8,128)S(1)} custom-call(f32[288]{0:T(512)S(1)} %copy-done.10, f32[288]{0:T(512)S(1)} %copy-done.11, s32[2]{0:T(128)S(1)} %pad_add_fusion.place_ref, f32[3,32,128]{2,1,0:T(8,128)S(1)} %pad_maximum_fusion.mask_ref, f32[288,32,128]{2,1,0:T(8,128)} %bitcast.32, f32[288,32,128]{2,1,0:T(8,128)} %collective-permute-done.3.mate_hbm, ...), custom_call_target="tpu_custom_call" | custom-call | flops 5242880 | bytes 2621440 | tf_op jit(solution)/shard_map/propagate/pallas_call | solution.py:347
  142.0 3.6 %collective-permute-done.14.refs_6_ = f32[40,32,128]{2,1,0:T(8,128)} collective-permute-done((f32[40,32,128]{2,1,0:T(8,128)}, f32[40,32,128]{2,1,0:T(8,128)}, u32[]{:S(2)}, u32[]{:S(2)}) %collective-permute-start.14) | collective-permute-done | bytes 655392 | tf_op jit(solution)/shard_map/ppermute | solution.py:486
  145.7 7.1 %quadruplets.2 = (f32[544,32,128]{2,1,0:T(8,128)S(1)}, f32[288,32,128]{2,1,0:T(8,128)}) custom-call(f32[1152]{0:T(1024)S(1)} %copy-done.12, s32[2,4]{1,0:T(2,128)S(1)} %bitcast.20, s32[1]{0:T(128)} %bitcast.1.first_ref, f32[24,32,128]{2,1,0:T(8,128)S(1)} %copy-done.3, f32[24,32,128]{2,1,0:T(8,128)S(1)} %copy-done.5, f32[24,32,128]{2,1,0:T(8,128)S(1)} %copy-done.9, ...), custom_call_target="tpu_custom_call" | custom-call | flops 13762560 | bytes 22020096 | tf_op jit(solution)/shard_map/quadruplets/pallas_call | solution.py:414
  152.8 3.2 %quadruplets.3 = (f32[544,32,128]{2,1,0:T(8,128)S(1)}, f32[288,32,128]{2,1,0:T(8,128)}) custom-call(f32[1152]{0:T(1024)S(1)} %copy-done.12, s32[2,4]{1,0:T(2,128)S(1)} %bitcast.21, s32[1]{0:T(128)} %bitcast.1.first_ref, f32[24,32,128]{2,1,0:T(8,128)} %collective-permute-done.7.refs_0_, ...), custom_call_target="tpu_custom_call", output_to_operand_aliasing={{0}: (5, {}), {1}: (6, {})} | custom-call | flops 3932160 | bytes 6291456 | tf_op jit(solution)/shard_map/quadruplets/pallas_call | solution.py:414
  (57 shorter events, 6.7 us)
Async XLA Ops:
  0.0 8.1 %copy-start.13 = (s32[2,2048]{1,0:T(2,128)S(1)}, s32[2,2048]{1,0:T(2,128)}, u32[]{:S(2)}) copy-start(s32[2,2048]{1,0:T(2,128)} %param.9) | copy-start | bytes 49156
  0.0 94.2 %collective-permute-start.3 = (f32[288,32,128]{2,1,0:T(8,128)}, f32[288,32,128]{2,1,0:T(8,128)}, u32[]{:S(2)}, u32[]{:S(2)}) collective-permute-start(f32[288,32,128]{2,1,0:T(8,128)} %bitcast.22), channel_id=1, source_target_pairs={{0,1},{1,0},{2,3},{3,2},{4,5},{5,4},{6,7},{7,6},{8,9},{9,8},{10,11... | collective-permute-start | bytes 14155784 | tf_op jit(solution)/shard_map/ppermute | solution.py:467
  3.9 17.9 %collective-permute-start.16 = (f32[80,32,128]{2,1,0:T(8,128)}, f32[80,32,128]{2,1,0:T(8,128)}, u32[]{:S(2)}, u32[]{:S(2)}) collective-permute-start(f32[80,32,128]{2,1,0:T(8,128)} %get-tuple-element.31), channel_id=1, source_target_pairs={{3,6},{4,1},{11,14},{12,9},{19,22},{20,17},{27,30},{28,25}} | collective-permute-start | bytes 3932168 | tf_op jit(solution)/shard_map/ppermute | solution.py:466
  8.1 13.7 %copy-start.10 = (f32[288]{0:T(512)S(1)}, f32[288]{0:T(512)}, u32[]{:S(2)}) copy-start(f32[288]{0:T(512)} %a_ref.17) | copy-start | bytes 3460
  11.0 24.9 %collective-permute-start.11 = (f32[80,32,128]{2,1,0:T(8,128)}, f32[80,32,128]{2,1,0:T(8,128)S(1)}, u32[]{:S(2)}, u32[]{:S(2)}) collective-permute-start(f32[80,32,128]{2,1,0:T(8,128)} %get-tuple-element.28), channel_id=1, source_target_pairs={{3,6},{4,1},{11,14},{12,9},{19,22},{20,17},{27,30},{28,25}} | collective-permute-start | bytes 3932168 | tf_op jit(solution)/shard_map/ppermute | solution.py:462
  12.4 37.5 %collective-permute-start.4 = (f32[80,32,128]{2,1,0:T(8,128)}, f32[80,32,128]{2,1,0:T(8,128)S(1)}, u32[]{:S(2)}, u32[]{:S(2)}) collective-permute-start(f32[80,32,128]{2,1,0:T(8,128)} %get-tuple-element.23), channel_id=1, source_target_pairs={{3,6},{4,1},{11,14},{12,9},{19,22},{20,17},{27,30},{28,25}} | collective-permute-start | bytes 3932168 | tf_op jit(solution)/shard_map/ppermute | solution.py:466
  13.7 38.9 %collective-permute-start = (f32[49,32,128]{2,1,0:T(8,128)}, f32[49,32,128]{2,1,0:T(8,128)S(1)}, u32[]{:S(2)}, u32[]{:S(2)}) collective-permute-start(f32[49,32,128]{2,1,0:T(8,128)} %get-tuple-element.22.own_ref), channel_id=1, source_target_pairs={{0,1},{1,0},{2,3},{3,2},{4,5},{5,4},{6,7},{7,6},{8,9},{9,8},{10,11... | collective-permute-start | bytes 2408456 | tf_op jit(solution)/shard_map/ppermute | solution.py:461
  24.6 30.2 %collective-permute-start.17 = (f32[80,32,128]{2,1,0:T(8,128)S(1)}, f32[80,32,128]{2,1,0:T(8,128)S(1)}, u32[]{:S(2)}, u32[]{:S(2)}) collective-permute-start(f32[80,32,128]{2,1,0:T(8,128)S(1)} %pack_message.5), channel_id=1, source_target_pairs={{1,2},{5,6},{2,1},{6,5},{9,10},{13,14},{10,9},{14,13},{17,18},{21,... | collective-permute-start | bytes 3932168 | tf_op jit(solution)/shard_map/ppermute | solution.py:471
  37.9 19.5 %collective-permute-start.12 = (f32[80,32,128]{2,1,0:T(8,128)S(1)}, f32[80,32,128]{2,1,0:T(8,128)S(1)}, u32[]{:S(2)}, u32[]{:S(2)}) collective-permute-start(f32[80,32,128]{2,1,0:T(8,128)S(1)} %pack_message.4), channel_id=1, source_target_pairs={{1,2},{5,6},{2,1},{6,5},{9,10},{13,14},{10,9},{14,13},{17,18},{21,... | collective-permute-start | bytes 3932168 | tf_op jit(solution)/shard_map/ppermute | solution.py:471
  51.9 42.3 %copy-start.11 = (f32[288]{0:T(512)S(1)}, f32[288]{0:T(512)}, u32[]{:S(2)}) copy-start(f32[288]{0:T(512)} %b_ref.9) | copy-start | bytes 3460
  51.9 6.8 %collective-permute-start.5 = (f32[80,32,128]{2,1,0:T(8,128)S(1)}, f32[80,32,128]{2,1,0:T(8,128)S(1)}, u32[]{:S(2)}, u32[]{:S(2)}) collective-permute-start(f32[80,32,128]{2,1,0:T(8,128)S(1)} %pack_message.3), channel_id=1, source_target_pairs={{1,2},{5,6},{2,1},{6,5},{9,10},{13,14},{10,9},{14,13},{17,18},{21,... | collective-permute-start | bytes 3932168 | tf_op jit(solution)/shard_map/ppermute | solution.py:471
  54.0 2.0 %collective-permute-start.1 = (f32[50,32,128]{2,1,0:T(8,128)S(1)}, f32[50,32,128]{2,1,0:T(8,128)S(1)}, u32[]{:S(2)}, u32[]{:S(2)}) collective-permute-start(f32[50,32,128]{2,1,0:T(8,128)S(1)} %pack_first.1), channel_id=1, source_target_pairs={{1,2},{5,6},{2,1},{6,5},{9,10},{13,14},{10,9},{14,13},{17,18},{21,... | collective-permute-start | bytes 2457608 | tf_op jit(solution)/shard_map/ppermute | solution.py:463
  54.7 46.2 %collective-permute-start.18 = (f32[80,32,128]{2,1,0:T(8,128)S(1)}, f32[80,32,128]{2,1,0:T(8,128)S(1)}, u32[]{:S(2)}, u32[]{:S(2)}) collective-permute-start(f32[80,32,128]{2,1,0:T(8,128)S(1)} %collective-permute-done.17.side_ref), channel_id=1, source_target_pairs={{5,4},{2,3},{13,12},{10,11},{21,20},{18,19},{29,28},{26,27}} | collective-permute-start | bytes 3932168 | tf_op jit(solution)/shard_map/ppermute | solution.py:472
  56.1 38.1 %collective-permute-start.2 = (f32[50,32,128]{2,1,0:T(8,128)S(1)}, f32[50,32,128]{2,1,0:T(8,128)S(1)}, u32[]{:S(2)}, u32[]{:S(2)}) collective-permute-start(f32[50,32,128]{2,1,0:T(8,128)S(1)} %collective-permute-done.1.side_ref), channel_id=1, source_target_pairs={{1,4},{6,3},{9,12},{14,11},{17,20},{22,19},{25,28},{30,27}} | collective-permute-start | bytes 2457608 | tf_op jit(solution)/shard_map/ppermute | solution.py:464
  57.4 53.7 %collective-permute-start.13 = (f32[80,32,128]{2,1,0:T(8,128)S(1)}, f32[80,32,128]{2,1,0:T(8,128)S(1)}, u32[]{:S(2)}, u32[]{:S(2)}) collective-permute-start(f32[80,32,128]{2,1,0:T(8,128)S(1)} %collective-permute-done.12.side_ref), channel_id=1, source_target_pairs={{5,4},{2,3},{13,12},{10,11},{21,20},{18,19},{29,28},{26,27}} | collective-permute-start | bytes 3932168 | tf_op jit(solution)/shard_map/ppermute | solution.py:472
  58.7 60.1 %collective-permute-start.6 = (f32[80,32,128]{2,1,0:T(8,128)S(1)}, f32[80,32,128]{2,1,0:T(8,128)S(1)}, u32[]{:S(2)}, u32[]{:S(2)}) collective-permute-start(f32[80,32,128]{2,1,0:T(8,128)S(1)} %collective-permute-done.5.side_ref), channel_id=1, source_target_pairs={{5,4},{2,3},{13,12},{10,11},{21,20},{18,19},{29,28},{26,27}} | collective-permute-start | bytes 3932168 | tf_op jit(solution)/shard_map/ppermute | solution.py:472
  98.6 9.1 %copy-start.2 = (f32[24,32,128]{2,1,0:T(8,128)}, f32[24,32,128]{2,1,0:T(8,128)S(1)}, u32[]{:S(2)}) copy-start(f32[24,32,128]{2,1,0:T(8,128)S(1)} %get-tuple-element.26.refs_0_) | copy-start | bytes 1179652
  98.6 11.2 %copy-start.4 = (f32[24,32,128]{2,1,0:T(8,128)}, f32[24,32,128]{2,1,0:T(8,128)S(1)}, u32[]{:S(2)}) copy-start(f32[24,32,128]{2,1,0:T(8,128)S(1)} %get-tuple-element.27.refs_1_) | copy-start | bytes 1179652
  98.6 25.7 %collective-permute-start.10 = (f32[24,32,128]{2,1,0:T(8,128)S(1)}, f32[24,32,128]{2,1,0:T(8,128)S(1)}, u32[]{:S(2)}, u32[]{:S(2)}) collective-permute-start(f32[24,32,128]{2,1,0:T(8,128)S(1)} %get-tuple-element.26.refs_0_), channel_id=1, source_target_pairs={{8,0},{16,8},{24,16},{9,1},{17,9},{25,17},{10,2},{18,10},{26,18},{... | collective-permute-start | bytes 1179656 | tf_op jit(solution)/shard_map/ppermute | solution.py:486
  107.7 24.7 %collective-permute-start.20 = (f32[40,32,128]{2,1,0:T(8,128)S(1)}, f32[40,32,128]{2,1,0:T(8,128)S(1)}, u32[]{:S(2)}, u32[]{:S(2)}) collective-permute-start(f32[40,32,128]{2,1,0:T(8,128)S(1)} %get-tuple-element.32.refs_8_), channel_id=1, source_target_pairs={{8,0},{16,8},{24,16},{9,1},{17,9},{25,17},{10,2},{18,10},{26,18},{... | collective-permute-start | bytes 1966088 | tf_op jit(solution)/shard_map/ppermute | solution.py:486
  109.8 20.6 %collective-permute-start.9 = (f32[24,32,128]{2,1,0:T(8,128)S(1)}, f32[24,32,128]{2,1,0:T(8,128)S(1)}, u32[]{:S(2)}, u32[]{:S(2)}) collective-permute-start(f32[24,32,128]{2,1,0:T(8,128)S(1)} %get-tuple-element.27.refs_1_), channel_id=1, source_target_pairs={{0,8},{8,16},{16,24},{1,9},{9,17},{17,25},{2,10},{10,18},{18,26},{... | collective-permute-start | bytes 1179656 | tf_op jit(solution)/shard_map/ppermute | solution.py:486
  111.1 30.9 %collective-permute-start.19 = (f32[40,32,128]{2,1,0:T(8,128)}, f32[40,32,128]{2,1,0:T(8,128)}, u32[]{:S(2)}, u32[]{:S(2)}) collective-permute-start(f32[40,32,128]{2,1,0:T(8,128)} %get-tuple-element.33.refs_9_), channel_id=1, source_target_pairs={{0,8},{8,16},{16,24},{1,9},{9,17},{17,25},{2,10},{10,18},{18,26},{... | collective-permute-start | bytes 1966088 | tf_op jit(solution)/shard_map/ppermute | solution.py:486
  118.8 23.2 %collective-permute-start.15 = (f32[40,32,128]{2,1,0:T(8,128)}, f32[40,32,128]{2,1,0:T(8,128)}, u32[]{:S(2)}, u32[]{:S(2)}) collective-permute-start(f32[40,32,128]{2,1,0:T(8,128)} %get-tuple-element.29.refs_4_), channel_id=1, source_target_pairs={{8,0},{16,8},{24,16},{9,1},{17,9},{25,17},{10,2},{18,10},{26,18},{... | collective-permute-start | bytes 1966088 | tf_op jit(solution)/shard_map/ppermute | solution.py:486
  124.3 21.3 %collective-permute-start.14 = (f32[40,32,128]{2,1,0:T(8,128)}, f32[40,32,128]{2,1,0:T(8,128)}, u32[]{:S(2)}, u32[]{:S(2)}) collective-permute-start(f32[40,32,128]{2,1,0:T(8,128)} %get-tuple-element.30.refs_5_), channel_id=1, source_target_pairs={{0,8},{8,16},{16,24},{1,9},{9,17},{17,25},{2,10},{10,18},{18,26},{... | collective-permute-start | bytes 1966088 | tf_op jit(solution)/shard_map/ppermute | solution.py:486
  131.1 21.7 %collective-permute-start.7 = (f32[24,32,128]{2,1,0:T(8,128)}, f32[24,32,128]{2,1,0:T(8,128)}, u32[]{:S(2)}, u32[]{:S(2)}) collective-permute-start(f32[24,32,128]{2,1,0:T(8,128)} %get-tuple-element.24.refs_13_), channel_id=1, source_target_pairs={{0,8},{8,16},{16,24},{1,9},{9,17},{17,25},{2,10},{10,18},{18,26},{... | collective-permute-start | bytes 1179656 | tf_op jit(solution)/shard_map/ppermute | solution.py:486
  133.2 19.6 %collective-permute-start.8 = (f32[24,32,128]{2,1,0:T(8,128)}, f32[24,32,128]{2,1,0:T(8,128)}, u32[]{:S(2)}, u32[]{:S(2)}) collective-permute-start(f32[24,32,128]{2,1,0:T(8,128)} %get-tuple-element.25.refs_12_), channel_id=1, source_target_pairs={{8,0},{16,8},{24,16},{9,1},{17,9},{25,17},{10,2},{18,10},{26,18},{... | collective-permute-start | bytes 1179656 | tf_op jit(solution)/shard_map/ppermute | solution.py:486
  138.6 7.1 %copy-start.3 = (f32[24,32,128]{2,1,0:T(8,128)S(1)}, f32[24,32,128]{2,1,0:T(8,128)}, u32[]{:S(2)}) copy-start(f32[24,32,128]{2,1,0:T(8,128)} %copy-done.2) | copy-start | bytes 1179652
  138.6 7.1 %copy-start.5 = (f32[24,32,128]{2,1,0:T(8,128)S(1)}, f32[24,32,128]{2,1,0:T(8,128)}, u32[]{:S(2)}) copy-start(f32[24,32,128]{2,1,0:T(8,128)} %copy-done.4) | copy-start | bytes 1179652
  138.6 7.1 %copy-start.7 = (f32[24,32,128]{2,1,0:T(8,128)S(1)}, f32[24,32,128]{2,1,0:T(8,128)}, u32[]{:S(2)}) copy-start(f32[24,32,128]{2,1,0:T(8,128)} %copy-done.6) | copy-start | bytes 1179652
  138.6 7.1 %copy-start.9 = (f32[24,32,128]{2,1,0:T(8,128)S(1)}, f32[24,32,128]{2,1,0:T(8,128)}, u32[]{:S(2)}) copy-start(f32[24,32,128]{2,1,0:T(8,128)} %copy-done.8) | copy-start | bytes 1179652
  138.6 7.1 %copy-start.12 = (f32[1152]{0:T(1024)S(1)}, f32[1152]{0:T(1024)}, u32[]{:S(2)}) copy-start(f32[1152]{0:T(1024)} %strength_ref.3) | copy-start | bytes 13828
  138.6 7.1 %copy-start.14 = (s32[4,2]{0,1:T(2,128)S(1)}, s32[4,2]{0,1:T(2,128)}, u32[]{:S(2)}) copy-start(s32[4,2]{0,1:T(2,128)} %param.11) | copy-start | bytes 100
  (4 other events, 14.6 us)

commit v7 on v6

--- a/solution.py
+++ b/solution.py
@@ -85,7 +85,7 @@
 LANES = 128
 PAIR = 2
 GROUP = 4
-CUTS = (0, 3, 8, 13, 16)
+CUTS = (0, 4, 11, 16)
 
 
 def vmem(shape):
@@ -494,12 +494,12 @@
     )
     places += [edge + start for start, _ in middle]
     shifts = quad_shift.T
+    late = -(-chunks[-1][0][1] // ND)
+    rims = list(range(late)) + list(range(local - late, local))
     window, inner = quadruplets(
-        None, parts, places, local, strength, shifts, first, list(range(1, local - 1)), None
+        None, parts, places, local, strength, shifts, first, list(range(late, local - late)), None
     )
-    window, result = quadruplets(
-        window, last, last_places, local, strength, shifts, first, [0, local - 1], inner
-    )
+    window, result = quadruplets(window, last, last_places, local, strength, shifts, first, rims, inner)
     return untiled(result, lat_dev)
 
 

time: 157 us -> 168 us (1.070)
  the two profiles are of different devices: /device:TPU:27 before, /device:TPU:19 now
where the time goes in v7:
time: 168 us; the launch traced here: 167 us
  waiting for transfers between devices  87.9 us (52%)
  Pallas kernels  46.6 us (28%)
  starting transfers between devices  29.5 us (18%)
  local copies, waits for them, and re-layouts  3.04 us (2%)
    ppermute x1, waiting for transfers between devices, halo_plan(): hands_in = [lax.ppermute(sides_in[0], 'lat', relays)]  46.8 us
    pallas_call x4, Pallas kernels, propagate(): pl.pallas_call(kernel, out_shape=[jax.ShapeDtypeStruct((length, rows, LAN...  23.8 us
    ppermute x6, starting transfers between devices, halo_plan(): last = [lax.ppermute(high, 'comp', z_up), lax.ppermute(low, 'comp', z_down)]  16.3 us
    ppermute x1, waiting for transfers between devices, halo_plan(): ahead += [lax.ppermute(part, 'lat', aheads) for part in rest]  15.7 us
    ppermute x1, waiting for transfers between devices, halo_plan(): ahead = [None, lax.ppermute(part, 'lat', aheads)]  14.4 us
    ppermute x6, waiting for transfers between devices, halo_plan(): last = [lax.ppermute(high, 'comp', z_up), lax.ppermute(low, 'comp', z_down)]  11.1 us
    pallas_call x2, Pallas kernels, quadruplets(): pl.pallas_call(kernel, out_shape=[vmem(((local + 2 * reach) * ND, rows, L...  9.83 us
    pallas_call x2, Pallas kernels, load(): pl.pallas_call(kernel, out_shape=[vmem((size, rows, LANES)) for size in s...  6.12 us
  transfers between devices with their start and end apart: 16, of which 4 were waited for; matrix products, arithmetic and copies ran while one was open for 0% of the time, Pallas kernels for 23%

profile of v7, /device:TPU:19, one launch (start us, length us, event | category | flops | bytes accessed | tf_op | source)
XLA Modules:
  0.0 167.5 jit_solution(1295500495887346250)
XLA Ops:
  0.0 0.7 copy-done.9
  0.7 3.4 %load.2 = (f32[65,32,128]{2,1,0:T(8,128)}, f32[112,32,128]{2,1,0:T(8,128)}, f32[1,32,128]{2,1,0:T(8,128)S(1)}) custom-call(f32[288,32,128]{2,1,0:T(8,128)} %bitcast.6.own_ref.own_hbm, s32[1,32,128]{2,1,0:T(8,128)S(1)} %bitcast.19), custom_call_target="tpu_custom_call" | custom-call | bytes 5767168 | tf_op jit(solution)/shard_map/load/pallas_call | solution.py:167
  4.1 5.0 %collective-permute-start.11 = (f32[112,32,128]{2,1,0:T(8,128)}, f32[112,32,128]{2,1,0:T(8,128)}, u32[]{:S(2)}, u32[]{:S(2)}) collective-permute-start(f32[112,32,128]{2,1,0:T(8,128)} %get-tuple-element.23), channel_id=1, source_target_pairs={{3,6},{4,1},{11,14},{12,9},{19,22},{20,17},{27,30},{28,25}} | collective-permute-start | bytes 5505032 | tf_op jit(solution)/shard_map/ppermute | solution.py:462
  9.1 2.7 %load.3 = f32[112,32,128]{2,1,0:T(8,128)} custom-call(f32[288,32,128]{2,1,0:T(8,128)} %bitcast.6.own_ref.own_hbm), custom_call_target="tpu_custom_call" | custom-call | bytes 3670016 | tf_op jit(solution)/shard_map/load/pallas_call | solution.py:167
  11.9 1.4 collective-permute-start.4
  14.0 14.4 %collective-permute-done.11.other_ref = f32[112,32,128]{2,1,0:T(8,128)} collective-permute-done((f32[112,32,128]{2,1,0:T(8,128)}, f32[112,32,128]{2,1,0:T(8,128)}, u32[]{:S(2)}, u32[]{:S(2)}) %collective-permute-start.11) | collective-permute-done | bytes 1835040 | tf_op jit(solution)/shard_map/ppermute | solution.py:462
  28.3 3.2 %pack_message.3 = f32[112,32,128]{2,1,0:T(8,128)S(1)} custom-call(f32[288]{0:T(512)S(1)} %copy-done.6, s32[2]{0:T(128)S(1)} %pad_add_fusion.place_ref, f32[288,32,128]{2,1,0:T(8,128)} %bitcast.6.own_ref.own_hbm, f32[112,32,128]{2,1,0:T(8,128)} %collective-permute-done.11.other_ref), custom_call_target="tpu_custom_call" | custom-call | bytes 5505024 | tf_op jit(solution)/shard_map/pack_message/pallas_call | solution.py:228
  31.5 0.8 collective-permute-start.12
  32.3 15.7 %collective-permute-done.4.other_ref = f32[112,32,128]{2,1,0:T(8,128)S(1)} collective-permute-done((f32[112,32,128]{2,1,0:T(8,128)}, f32[112,32,128]{2,1,0:T(8,128)S(1)}, u32[]{:S(2)}, u32[]{:S(2)}) %collective-permute-start.4) | collective-permute-done | bytes 1835040 | tf_op jit(solution)/shard_map/ppermute | solution.py:466
  48.0 2.2 %pack_message.2 = f32[112,32,128]{2,1,0:T(8,128)S(1)} custom-call(f32[288]{0:T(512)S(1)} %copy-done.6, s32[2]{0:T(128)S(1)} %pad_add_fusion.place_ref, f32[288,32,128]{2,1,0:T(8,128)} %bitcast.6.own_ref.own_hbm, f32[112,32,128]{2,1,0:T(8,128)S(1)} %collective-permute-done.4.other_ref), custom_call_target="tpu_custom_call" | custom-call | bytes 5505024 | tf_op jit(solution)/shard_map/pack_message/pallas_call | solution.py:228
  50.2 0.8 collective-permute-start.5
  51.0 1.5 pack_first.1
  52.5 0.7 collective-permute-start.1
  53.2 1.3 collective-permute-start.13
  54.5 1.3 collective-permute-start.6
  55.8 1.3 collective-permute-start.2
  57.2 46.8 %collective-permute-done.2.hand_ref = f32[66,32,128]{2,1,0:T(8,128)S(1)} collective-permute-done((f32[66,32,128]{2,1,0:T(8,128)S(1)}, f32[66,32,128]{2,1,0:T(8,128)S(1)}, u32[]{:S(2)}, u32[]{:S(2)}) %collective-permute-start.2) | collective-permute-done | bytes 1081376 | tf_op jit(solution)/shard_map/ppermute | solution.py:464
  104.0 5.6 %propagate.5 = (f32[32,32,128]{2,1,0:T(8,128)S(1)}, f32[32,32,128]{2,1,0:T(8,128)}) custom-call(f32[288]{0:T(512)S(1)} %copy-done.6, f32[288]{0:T(512)S(1)} %copy-done.8, s32[2]{0:T(128)S(1)} %pad_add_fusion.place_ref, f32[3,32,128]{2,1,0:T(8,128)S(1)} %pad_maximum_fusion.mask_ref, f32[288,32,128]{2,1,0:T(8,128)} %bitcast.6.own_ref.own_hbm, ...), custom_call_target="tpu_custom_call" | custom-call | flops 10485760 | bytes 5242880 | tf_op jit(solution)/shard_map/propagate/pallas_call | solution.py:347
  109.6 2.1 %collective-permute-start.10 = (f32[32,32,128]{2,1,0:T(8,128)S(1)}, f32[32,32,128]{2,1,0:T(8,128)S(1)}, u32[]{:S(2)}, u32[]{:S(2)}) collective-permute-start(f32[32,32,128]{2,1,0:T(8,128)S(1)} %get-tuple-element.21.refs_0_), channel_id=1, source_target_pairs={{8,0},{16,8},{24,16},{9,1},{17,9},{25,17},{10,2},{18,10},{26,18},{... | collective-permute-start | bytes 1572872 | tf_op jit(solution)/shard_map/ppermute | solution.py:486
  111.7 8.4 %propagate.6 = (f32[56,32,128]{2,1,0:T(8,128)S(1)}, f32[56,32,128]{2,1,0:T(8,128)}) custom-call(f32[288]{0:T(512)S(1)} %copy-done.6, f32[288]{0:T(512)S(1)} %copy-done.8, s32[2]{0:T(128)S(1)} %pad_add_fusion.place_ref, f32[3,32,128]{2,1,0:T(8,128)S(1)} %pad_maximum_fusion.mask_ref, f32[288,32,128]{2,1,0:T(8,128)} %bitcast.6.own_ref.own_hbm, ...), custom_call_target="tpu_custom_call" | custom-call | flops 18350080 | bytes 9175040 | tf_op jit(solution)/shard_map/propagate/pallas_call | solution.py:347
  120.1 2.0 %collective-permute-start.15 = (f32[56,32,128]{2,1,0:T(8,128)S(1)}, f32[56,32,128]{2,1,0:T(8,128)}, u32[]{:S(2)}, u32[]{:S(2)}) collective-permute-start(f32[56,32,128]{2,1,0:T(8,128)S(1)} %get-tuple-element.24.refs_4_), channel_id=1, source_target_pairs={{8,0},{16,8},{24,16},{9,1},{17,9},{25,17},{10,2},{18,10},{26,18},{... | collective-permute-start | bytes 2752520 | tf_op jit(solution)/shard_map/ppermute | solution.py:486
  122.1 4.2 %collective-permute-start.14 = (f32[56,32,128]{2,1,0:T(8,128)}, f32[56,32,128]{2,1,0:T(8,128)}, u32[]{:S(2)}, u32[]{:S(2)}) collective-permute-start(f32[56,32,128]{2,1,0:T(8,128)} %get-tuple-element.25.refs_5_), channel_id=1, source_target_pairs={{0,8},{8,16},{16,24},{1,9},{9,17},{17,25},{2,10},{10,18},{18,26},{... | collective-permute-start | bytes 2752520 | tf_op jit(solution)/shard_map/ppermute | solution.py:486
  126.3 6.5 %propagate.4 = (f32[40,32,128]{2,1,0:T(8,128)}, f32[40,32,128]{2,1,0:T(8,128)}) custom-call(f32[288]{0:T(512)S(1)} %copy-done.6, f32[288]{0:T(512)S(1)} %copy-done.8, s32[2]{0:T(128)S(1)} %pad_add_fusion.place_ref, f32[3,32,128]{2,1,0:T(8,128)S(1)} %pad_maximum_fusion.mask_ref, f32[288,32,128]{2,1,0:T(8,128)} %bitcast.6.own_ref.own_hbm, ...), custom_call_target="tpu_custom_call" | custom-call | flops 13107200 | bytes 6553600 | tf_op jit(solution)/shard_map/propagate/pallas_call | solution.py:347
  132.9 1.9 %collective-permute-start.7 = (f32[40,32,128]{2,1,0:T(8,128)}, f32[40,32,128]{2,1,0:T(8,128)S(1)}, u32[]{:S(2)}, u32[]{:S(2)}) collective-permute-start(f32[40,32,128]{2,1,0:T(8,128)} %get-tuple-element.19.refs_9_), channel_id=1, source_target_pairs={{0,8},{8,16},{16,24},{1,9},{9,17},{17,25},{2,10},{10,18},{18,26},{... | collective-permute-start | bytes 1966088 | tf_op jit(solution)/shard_map/ppermute | solution.py:486
  134.8 3.4 %collective-permute-start.8 = (f32[40,32,128]{2,1,0:T(8,128)}, f32[40,32,128]{2,1,0:T(8,128)}, u32[]{:S(2)}, u32[]{:S(2)}) collective-permute-start(f32[40,32,128]{2,1,0:T(8,128)} %get-tuple-element.20.refs_8_), channel_id=1, source_target_pairs={{8,0},{16,8},{24,16},{9,1},{17,9},{25,17},{10,2},{18,10},{26,18},{... | collective-permute-start | bytes 1966088 | tf_op jit(solution)/shard_map/ppermute | solution.py:486
  138.2 0.8 copy-done.4
  139.0 2.7 %collective-permute-start.9 = (f32[32,32,128]{2,1,0:T(8,128)}, f32[32,32,128]{2,1,0:T(8,128)}, u32[]{:S(2)}, u32[]{:S(2)}) collective-permute-start(f32[32,32,128]{2,1,0:T(8,128)} %get-tuple-element.22.refs_1_), channel_id=1, source_target_pairs={{0,8},{8,16},{16,24},{1,9},{9,17},{17,25},{2,10},{10,18},{18,26},{... | collective-permute-start | bytes 1572872 | tf_op jit(solution)/shard_map/ppermute | solution.py:486
  141.7 1.5 copy-done.1
  143.2 3.3 %propagate.7.refs_10_ = f32[32,32,128]{2,1,0:T(8,128)S(1)} custom-call(f32[288]{0:T(512)S(1)} %copy-done.6, f32[288]{0:T(512)S(1)} %copy-done.8, s32[2]{0:T(128)S(1)} %pad_add_fusion.place_ref, f32[3,32,128]{2,1,0:T(8,128)S(1)} %pad_maximum_fusion.mask_ref, f32[288,32,128]{2,1,0:T(8,128)} %bitcast.6.own_ref.own_hbm, ...), custom_call_target="tpu_custom_call" | custom-call | flops 5242880 | bytes 2621440 | tf_op jit(solution)/shard_map/propagate/pallas_call | solution.py:347
  146.5 11.1 %collective-permute-done.9.refs_2_ = f32[32,32,128]{2,1,0:T(8,128)} collective-permute-done((f32[32,32,128]{2,1,0:T(8,128)}, f32[32,32,128]{2,1,0:T(8,128)}, u32[]{:S(2)}, u32[]{:S(2)}) %collective-permute-start.9) | collective-permute-done | bytes 524320 | tf_op jit(solution)/shard_map/ppermute | solution.py:486
  157.6 5.8 %quadruplets.2 = (f32[544,32,128]{2,1,0:T(8,128)S(1)}, f32[288,32,128]{2,1,0:T(8,128)}) custom-call(f32[1152]{0:T(1024)S(1)} %copy-done.7, s32[2,4]{1,0:T(2,128)S(1)} %bitcast.20, s32[1]{0:T(128)} %bitcast.1.first_ref, f32[32,32,128]{2,1,0:T(8,128)S(1)} %copy-done.3, f32[32,32,128]{2,1,0:T(8,128)} %get-tuple-element.22.refs_1_, ...), custom_call_target="tpu_custom_call" | custom-call | flops 9830400 | bytes 15728640 | tf_op jit(solution)/shard_map/quadruplets/pallas_call | solution.py:414
  163.4 4.1 %quadruplets.3 = (f32[544,32,128]{2,1,0:T(8,128)S(1)}, f32[288,32,128]{2,1,0:T(8,128)}) custom-call(f32[1152]{0:T(1024)S(1)} %copy-done.7, s32[2,4]{1,0:T(2,128)S(1)} %bitcast.21, s32[1]{0:T(128)} %bitcast.1.first_ref, f32[40,32,128]{2,1,0:T(8,128)S(1)} %collective-permute-done.7.refs_0_, ...), custom_call_target="tpu_custom_call", output_to_operand_aliasing={{0}: (5, {}), {1}: (6, {})} | custom-call | flops 7864320 | bytes 12582912 | tf_op jit(solution)/shard_map/quadruplets/pallas_call | solution.py:414
  (37 shorter events, 0.7 us)
Async XLA Ops:
  0.0 0.7 copy-start.9
  4.1 24.2 %copy-start.6 = (f32[288]{0:T(512)S(1)}, f32[288]{0:T(512)}, u32[]{:S(2)}) copy-start(f32[288]{0:T(512)} %a_ref.13) | copy-start | bytes 3460
  4.1 24.2 %collective-permute-start.11 = (f32[112,32,128]{2,1,0:T(8,128)}, f32[112,32,128]{2,1,0:T(8,128)}, u32[]{:S(2)}, u32[]{:S(2)}) collective-permute-start(f32[112,32,128]{2,1,0:T(8,128)} %get-tuple-element.23), channel_id=1, source_target_pairs={{3,6},{4,1},{11,14},{12,9},{19,22},{20,17},{27,30},{28,25}} | collective-permute-start | bytes 5505032 | tf_op jit(solution)/shard_map/ppermute | solution.py:462
  11.9 36.1 %collective-permute-start.4 = (f32[112,32,128]{2,1,0:T(8,128)}, f32[112,32,128]{2,1,0:T(8,128)S(1)}, u32[]{:S(2)}, u32[]{:S(2)}) collective-permute-start(f32[112,32,128]{2,1,0:T(8,128)} %load.3), channel_id=1, source_target_pairs={{3,6},{4,1},{11,14},{12,9},{19,22},{20,17},{27,30},{28,25}} | collective-permute-start | bytes 5505032 | tf_op jit(solution)/shard_map/ppermute | solution.py:466
  13.3 90.7 %collective-permute-start.3 = (f32[288,32,128]{2,1,0:T(8,128)}, f32[288,32,128]{2,1,0:T(8,128)}, u32[]{:S(2)}, u32[]{:S(2)}) collective-permute-start(f32[288,32,128]{2,1,0:T(8,128)} %bitcast.6.own_ref.own_hbm), channel_id=1, source_target_pairs={{0,1},{1,0},{2,3},{3,2},{4,5},{5,4},{6,7},{7,6},{8,9},{9,8},{10,11... | collective-permute-start | bytes 14155784 | tf_op jit(solution)/shard_map/ppermute | solution.py:467
  13.4 37.6 %collective-permute-start = (f32[65,32,128]{2,1,0:T(8,128)}, f32[65,32,128]{2,1,0:T(8,128)S(1)}, u32[]{:S(2)}, u32[]{:S(2)}) collective-permute-start(f32[65,32,128]{2,1,0:T(8,128)} %get-tuple-element.18.own_ref), channel_id=1, source_target_pairs={{0,1},{1,0},{2,3},{3,2},{4,5},{5,4},{6,7},{7,6},{8,9},{9,8},{10,11... | collective-permute-start | bytes 3194888 | tf_op jit(solution)/shard_map/ppermute | solution.py:461
  31.5 21.7 %collective-permute-start.12 = (f32[112,32,128]{2,1,0:T(8,128)S(1)}, f32[112,32,128]{2,1,0:T(8,128)S(1)}, u32[]{:S(2)}, u32[]{:S(2)}) collective-permute-start(f32[112,32,128]{2,1,0:T(8,128)S(1)} %pack_message.3), channel_id=1, source_target_pairs={{1,2},{5,6},{2,1},{6,5},{9,10},{13,14},{10,9},{14,13},{17,18},{21,... | collective-permute-start | bytes 5505032 | tf_op jit(solution)/shard_map/ppermute | solution.py:471
  50.1 53.8 %copy-start.8 = (f32[288]{0:T(512)S(1)}, f32[288]{0:T(512)}, u32[]{:S(2)}) copy-start(f32[288]{0:T(512)} %b_ref.7) | copy-start | bytes 3460
  50.2 4.4 %collective-permute-start.5 = (f32[112,32,128]{2,1,0:T(8,128)S(1)}, f32[112,32,128]{2,1,0:T(8,128)S(1)}, u32[]{:S(2)}, u32[]{:S(2)}) collective-permute-start(f32[112,32,128]{2,1,0:T(8,128)S(1)} %pack_message.2), channel_id=1, source_target_pairs={{1,2},{5,6},{2,1},{6,5},{9,10},{13,14},{10,9},{14,13},{17,18},{21,... | collective-permute-start | bytes 5505032 | tf_op jit(solution)/shard_map/ppermute | solution.py:471
  52.5 3.4 %collective-permute-start.1 = (f32[66,32,128]{2,1,0:T(8,128)S(1)}, f32[66,32,128]{2,1,0:T(8,128)S(1)}, u32[]{:S(2)}, u32[]{:S(2)}) collective-permute-start(f32[66,32,128]{2,1,0:T(8,128)S(1)} %pack_first.1), channel_id=1, source_target_pairs={{1,2},{5,6},{2,1},{6,5},{9,10},{13,14},{10,9},{14,13},{17,18},{21,... | collective-permute-start | bytes 3244040 | tf_op jit(solution)/shard_map/ppermute | solution.py:463
  53.2 58.4 %collective-permute-start.13 = (f32[112,32,128]{2,1,0:T(8,128)S(1)}, f32[112,32,128]{2,1,0:T(8,128)S(1)}, u32[]{:S(2)}, u32[]{:S(2)}) collective-permute-start(f32[112,32,128]{2,1,0:T(8,128)S(1)} %collective-permute-done.12.side_ref), channel_id=1, source_target_pairs={{5,4},{2,3},{13,12},{10,11},{21,20},{18,19},{29,28},{26,27}} | collective-permute-start | bytes 5505032 | tf_op jit(solution)/shard_map/ppermute | solution.py:472
  54.5 71.8 %collective-permute-start.6 = (f32[112,32,128]{2,1,0:T(8,128)S(1)}, f32[112,32,128]{2,1,0:T(8,128)S(1)}, u32[]{:S(2)}, u32[]{:S(2)}) collective-permute-start(f32[112,32,128]{2,1,0:T(8,128)S(1)} %collective-permute-done.5.side_ref), channel_id=1, source_target_pairs={{5,4},{2,3},{13,12},{10,11},{21,20},{18,19},{29,28},{26,27}} | collective-permute-start | bytes 5505032 | tf_op jit(solution)/shard_map/ppermute | solution.py:472
  55.8 48.1 %collective-permute-start.2 = (f32[66,32,128]{2,1,0:T(8,128)S(1)}, f32[66,32,128]{2,1,0:T(8,128)S(1)}, u32[]{:S(2)}, u32[]{:S(2)}) collective-permute-start(f32[66,32,128]{2,1,0:T(8,128)S(1)} %collective-permute-done.1.side_ref), channel_id=1, source_target_pairs={{1,4},{6,3},{9,12},{14,11},{17,20},{22,19},{25,28},{30,27}} | collective-permute-start | bytes 3244040 | tf_op jit(solution)/shard_map/ppermute | solution.py:464
  109.5 10.5 %copy-start.2 = (f32[32,32,128]{2,1,0:T(8,128)}, f32[32,32,128]{2,1,0:T(8,128)S(1)}, u32[]{:S(2)}) copy-start(f32[32,32,128]{2,1,0:T(8,128)S(1)} %get-tuple-element.21.refs_0_) | copy-start | bytes 1572868
  109.6 28.6 %collective-permute-start.10 = (f32[32,32,128]{2,1,0:T(8,128)S(1)}, f32[32,32,128]{2,1,0:T(8,128)S(1)}, u32[]{:S(2)}, u32[]{:S(2)}) collective-permute-start(f32[32,32,128]{2,1,0:T(8,128)S(1)} %get-tuple-element.21.refs_0_), channel_id=1, source_target_pairs={{8,0},{16,8},{24,16},{9,1},{17,9},{25,17},{10,2},{18,10},{26,18},{... | collective-permute-start | bytes 1572872 | tf_op jit(solution)/shard_map/ppermute | solution.py:486
  120.1 37.5 %collective-permute-start.15 = (f32[56,32,128]{2,1,0:T(8,128)S(1)}, f32[56,32,128]{2,1,0:T(8,128)}, u32[]{:S(2)}, u32[]{:S(2)}) collective-permute-start(f32[56,32,128]{2,1,0:T(8,128)S(1)} %get-tuple-element.24.refs_4_), channel_id=1, source_target_pairs={{8,0},{16,8},{24,16},{9,1},{17,9},{25,17},{10,2},{18,10},{26,18},{... | collective-permute-start | bytes 2752520 | tf_op jit(solution)/shard_map/ppermute | solution.py:486
  122.1 35.5 %collective-permute-start.14 = (f32[56,32,128]{2,1,0:T(8,128)}, f32[56,32,128]{2,1,0:T(8,128)}, u32[]{:S(2)}, u32[]{:S(2)}) collective-permute-start(f32[56,32,128]{2,1,0:T(8,128)} %get-tuple-element.25.refs_5_), channel_id=1, source_target_pairs={{0,8},{8,16},{16,24},{1,9},{9,17},{17,25},{2,10},{10,18},{18,26},{... | collective-permute-start | bytes 2752520 | tf_op jit(solution)/shard_map/ppermute | solution.py:486
  126.3 6.5 %copy-start = (f32[112,32,128]{2,1,0:T(8,128)}, f32[112,32,128]{2,1,0:T(8,128)S(1)}, u32[]{:S(2)}) copy-start(f32[112,32,128]{2,1,0:T(8,128)S(1)} %collective-permute-done.6.hand_ref) | copy-start | bytes 5505028
  132.9 30.6 %collective-permute-start.7 = (f32[40,32,128]{2,1,0:T(8,128)}, f32[40,32,128]{2,1,0:T(8,128)S(1)}, u32[]{:S(2)}, u32[]{:S(2)}) collective-permute-start(f32[40,32,128]{2,1,0:T(8,128)} %get-tuple-element.19.refs_9_), channel_id=1, source_target_pairs={{0,8},{8,16},{16,24},{1,9},{9,17},{17,25},{2,10},{10,18},{18,26},{... | collective-permute-start | bytes 1966088 | tf_op jit(solution)/shard_map/ppermute | solution.py:486
  134.8 28.6 %collective-permute-start.8 = (f32[40,32,128]{2,1,0:T(8,128)}, f32[40,32,128]{2,1,0:T(8,128)}, u32[]{:S(2)}, u32[]{:S(2)}) collective-permute-start(f32[40,32,128]{2,1,0:T(8,128)} %get-tuple-element.20.refs_8_), channel_id=1, source_target_pairs={{8,0},{16,8},{24,16},{9,1},{17,9},{25,17},{10,2},{18,10},{26,18},{... | collective-permute-start | bytes 1966088 | tf_op jit(solution)/shard_map/ppermute | solution.py:486
  138.2 0.8 copy-start.4
  139.0 18.6 %collective-permute-start.9 = (f32[32,32,128]{2,1,0:T(8,128)}, f32[32,32,128]{2,1,0:T(8,128)}, u32[]{:S(2)}, u32[]{:S(2)}) collective-permute-start(f32[32,32,128]{2,1,0:T(8,128)} %get-tuple-element.22.refs_1_), channel_id=1, source_target_pairs={{0,8},{8,16},{16,24},{1,9},{9,17},{17,25},{2,10},{10,18},{18,26},{... | collective-permute-start | bytes 1572872 | tf_op jit(solution)/shard_map/ppermute | solution.py:486
  141.7 1.5 copy-start.1
  143.2 14.4 %copy-start.3 = (f32[32,32,128]{2,1,0:T(8,128)S(1)}, f32[32,32,128]{2,1,0:T(8,128)}, u32[]{:S(2)}) copy-start(f32[32,32,128]{2,1,0:T(8,128)} %copy-done.2) | copy-start | bytes 1572868
  143.2 14.4 %copy-start.5 = (f32[32,32,128]{2,1,0:T(8,128)S(1)}, f32[32,32,128]{2,1,0:T(8,128)}, u32[]{:S(2)}) copy-start(f32[32,32,128]{2,1,0:T(8,128)} %copy-done.4) | copy-start | bytes 1572868
  143.2 14.4 %copy-start.7 = (f32[1152]{0:T(1024)S(1)}, f32[1152]{0:T(1024)}, u32[]{:S(2)}) copy-start(f32[1152]{0:T(1024)} %strength_ref.3) | copy-start | bytes 13828
  143.2 14.4 %copy-start.10 = (s32[4,2]{0,1:T(2,128)S(1)}, s32[4,2]{0,1:T(2,128)}, u32[]{:S(2)}) copy-start(s32[4,2]{0,1:T(2,128)} %param.11) | copy-start | bytes 100

commit v8 on v7

--- a/solution.py
+++ b/solution.py
@@ -84,8 +84,8 @@
 
 LANES = 128
 PAIR = 2
-GROUP = 4
-CUTS = (0, 4, 11, 16)
+GROUP = 8
+CUTS = (0, 4, 9, 13, 16)
 
 
 def vmem(shape):
@@ -284,6 +284,7 @@
                     j=j,
                     a=jnp.abs(a),
                     b=jnp.abs(b),
+                    keep=1.0 - jnp.abs(a) - jnp.abs(b),
                     west=west,
                     fore=fore,
                     back=back,
@@ -302,28 +303,39 @@
                     ],
                 )
 
+            def across(c, ahead, behind):
+                return ahead if ahead is behind else jnp.where(c["west"], ahead, behind)
+
             def beside(c, x):
                 turned = pltpu.roll(x, c["turn"], 1)
                 rolled = [pltpu.roll(turned[8 * t:8 * t + 8], c["step"], 0) for t in range(half // 8)]
                 over = [
-                    jnp.where(c["first"], jnp.where(c["west"], rolled[t - 1], rolled[(t + 1) % len(rolled)]), rolled[t])
+                    jnp.where(c["first"], across(c, rolled[t - 1], rolled[(t + 1) % len(rolled)]), rolled[t])
                     for t in range(len(rolled))
                 ]
                 return jnp.where(c["edge"], jnp.concatenate(over, 0), turned)
 
             def moved(c, x, before, mask):
-                return (x - c["a"] * (x - before) - c["b"] * (x - beside(c, x))) * mask
+                return (c["keep"] * x + c["a"] * before + c["b"] * beside(c, x)) * mask
+
+            def early(i):
+                c = prepare(i)
+                y1 = moved(c, c["x"][1], c["x"][0], c["halo_mask"])
+                y2 = moved(c, c["x"][2], c["x"][1], c["fore_mask"])
+                y3 = moved(c, c["x"][3], c["x"][2], c["back_mask"])
+                return c, y1, y2, y3
+
+            def late(c, y1, y2, y3):
+                done_ref[c["j"], pl.ds(c["fore"], half, stride=PAIR), :] = moved(c, y2, y1, c["fore_mask"])
+                done_ref[c["j"], pl.ds(c["back"], half, stride=PAIR), :] = moved(c, y3, y2, c["back_mask"])
 
             def some(group, carry):
-                comps = [prepare(group * GROUP + u) for u in range(GROUP)]
-                y1 = [moved(c, c["x"][1], c["x"][0], c["halo_mask"]) for c in comps]
-                y2 = [moved(c, c["x"][2], c["x"][1], c["fore_mask"]) for c in comps]
-                y3 = [moved(c, c["x"][3], c["x"][2], c["back_mask"]) for c in comps]
-                z2 = [moved(c, v, u, c["fore_mask"]) for c, v, u in zip(comps, y2, y1)]
-                z3 = [moved(c, v, u, c["back_mask"]) for c, v, u in zip(comps, y3, y2)]
-                for c, v, u in zip(comps, z2, z3):
-                    done_ref[c["j"], pl.ds(c["fore"], half, stride=PAIR), :] = v
-                    done_ref[c["j"], pl.ds(c["back"], half, stride=PAIR), :] = u
+                held = early(group * GROUP)
+                for u in range(1, GROUP):
+                    following = early(group * GROUP + u)
+                    late(*held)
+                    held = following
+                late(*held)
                 return carry
 
             lax.fori_loop(0, length // GROUP, some, 0)

time: 168 us -> 137 us (0.82)
  the two profiles are of different devices: /device:TPU:19 before, /device:TPU:26 now
where the time goes in v8:
time: 137 us; the launch traced here: 136 us
  starting transfers between devices  64.6 us (47%)
  Pallas kernels  44.4 us (32%)
  waiting for transfers between devices  23.4 us (17%)
  local copies, waits for them, and re-layouts  3.08 us (2%)
    ppermute x3, starting transfers between devices, halo_plan(): sides_in.append(lax.ppermute(message, 'lat', sides))  31.4 us
    ppermute x8, starting transfers between devices, halo_plan(): last = [lax.ppermute(high, 'comp', z_up), lax.ppermute(low, 'comp', z_down)]  21.8 us
    pallas_call x5, Pallas kernels, propagate(): pl.pallas_call(kernel, out_shape=[jax.ShapeDtypeStruct((length, rows, LAN...  20.6 us
    ppermute x8, waiting for transfers between devices, halo_plan(): last = [lax.ppermute(high, 'comp', z_up), lax.ppermute(low, 'comp', z_down)]  11.9 us
    ppermute x3, waiting for transfers between devices, halo_plan(): sides_in.append(lax.ppermute(message, 'lat', sides))  11.5 us
    pallas_call x2, Pallas kernels, quadruplets(): pl.pallas_call(kernel, out_shape=[vmem(((local + 2 * reach) * ND, rows, L...  9.19 us
    pallas_call x3, Pallas kernels, pack_message(): pl.pallas_call(kernel, out_shape=vmem(shape), in_specs=[whole(pltpu.SMEM)...  6.6 us
    pallas_call x2, Pallas kernels, load(): pl.pallas_call(kernel, out_shape=[vmem((size, rows, LANES)) for size in s...  6.17 us
  transfers between devices with their start and end apart: 21, of which 3 were waited for; matrix products, arithmetic and copies ran while one was open for 1% of the time, Pallas kernels for 30%

profile of v8, /device:TPU:26, one launch (start us, length us, event | category | flops | bytes accessed | tf_op | source)
XLA Modules:
  0.0 136.1 jit_solution(17736685637213807096)
XLA Ops:
  0.7 3.0 %load.2 = (f32[65,32,128]{2,1,0:T(8,128)}, f32[80,32,128]{2,1,0:T(8,128)}, f32[1,32,128]{2,1,0:T(8,128)S(1)}) custom-call(f32[288,32,128]{2,1,0:T(8,128)} %bitcast.23, s32[1,32,128]{2,1,0:T(8,128)S(1)} %bitcast.19), custom_call_target="tpu_custom_call" | custom-call | bytes 4718592 | tf_op jit(solution)/shard_map/load/pallas_call | solution.py:167
  5.2 3.1 %load.3 = (f32[64,32,128]{2,1,0:T(8,128)}, f32[80,32,128]{2,1,0:T(8,128)}) custom-call(f32[288,32,128]{2,1,0:T(8,128)} %bitcast.24), custom_call_target="tpu_custom_call" | custom-call | bytes 4718592 | tf_op jit(solution)/shard_map/load/pallas_call | solution.py:167
  9.1 1.7 %collective-permute-start.16 = (f32[64,32,128]{2,1,0:T(8,128)}, f32[64,32,128]{2,1,0:T(8,128)}, u32[]{:S(2)}, u32[]{:S(2)}) collective-permute-start(f32[64,32,128]{2,1,0:T(8,128)} %get-tuple-element.31), channel_id=1, source_target_pairs={{3,6},{4,1},{11,14},{12,9},{19,22},{20,17},{27,30},{28,25}} | collective-permute-start | bytes 3145736 | tf_op jit(solution)/shard_map/ppermute | solution.py:478
  10.9 1.8 %pack_first.1 = f32[66,32,128]{2,1,0:T(8,128)S(1)} custom-call(f32[288]{0:T(512)S(1)} %copy-done.12, s32[2]{0:T(128)S(1)} %pad_add_fusion.place_ref, f32[65,32,128]{2,1,0:T(8,128)} %get-tuple-element.22.own_ref, f32[65,32,128]{2,1,0:T(8,128)} %collective-permute-done.mate_ref), custom_call_target="tpu_custom_call" | custom-call | bytes 3145728 | tf_op jit(solution)/shard_map/pack_first/pallas_call | solution.py:195
  12.7 2.7 %collective-permute-start.1 = (f32[66,32,128]{2,1,0:T(8,128)S(1)}, f32[66,32,128]{2,1,0:T(8,128)S(1)}, u32[]{:S(2)}, u32[]{:S(2)}) collective-permute-start(f32[66,32,128]{2,1,0:T(8,128)S(1)} %pack_first.1), channel_id=1, source_target_pairs={{1,2},{5,6},{2,1},{6,5},{9,10},{13,14},{10,9},{14,13},{17,18},{21,... | collective-permute-start | bytes 3244040 | tf_op jit(solution)/shard_map/ppermute | solution.py:475
  15.4 2.0 %pack_message.4 = f32[80,32,128]{2,1,0:T(8,128)S(1)} custom-call(f32[288]{0:T(512)S(1)} %copy-done.12, s32[2]{0:T(128)S(1)} %pad_add_fusion.place_ref, f32[288,32,128]{2,1,0:T(8,128)} %bitcast.25, f32[80,32,128]{2,1,0:T(8,128)S(1)} %collective-permute-done.11.other_ref), custom_call_target="tpu_custom_call" | custom-call | bytes 3932160 | tf_op jit(solution)/shard_map/pack_message/pallas_call | solution.py:228
  17.4 10.1 %collective-permute-start.12 = (f32[80,32,128]{2,1,0:T(8,128)S(1)}, f32[80,32,128]{2,1,0:T(8,128)S(1)}, u32[]{:S(2)}, u32[]{:S(2)}) collective-permute-start(f32[80,32,128]{2,1,0:T(8,128)S(1)} %pack_message.4), channel_id=1, source_target_pairs={{1,2},{5,6},{2,1},{6,5},{9,10},{13,14},{10,9},{14,13},{17,18},{21,... | collective-permute-start | bytes 3932168 | tf_op jit(solution)/shard_map/ppermute | solution.py:483
  27.6 2.0 %pack_message.3 = f32[80,32,128]{2,1,0:T(8,128)S(1)} custom-call(f32[288]{0:T(512)S(1)} %copy-done.12, s32[2]{0:T(128)S(1)} %pad_add_fusion.place_ref, f32[288,32,128]{2,1,0:T(8,128)} %bitcast.26, f32[80,32,128]{2,1,0:T(8,128)S(1)} %collective-permute-done.4.other_ref), custom_call_target="tpu_custom_call" | custom-call | bytes 3932160 | tf_op jit(solution)/shard_map/pack_message/pallas_call | solution.py:228
  29.6 12.0 %collective-permute-start.5 = (f32[80,32,128]{2,1,0:T(8,128)S(1)}, f32[80,32,128]{2,1,0:T(8,128)S(1)}, u32[]{:S(2)}, u32[]{:S(2)}) collective-permute-start(f32[80,32,128]{2,1,0:T(8,128)S(1)} %pack_message.3), channel_id=1, source_target_pairs={{1,2},{5,6},{2,1},{6,5},{9,10},{13,14},{10,9},{14,13},{17,18},{21,... | collective-permute-start | bytes 3932168 | tf_op jit(solution)/shard_map/ppermute | solution.py:483
  41.6 2.6 %pack_message.5 = f32[64,32,128]{2,1,0:T(8,128)S(1)} custom-call(f32[288]{0:T(512)S(1)} %copy-done.12, s32[2]{0:T(128)S(1)} %pad_add_fusion.place_ref, f32[288,32,128]{2,1,0:T(8,128)} %bitcast.27, f32[64,32,128]{2,1,0:T(8,128)} %collective-permute-done.16.other_ref), custom_call_target="tpu_custom_call" | custom-call | bytes 3145728 | tf_op jit(solution)/shard_map/pack_message/pallas_call | solution.py:228
  44.2 9.3 %collective-permute-start.17 = (f32[64,32,128]{2,1,0:T(8,128)S(1)}, f32[64,32,128]{2,1,0:T(8,128)S(1)}, u32[]{:S(2)}, u32[]{:S(2)}) collective-permute-start(f32[64,32,128]{2,1,0:T(8,128)S(1)} %pack_message.5), channel_id=1, source_target_pairs={{1,2},{5,6},{2,1},{6,5},{9,10},{13,14},{10,9},{14,13},{17,18},{21,... | collective-permute-start | bytes 3145736 | tf_op jit(solution)/shard_map/ppermute | solution.py:483
  54.3 1.4 %collective-permute-start.13 = (f32[80,32,128]{2,1,0:T(8,128)S(1)}, f32[80,32,128]{2,1,0:T(8,128)S(1)}, u32[]{:S(2)}, u32[]{:S(2)}) collective-permute-start(f32[80,32,128]{2,1,0:T(8,128)S(1)} %collective-permute-done.12.side_ref), channel_id=1, source_target_pairs={{5,4},{2,3},{13,12},{10,11},{21,20},{18,19},{29,28},{26,27}} | collective-permute-start | bytes 3932168 | tf_op jit(solution)/shard_map/ppermute | solution.py:484
  55.7 1.6 %collective-permute-done.5.side_ref = f32[80,32,128]{2,1,0:T(8,128)S(1)} collective-permute-done((f32[80,32,128]{2,1,0:T(8,128)S(1)}, f32[80,32,128]{2,1,0:T(8,128)S(1)}, u32[]{:S(2)}, u32[]{:S(2)}) %collective-permute-start.5) | collective-permute-done | bytes 1310752 | tf_op jit(solution)/shard_map/ppermute | solution.py:483
  57.3 1.4 %collective-permute-start.6 = (f32[80,32,128]{2,1,0:T(8,128)S(1)}, f32[80,32,128]{2,1,0:T(8,128)S(1)}, u32[]{:S(2)}, u32[]{:S(2)}) collective-permute-start(f32[80,32,128]{2,1,0:T(8,128)S(1)} %collective-permute-done.5.side_ref), channel_id=1, source_target_pairs={{5,4},{2,3},{13,12},{10,11},{21,20},{18,19},{29,28},{26,27}} | collective-permute-start | bytes 3932168 | tf_op jit(solution)/shard_map/ppermute | solution.py:484
  58.6 9.9 %collective-permute-done.17.side_ref = f32[64,32,128]{2,1,0:T(8,128)S(1)} collective-permute-done((f32[64,32,128]{2,1,0:T(8,128)S(1)}, f32[64,32,128]{2,1,0:T(8,128)S(1)}, u32[]{:S(2)}, u32[]{:S(2)}) %collective-permute-start.17) | collective-permute-done | bytes 1048608 | tf_op jit(solution)/shard_map/ppermute | solution.py:483
  68.5 1.3 collective-permute-start.18
  70.6 3.8 %propagate.6 = (f32[32,32,128]{2,1,0:T(8,128)S(1)}, f32[32,32,128]{2,1,0:T(8,128)S(1)}) custom-call(f32[288]{0:T(512)S(1)} %copy-done.12, f32[288]{0:T(512)S(1)} %copy-done.13, s32[2]{0:T(128)S(1)} %pad_add_fusion.place_ref, f32[3,32,128]{2,1,0:T(8,128)S(1)} %pad_maximum_fusion.mask_ref, f32[288,32,128]{2,1,0:T(8,128)} %bitcast.28, ...), custom_call_target="tpu_custom_call" | custom-call | flops 10485760 | bytes 5242880 | tf_op jit(solution)/shard_map/propagate/pallas_call | solution.py:359
  74.4 2.4 %collective-permute-start.10 = (f32[32,32,128]{2,1,0:T(8,128)S(1)}, f32[32,32,128]{2,1,0:T(8,128)S(1)}, u32[]{:S(2)}, u32[]{:S(2)}) collective-permute-start(f32[32,32,128]{2,1,0:T(8,128)S(1)} %get-tuple-element.26.refs_0_), channel_id=1, source_target_pairs={{8,0},{16,8},{24,16},{9,1},{17,9},{25,17},{10,2},{18,10},{26,18},{... | collective-permute-start | bytes 1572872 | tf_op jit(solution)/shard_map/ppermute | solution.py:498
  76.8 1.3 collective-permute-start.9
  78.1 4.5 %propagate.8 = (f32[32,32,128]{2,1,0:T(8,128)S(1)}, f32[32,32,128]{2,1,0:T(8,128)}) custom-call(f32[288]{0:T(512)S(1)} %copy-done.12, f32[288]{0:T(512)S(1)} %copy-done.13, s32[2]{0:T(128)S(1)} %pad_add_fusion.place_ref, f32[3,32,128]{2,1,0:T(8,128)S(1)} %pad_maximum_fusion.mask_ref, f32[288,32,128]{2,1,0:T(8,128)} %bitcast.29, ...), custom_call_target="tpu_custom_call" | custom-call | flops 10485760 | bytes 5242880 | tf_op jit(solution)/shard_map/propagate/pallas_call | solution.py:359
  82.7 4.6 %collective-permute-start.20 = (f32[32,32,128]{2,1,0:T(8,128)S(1)}, f32[32,32,128]{2,1,0:T(8,128)S(1)}, u32[]{:S(2)}, u32[]{:S(2)}) collective-permute-start(f32[32,32,128]{2,1,0:T(8,128)S(1)} %get-tuple-element.32.refs_8_), channel_id=1, source_target_pairs={{8,0},{16,8},{24,16},{9,1},{17,9},{25,17},{10,2},{18,10},{26,18},{... | collective-permute-start | bytes 1572872 | tf_op jit(solution)/shard_map/ppermute | solution.py:498
  87.3 5.4 %propagate.7 = (f32[40,32,128]{2,1,0:T(8,128)S(1)}, f32[40,32,128]{2,1,0:T(8,128)}) custom-call(f32[288]{0:T(512)S(1)} %copy-done.12, f32[288]{0:T(512)S(1)} %copy-done.13, s32[2]{0:T(128)S(1)} %pad_add_fusion.place_ref, f32[3,32,128]{2,1,0:T(8,128)S(1)} %pad_maximum_fusion.mask_ref, f32[288,32,128]{2,1,0:T(8,128)} %bitcast.30, ...), custom_call_target="tpu_custom_call" | custom-call | flops 13107200 | bytes 6553600 | tf_op jit(solution)/shard_map/propagate/pallas_call | solution.py:359
  92.6 3.2 %collective-permute-start.15 = (f32[40,32,128]{2,1,0:T(8,128)S(1)}, f32[40,32,128]{2,1,0:T(8,128)}, u32[]{:S(2)}, u32[]{:S(2)}) collective-permute-start(f32[40,32,128]{2,1,0:T(8,128)S(1)} %get-tuple-element.29.refs_4_), channel_id=1, source_target_pairs={{8,0},{16,8},{24,16},{9,1},{17,9},{25,17},{10,2},{18,10},{26,18},{... | collective-permute-start | bytes 1966088 | tf_op jit(solution)/shard_map/ppermute | solution.py:498
  95.8 1.3 collective-permute-start.14
  97.1 1.3 collective-permute-start.19
  98.4 3.9 %propagate.5 = (f32[24,32,128]{2,1,0:T(8,128)}, f32[24,32,128]{2,1,0:T(8,128)}) custom-call(f32[288]{0:T(512)S(1)} %copy-done.12, f32[288]{0:T(512)S(1)} %copy-done.13, s32[2]{0:T(128)S(1)} %pad_add_fusion.place_ref, f32[3,32,128]{2,1,0:T(8,128)S(1)} %pad_maximum_fusion.mask_ref, f32[288,32,128]{2,1,0:T(8,128)} %bitcast.31, ...), custom_call_target="tpu_custom_call" | custom-call | flops 7864320 | bytes 3932160 | tf_op jit(solution)/shard_map/propagate/pallas_call | solution.py:359
  103.1 1.3 collective-permute-start.7
  105.2 6.6 %collective-permute-start.8 = (f32[24,32,128]{2,1,0:T(8,128)}, f32[24,32,128]{2,1,0:T(8,128)}, u32[]{:S(2)}, u32[]{:S(2)}) collective-permute-start(f32[24,32,128]{2,1,0:T(8,128)} %get-tuple-element.25.refs_12_), channel_id=1, source_target_pairs={{8,0},{16,8},{24,16},{9,1},{17,9},{25,17},{10,2},{18,10},{26,18},{... | collective-permute-start | bytes 1179656 | tf_op jit(solution)/shard_map/ppermute | solution.py:498
  111.8 3.1 %propagate.9.refs_14_ = f32[32,32,128]{2,1,0:T(8,128)S(1)} custom-call(f32[288]{0:T(512)S(1)} %copy-done.12, f32[288]{0:T(512)S(1)} %copy-done.13, s32[2]{0:T(128)S(1)} %pad_add_fusion.place_ref, f32[3,32,128]{2,1,0:T(8,128)S(1)} %pad_maximum_fusion.mask_ref, f32[288,32,128]{2,1,0:T(8,128)} %bitcast.32, f32[288,32,128]{2,1,0:T(8,128)} %collective-permute-done.3.mate_hbm, ...), custom_call_target="tpu_custom_call" | custom-call | flops 5242880 | bytes 2621440 | tf_op jit(solution)/shard_map/propagate/pallas_call | solution.py:359
  114.9 11.9 %collective-permute-done.19.refs_10_ = f32[32,32,128]{2,1,0:T(8,128)} collective-permute-done((f32[32,32,128]{2,1,0:T(8,128)}, f32[32,32,128]{2,1,0:T(8,128)}, u32[]{:S(2)}, u32[]{:S(2)}) %collective-permute-start.19) | collective-permute-done | bytes 524320 | tf_op jit(solution)/shard_map/ppermute | solution.py:498
  126.9 6.1 %quadruplets.2 = (f32[544,32,128]{2,1,0:T(8,128)S(1)}, f32[288,32,128]{2,1,0:T(8,128)}) custom-call(f32[1152]{0:T(1024)S(1)} %copy-done.14, s32[2,4]{1,0:T(2,128)S(1)} %bitcast.20, s32[1]{0:T(128)} %bitcast.1.first_ref, f32[32,32,128]{2,1,0:T(8,128)S(1)} %copy-done.1, f32[32,32,128]{2,1,0:T(8,128)S(1)} %copy-done.3, f32[32,32,128]{2,1,0:T(8,128)S(1)} %copy-done.7, ...), custom_call_target="tpu_custom_call" | custom-call | flops 13762560 | bytes 22020096 | tf_op jit(solution)/shard_map/quadruplets/pallas_call | solution.py:426
  133.0 3.1 %quadruplets.3 = (f32[544,32,128]{2,1,0:T(8,128)S(1)}, f32[288,32,128]{2,1,0:T(8,128)}) custom-call(f32[1152]{0:T(1024)S(1)} %copy-done.14, s32[2,4]{1,0:T(2,128)S(1)} %bitcast.21, s32[1]{0:T(128)} %bitcast.1.first_ref, f32[24,32,128]{2,1,0:T(8,128)} %collective-permute-done.7.refs_0_, ...), custom_call_target="tpu_custom_call", output_to_operand_aliasing={{0}: (5, {}), {1}: (6, {})} | custom-call | flops 3932160 | bytes 6291456 | tf_op jit(solution)/shard_map/quadruplets/pallas_call | solution.py:426
  (61 shorter events, 6.1 us)
Async XLA Ops:
  0.0 70.6 %collective-permute-start.3 = (f32[288,32,128]{2,1,0:T(8,128)}, f32[288,32,128]{2,1,0:T(8,128)}, u32[]{:S(2)}, u32[]{:S(2)}) collective-permute-start(f32[288,32,128]{2,1,0:T(8,128)} %bitcast.22), channel_id=1, source_target_pairs={{0,1},{1,0},{2,3},{3,2},{4,5},{5,4},{6,7},{7,6},{8,9},{9,8},{10,11... | collective-permute-start | bytes 14155784 | tf_op jit(solution)/shard_map/ppermute | solution.py:479
  3.8 7.1 %collective-permute-start = (f32[65,32,128]{2,1,0:T(8,128)}, f32[65,32,128]{2,1,0:T(8,128)}, u32[]{:S(2)}, u32[]{:S(2)}) collective-permute-start(f32[65,32,128]{2,1,0:T(8,128)} %get-tuple-element.22.own_ref), channel_id=1, source_target_pairs={{0,1},{1,0},{2,3},{3,2},{4,5},{5,4},{6,7},{7,6},{8,9},{9,8},{10,11... | collective-permute-start | bytes 3194888 | tf_op jit(solution)/shard_map/ppermute | solution.py:473
  4.3 11.1 %collective-permute-start.11 = (f32[80,32,128]{2,1,0:T(8,128)}, f32[80,32,128]{2,1,0:T(8,128)S(1)}, u32[]{:S(2)}, u32[]{:S(2)}) collective-permute-start(f32[80,32,128]{2,1,0:T(8,128)} %get-tuple-element.28), channel_id=1, source_target_pairs={{3,6},{4,1},{11,14},{12,9},{19,22},{20,17},{27,30},{28,25}} | collective-permute-start | bytes 3932168 | tf_op jit(solution)/shard_map/ppermute | solution.py:474
  8.4 19.2 %collective-permute-start.4 = (f32[80,32,128]{2,1,0:T(8,128)}, f32[80,32,128]{2,1,0:T(8,128)S(1)}, u32[]{:S(2)}, u32[]{:S(2)}) collective-permute-start(f32[80,32,128]{2,1,0:T(8,128)} %get-tuple-element.23), channel_id=1, source_target_pairs={{3,6},{4,1},{11,14},{12,9},{19,22},{20,17},{27,30},{28,25}} | collective-permute-start | bytes 3932168 | tf_op jit(solution)/shard_map/ppermute | solution.py:478
  9.1 32.5 %collective-permute-start.16 = (f32[64,32,128]{2,1,0:T(8,128)}, f32[64,32,128]{2,1,0:T(8,128)}, u32[]{:S(2)}, u32[]{:S(2)}) collective-permute-start(f32[64,32,128]{2,1,0:T(8,128)} %get-tuple-element.31), channel_id=1, source_target_pairs={{3,6},{4,1},{11,14},{12,9},{19,22},{20,17},{27,30},{28,25}} | collective-permute-start | bytes 3145736 | tf_op jit(solution)/shard_map/ppermute | solution.py:478
  12.7 40.8 %collective-permute-start.1 = (f32[66,32,128]{2,1,0:T(8,128)S(1)}, f32[66,32,128]{2,1,0:T(8,128)S(1)}, u32[]{:S(2)}, u32[]{:S(2)}) collective-permute-start(f32[66,32,128]{2,1,0:T(8,128)S(1)} %pack_first.1), channel_id=1, source_target_pairs={{1,2},{5,6},{2,1},{6,5},{9,10},{13,14},{10,9},{14,13},{17,18},{21,... | collective-permute-start | bytes 3244040 | tf_op jit(solution)/shard_map/ppermute | solution.py:475
  17.4 36.8 %collective-permute-start.12 = (f32[80,32,128]{2,1,0:T(8,128)S(1)}, f32[80,32,128]{2,1,0:T(8,128)S(1)}, u32[]{:S(2)}, u32[]{:S(2)}) collective-permute-start(f32[80,32,128]{2,1,0:T(8,128)S(1)} %pack_message.4), channel_id=1, source_target_pairs={{1,2},{5,6},{2,1},{6,5},{9,10},{13,14},{10,9},{14,13},{17,18},{21,... | collective-permute-start | bytes 3932168 | tf_op jit(solution)/shard_map/ppermute | solution.py:483
  29.6 41.0 %copy-start.13 = (f32[288]{0:T(512)S(1)}, f32[288]{0:T(512)}, u32[]{:S(2)}) copy-start(f32[288]{0:T(512)} %b_ref.9) | copy-start | bytes 3460
  29.6 27.6 %collective-permute-start.5 = (f32[80,32,128]{2,1,0:T(8,128)S(1)}, f32[80,32,128]{2,1,0:T(8,128)S(1)}, u32[]{:S(2)}, u32[]{:S(2)}) collective-permute-start(f32[80,32,128]{2,1,0:T(8,128)S(1)} %pack_message.3), channel_id=1, source_target_pairs={{1,2},{5,6},{2,1},{6,5},{9,10},{13,14},{10,9},{14,13},{17,18},{21,... | collective-permute-start | bytes 3932168 | tf_op jit(solution)/shard_map/ppermute | solution.py:483
  44.2 24.3 %collective-permute-start.17 = (f32[64,32,128]{2,1,0:T(8,128)S(1)}, f32[64,32,128]{2,1,0:T(8,128)S(1)}, u32[]{:S(2)}, u32[]{:S(2)}) collective-permute-start(f32[64,32,128]{2,1,0:T(8,128)S(1)} %pack_message.5), channel_id=1, source_target_pairs={{1,2},{5,6},{2,1},{6,5},{9,10},{13,14},{10,9},{14,13},{17,18},{21,... | collective-permute-start | bytes 3145736 | tf_op jit(solution)/shard_map/ppermute | solution.py:483
  53.5 17.0 %collective-permute-start.2 = (f32[66,32,128]{2,1,0:T(8,128)S(1)}, f32[66,32,128]{2,1,0:T(8,128)S(1)}, u32[]{:S(2)}, u32[]{:S(2)}) collective-permute-start(f32[66,32,128]{2,1,0:T(8,128)S(1)} %collective-permute-done.1.side_ref), channel_id=1, source_target_pairs={{1,4},{6,3},{9,12},{14,11},{17,20},{22,19},{25,28},{30,27}} | collective-permute-start | bytes 3244040 | tf_op jit(solution)/shard_map/ppermute | solution.py:476
  54.3 33.0 %collective-permute-start.13 = (f32[80,32,128]{2,1,0:T(8,128)S(1)}, f32[80,32,128]{2,1,0:T(8,128)S(1)}, u32[]{:S(2)}, u32[]{:S(2)}) collective-permute-start(f32[80,32,128]{2,1,0:T(8,128)S(1)} %collective-permute-done.12.side_ref), channel_id=1, source_target_pairs={{5,4},{2,3},{13,12},{10,11},{21,20},{18,19},{29,28},{26,27}} | collective-permute-start | bytes 3932168 | tf_op jit(solution)/shard_map/ppermute | solution.py:484
  57.3 38.5 %collective-permute-start.6 = (f32[80,32,128]{2,1,0:T(8,128)S(1)}, f32[80,32,128]{2,1,0:T(8,128)S(1)}, u32[]{:S(2)}, u32[]{:S(2)}) collective-permute-start(f32[80,32,128]{2,1,0:T(8,128)S(1)} %collective-permute-done.5.side_ref), channel_id=1, source_target_pairs={{5,4},{2,3},{13,12},{10,11},{21,20},{18,19},{29,28},{26,27}} | collective-permute-start | bytes 3932168 | tf_op jit(solution)/shard_map/ppermute | solution.py:484
  68.5 9.6 %collective-permute-start.18 = (f32[64,32,128]{2,1,0:T(8,128)S(1)}, f32[64,32,128]{2,1,0:T(8,128)S(1)}, u32[]{:S(2)}, u32[]{:S(2)}) collective-permute-start(f32[64,32,128]{2,1,0:T(8,128)S(1)} %collective-permute-done.17.side_ref), channel_id=1, source_target_pairs={{5,4},{2,3},{13,12},{10,11},{21,20},{18,19},{29,28},{26,27}} | collective-permute-start | bytes 3145736 | tf_op jit(solution)/shard_map/ppermute | solution.py:484
  74.4 8.2 %copy-start = (f32[32,32,128]{2,1,0:T(8,128)}, f32[32,32,128]{2,1,0:T(8,128)S(1)}, u32[]{:S(2)}) copy-start(f32[32,32,128]{2,1,0:T(8,128)S(1)} %get-tuple-element.26.refs_0_) | copy-start | bytes 1572868
  74.4 22.7 %collective-permute-start.10 = (f32[32,32,128]{2,1,0:T(8,128)S(1)}, f32[32,32,128]{2,1,0:T(8,128)S(1)}, u32[]{:S(2)}, u32[]{:S(2)}) collective-permute-start(f32[32,32,128]{2,1,0:T(8,128)S(1)} %get-tuple-element.26.refs_0_), channel_id=1, source_target_pairs={{8,0},{16,8},{24,16},{9,1},{17,9},{25,17},{10,2},{18,10},{26,18},{... | collective-permute-start | bytes 1572872 | tf_op jit(solution)/shard_map/ppermute | solution.py:498
  76.8 25.5 %collective-permute-start.9 = (f32[32,32,128]{2,1,0:T(8,128)S(1)}, f32[32,32,128]{2,1,0:T(8,128)S(1)}, u32[]{:S(2)}, u32[]{:S(2)}) collective-permute-start(f32[32,32,128]{2,1,0:T(8,128)S(1)} %get-tuple-element.27.refs_1_), channel_id=1, source_target_pairs={{0,8},{8,16},{16,24},{1,9},{9,17},{17,25},{2,10},{10,18},{18,26},{... | collective-permute-start | bytes 1572872 | tf_op jit(solution)/shard_map/ppermute | solution.py:498
  82.7 10.0 %copy-start.8 = (f32[32,32,128]{2,1,0:T(8,128)}, f32[32,32,128]{2,1,0:T(8,128)S(1)}, u32[]{:S(2)}) copy-start(f32[32,32,128]{2,1,0:T(8,128)S(1)} %get-tuple-element.32.refs_8_) | copy-start | bytes 1572868
  82.7 21.7 %collective-permute-start.20 = (f32[32,32,128]{2,1,0:T(8,128)S(1)}, f32[32,32,128]{2,1,0:T(8,128)S(1)}, u32[]{:S(2)}, u32[]{:S(2)}) collective-permute-start(f32[32,32,128]{2,1,0:T(8,128)S(1)} %get-tuple-element.32.refs_8_), channel_id=1, source_target_pairs={{8,0},{16,8},{24,16},{9,1},{17,9},{25,17},{10,2},{18,10},{26,18},{... | collective-permute-start | bytes 1572872 | tf_op jit(solution)/shard_map/ppermute | solution.py:498
  92.6 34.2 %collective-permute-start.15 = (f32[40,32,128]{2,1,0:T(8,128)S(1)}, f32[40,32,128]{2,1,0:T(8,128)}, u32[]{:S(2)}, u32[]{:S(2)}) collective-permute-start(f32[40,32,128]{2,1,0:T(8,128)S(1)} %get-tuple-element.29.refs_4_), channel_id=1, source_target_pairs={{8,0},{16,8},{24,16},{9,1},{17,9},{25,17},{10,2},{18,10},{26,18},{... | collective-permute-start | bytes 1966088 | tf_op jit(solution)/shard_map/ppermute | solution.py:498
  95.8 31.0 %collective-permute-start.14 = (f32[40,32,128]{2,1,0:T(8,128)}, f32[40,32,128]{2,1,0:T(8,128)}, u32[]{:S(2)}, u32[]{:S(2)}) collective-permute-start(f32[40,32,128]{2,1,0:T(8,128)} %get-tuple-element.30.refs_5_), channel_id=1, source_target_pairs={{0,8},{8,16},{16,24},{1,9},{9,17},{17,25},{2,10},{10,18},{18,26},{... | collective-permute-start | bytes 1966088 | tf_op jit(solution)/shard_map/ppermute | solution.py:498
  97.1 29.7 %collective-permute-start.19 = (f32[32,32,128]{2,1,0:T(8,128)}, f32[32,32,128]{2,1,0:T(8,128)}, u32[]{:S(2)}, u32[]{:S(2)}) collective-permute-start(f32[32,32,128]{2,1,0:T(8,128)} %get-tuple-element.33.refs_9_), channel_id=1, source_target_pairs={{0,8},{8,16},{16,24},{1,9},{9,17},{17,25},{2,10},{10,18},{18,26},{... | collective-permute-start | bytes 1572872 | tf_op jit(solution)/shard_map/ppermute | solution.py:498
  103.1 29.9 %collective-permute-start.7 = (f32[24,32,128]{2,1,0:T(8,128)}, f32[24,32,128]{2,1,0:T(8,128)}, u32[]{:S(2)}, u32[]{:S(2)}) collective-permute-start(f32[24,32,128]{2,1,0:T(8,128)} %get-tuple-element.24.refs_13_), channel_id=1, source_target_pairs={{0,8},{8,16},{16,24},{1,9},{9,17},{17,25},{2,10},{10,18},{18,26},{... | collective-permute-start | bytes 1179656 | tf_op jit(solution)/shard_map/ppermute | solution.py:498
  105.2 27.8 %collective-permute-start.8 = (f32[24,32,128]{2,1,0:T(8,128)}, f32[24,32,128]{2,1,0:T(8,128)}, u32[]{:S(2)}, u32[]{:S(2)}) collective-permute-start(f32[24,32,128]{2,1,0:T(8,128)} %get-tuple-element.25.refs_12_), channel_id=1, source_target_pairs={{8,0},{16,8},{24,16},{9,1},{17,9},{25,17},{10,2},{18,10},{26,18},{... | collective-permute-start | bytes 1179656 | tf_op jit(solution)/shard_map/ppermute | solution.py:498
  111.8 15.1 %copy-start.1 = (f32[32,32,128]{2,1,0:T(8,128)S(1)}, f32[32,32,128]{2,1,0:T(8,128)}, u32[]{:S(2)}) copy-start(f32[32,32,128]{2,1,0:T(8,128)} %copy-done) | copy-start | bytes 1572868
  111.8 15.1 %copy-start.3 = (f32[32,32,128]{2,1,0:T(8,128)S(1)}, f32[32,32,128]{2,1,0:T(8,128)}, u32[]{:S(2)}) copy-start(f32[32,32,128]{2,1,0:T(8,128)} %copy-done.2) | copy-start | bytes 1572868
  111.8 15.1 %copy-start.5 = (f32[32,32,128]{2,1,0:T(8,128)S(1)}, f32[32,32,128]{2,1,0:T(8,128)}, u32[]{:S(2)}) copy-start(f32[32,32,128]{2,1,0:T(8,128)} %copy-done.4) | copy-start | bytes 1572868
  111.8 15.1 %copy-start.7 = (f32[32,32,128]{2,1,0:T(8,128)S(1)}, f32[32,32,128]{2,1,0:T(8,128)}, u32[]{:S(2)}) copy-start(f32[32,32,128]{2,1,0:T(8,128)} %copy-done.6) | copy-start | bytes 1572868
  111.8 15.1 %copy-start.9 = (f32[32,32,128]{2,1,0:T(8,128)S(1)}, f32[32,32,128]{2,1,0:T(8,128)}, u32[]{:S(2)}) copy-start(f32[32,32,128]{2,1,0:T(8,128)} %copy-done.8) | copy-start | bytes 1572868
  111.8 15.1 %copy-start.11 = (f32[32,32,128]{2,1,0:T(8,128)S(1)}, f32[32,32,128]{2,1,0:T(8,128)}, u32[]{:S(2)}) copy-start(f32[32,32,128]{2,1,0:T(8,128)} %copy-done.10) | copy-start | bytes 1572868
  111.8 15.1 %copy-start.14 = (f32[1152]{0:T(1024)S(1)}, f32[1152]{0:T(1024)}, u32[]{:S(2)}) copy-start(f32[1152]{0:T(1024)} %strength_ref.3) | copy-start | bytes 13828
  111.8 15.1 %copy-start.16 = (s32[4,2]{0,1:T(2,128)S(1)}, s32[4,2]{0,1:T(2,128)}, u32[]{:S(2)}) copy-start(s32[4,2]{0,1:T(2,128)} %param.11) | copy-start | bytes 100
  (6 other events, 22.3 us)

commit v9 on v8

--- a/solution.py
+++ b/solution.py
@@ -384,14 +384,15 @@
             pltpu.make_async_copy(part_refs[n], held_ref.at[pl.ds(place, parts[n].shape[0])], part_sems.at[n])
             for n, place in enumerate(places)
         ]
-        for one in arrivals:
-            one.start()
-        for one in arrivals:
-            one.wait()
+        waiting = sorted(range(count), key=lambda n: places[n])
+        for n in waiting:
+            arrivals[n].start()
         base = first_ref[0]
         turns = [shift_ref[1, q] for q in range(NQ)]
         copies = []
         for n, f in enumerate(freqs):
+            while waiting and places[waiting[0]] < (f + 2 * reach + 1) * ND:
+                arrivals[waiting.pop(0)].wait()
             bases = [(f + reach + shift_ref[0, q]) * ND for q in range(NQ)]
 
             def some(group, carry):
@@ -413,6 +414,8 @@
                 pltpu.make_async_copy(done.at[pl.ds(n * ND, ND)], out_ref.at[pl.ds(f * ND, ND)], sems.at[n])
             )
             copies[-1].start()
+        for n in waiting:
+            arrivals[n].wait()
         for one in copies:
             one.wait()
 

time: 137 us -> 137 us (level)
  the two profiles are of different devices: /device:TPU:26 before, /device:TPU:29 now
where the time goes in v9:
time: 137 us; the launch traced here: 136 us
  starting transfers between devices  64.7 us (47%)
  Pallas kernels  43.6 us (32%)
  waiting for transfers between devices  23.6 us (17%)
  local copies, waits for them, and re-layouts  3.09 us (2%)
    ppermute x3, starting transfers between devices, halo_plan(): sides_in.append(lax.ppermute(message, 'lat', sides))  31.4 us
    pallas_call x5, Pallas kernels, propagate(): pl.pallas_call(kernel, out_shape=[jax.ShapeDtypeStruct((length, rows, LAN...  20.6 us
    ppermute x8, starting transfers between devices, halo_plan(): last = [lax.ppermute(high, 'comp', z_up), lax.ppermute(low, 'comp', z_down)]  20.2 us
    ppermute x8, waiting for transfers between devices, halo_plan(): last = [lax.ppermute(high, 'comp', z_up), lax.ppermute(low, 'comp', z_down)]  12.4 us
    ppermute x3, waiting for transfers between devices, halo_plan(): sides_in.append(lax.ppermute(message, 'lat', sides))  11.1 us
    pallas_call x2, Pallas kernels, quadruplets(): pl.pallas_call(kernel, out_shape=[vmem(((local + 2 * reach) * ND, rows, L...  8.42 us
    pallas_call x3, Pallas kernels, pack_message(): pl.pallas_call(kernel, out_shape=vmem(shape), in_specs=[whole(pltpu.SMEM)...  6.6 us
    pallas_call x2, Pallas kernels, load(): pl.pallas_call(kernel, out_shape=[vmem((size, rows, LANES)) for size in s...  6.17 us
  transfers between devices with their start and end apart: 21, of which 4 were waited for; matrix products, arithmetic and copies ran while one was open for 1% of the time, Pallas kernels for 30%

profile of v9, /device:TPU:29, one launch (start us, length us, event | category | flops | bytes accessed | tf_op | source)
XLA Modules:
  0.0 135.5 jit_solution(17473361379818881629)
XLA Ops:
  1.4 3.0 %load.2 = (f32[65,32,128]{2,1,0:T(8,128)}, f32[80,32,128]{2,1,0:T(8,128)}, f32[1,32,128]{2,1,0:T(8,128)S(1)}) custom-call(f32[288,32,128]{2,1,0:T(8,128)} %bitcast.23, s32[1,32,128]{2,1,0:T(8,128)S(1)} %bitcast.19), custom_call_target="tpu_custom_call" | custom-call | bytes 4718592 | tf_op jit(solution)/shard_map/load/pallas_call | solution.py:167
  5.3 3.1 %load.3 = (f32[64,32,128]{2,1,0:T(8,128)}, f32[80,32,128]{2,1,0:T(8,128)}) custom-call(f32[288,32,128]{2,1,0:T(8,128)} %bitcast.24), custom_call_target="tpu_custom_call" | custom-call | bytes 4718592 | tf_op jit(solution)/shard_map/load/pallas_call | solution.py:167
  9.2 1.7 %collective-permute-start.16 = (f32[64,32,128]{2,1,0:T(8,128)}, f32[64,32,128]{2,1,0:T(8,128)}, u32[]{:S(2)}, u32[]{:S(2)}) collective-permute-start(f32[64,32,128]{2,1,0:T(8,128)} %get-tuple-element.31), channel_id=1, source_target_pairs={{3,6},{4,1},{11,14},{12,9},{19,22},{20,17},{27,30},{28,25}} | collective-permute-start | bytes 3145736 | tf_op jit(solution)/shard_map/ppermute | solution.py:481
  10.9 1.8 %pack_first.1 = f32[66,32,128]{2,1,0:T(8,128)S(1)} custom-call(f32[288]{0:T(512)S(1)} %copy-done.12, s32[2]{0:T(128)S(1)} %pad_add_fusion.place_ref, f32[65,32,128]{2,1,0:T(8,128)} %get-tuple-element.22.own_ref, f32[65,32,128]{2,1,0:T(8,128)} %collective-permute-done.mate_ref), custom_call_target="tpu_custom_call" | custom-call | bytes 3145728 | tf_op jit(solution)/shard_map/pack_first/pallas_call | solution.py:195
  12.8 4.4 %collective-permute-start.1 = (f32[66,32,128]{2,1,0:T(8,128)S(1)}, f32[66,32,128]{2,1,0:T(8,128)S(1)}, u32[]{:S(2)}, u32[]{:S(2)}) collective-permute-start(f32[66,32,128]{2,1,0:T(8,128)S(1)} %pack_first.1), channel_id=1, source_target_pairs={{1,2},{5,6},{2,1},{6,5},{9,10},{13,14},{10,9},{14,13},{17,18},{21,... | collective-permute-start | bytes 3244040 | tf_op jit(solution)/shard_map/ppermute | solution.py:478
  17.1 2.0 %pack_message.4 = f32[80,32,128]{2,1,0:T(8,128)S(1)} custom-call(f32[288]{0:T(512)S(1)} %copy-done.12, s32[2]{0:T(128)S(1)} %pad_add_fusion.place_ref, f32[288,32,128]{2,1,0:T(8,128)} %bitcast.25, f32[80,32,128]{2,1,0:T(8,128)S(1)} %collective-permute-done.11.other_ref), custom_call_target="tpu_custom_call" | custom-call | bytes 3932160 | tf_op jit(solution)/shard_map/pack_message/pallas_call | solution.py:228
  19.2 10.1 %collective-permute-start.12 = (f32[80,32,128]{2,1,0:T(8,128)S(1)}, f32[80,32,128]{2,1,0:T(8,128)S(1)}, u32[]{:S(2)}, u32[]{:S(2)}) collective-permute-start(f32[80,32,128]{2,1,0:T(8,128)S(1)} %pack_message.4), channel_id=1, source_target_pairs={{1,2},{5,6},{2,1},{6,5},{9,10},{13,14},{10,9},{14,13},{17,18},{21,... | collective-permute-start | bytes 3932168 | tf_op jit(solution)/shard_map/ppermute | solution.py:486
  29.3 2.0 %pack_message.3 = f32[80,32,128]{2,1,0:T(8,128)S(1)} custom-call(f32[288]{0:T(512)S(1)} %copy-done.12, s32[2]{0:T(128)S(1)} %pad_add_fusion.place_ref, f32[288,32,128]{2,1,0:T(8,128)} %bitcast.26, f32[80,32,128]{2,1,0:T(8,128)S(1)} %collective-permute-done.4.other_ref), custom_call_target="tpu_custom_call" | custom-call | bytes 3932160 | tf_op jit(solution)/shard_map/pack_message/pallas_call | solution.py:228
  31.3 12.0 %collective-permute-start.5 = (f32[80,32,128]{2,1,0:T(8,128)S(1)}, f32[80,32,128]{2,1,0:T(8,128)S(1)}, u32[]{:S(2)}, u32[]{:S(2)}) collective-permute-start(f32[80,32,128]{2,1,0:T(8,128)S(1)} %pack_message.3), channel_id=1, source_target_pairs={{1,2},{5,6},{2,1},{6,5},{9,10},{13,14},{10,9},{14,13},{17,18},{21,... | collective-permute-start | bytes 3932168 | tf_op jit(solution)/shard_map/ppermute | solution.py:486
  43.4 2.6 %pack_message.5 = f32[64,32,128]{2,1,0:T(8,128)S(1)} custom-call(f32[288]{0:T(512)S(1)} %copy-done.12, s32[2]{0:T(128)S(1)} %pad_add_fusion.place_ref, f32[288,32,128]{2,1,0:T(8,128)} %bitcast.27, f32[64,32,128]{2,1,0:T(8,128)} %collective-permute-done.16.other_ref), custom_call_target="tpu_custom_call" | custom-call | bytes 3145728 | tf_op jit(solution)/shard_map/pack_message/pallas_call | solution.py:228
  45.9 9.3 %collective-permute-start.17 = (f32[64,32,128]{2,1,0:T(8,128)S(1)}, f32[64,32,128]{2,1,0:T(8,128)S(1)}, u32[]{:S(2)}, u32[]{:S(2)}) collective-permute-start(f32[64,32,128]{2,1,0:T(8,128)S(1)} %pack_message.5), channel_id=1, source_target_pairs={{1,2},{5,6},{2,1},{6,5},{9,10},{13,14},{10,9},{14,13},{17,18},{21,... | collective-permute-start | bytes 3145736 | tf_op jit(solution)/shard_map/ppermute | solution.py:486
  56.0 1.4 %collective-permute-start.13 = (f32[80,32,128]{2,1,0:T(8,128)S(1)}, f32[80,32,128]{2,1,0:T(8,128)S(1)}, u32[]{:S(2)}, u32[]{:S(2)}) collective-permute-start(f32[80,32,128]{2,1,0:T(8,128)S(1)} %collective-permute-done.12.side_ref), channel_id=1, source_target_pairs={{5,4},{2,3},{13,12},{10,11},{21,20},{18,19},{29,28},{26,27}} | collective-permute-start | bytes 3932168 | tf_op jit(solution)/shard_map/ppermute | solution.py:487
  57.4 1.5 %collective-permute-done.5.side_ref = f32[80,32,128]{2,1,0:T(8,128)S(1)} collective-permute-done((f32[80,32,128]{2,1,0:T(8,128)S(1)}, f32[80,32,128]{2,1,0:T(8,128)S(1)}, u32[]{:S(2)}, u32[]{:S(2)}) %collective-permute-start.5) | collective-permute-done | bytes 1310752 | tf_op jit(solution)/shard_map/ppermute | solution.py:486
  58.9 1.4 %collective-permute-start.6 = (f32[80,32,128]{2,1,0:T(8,128)S(1)}, f32[80,32,128]{2,1,0:T(8,128)S(1)}, u32[]{:S(2)}, u32[]{:S(2)}) collective-permute-start(f32[80,32,128]{2,1,0:T(8,128)S(1)} %collective-permute-done.5.side_ref), channel_id=1, source_target_pairs={{5,4},{2,3},{13,12},{10,11},{21,20},{18,19},{29,28},{26,27}} | collective-permute-start | bytes 3932168 | tf_op jit(solution)/shard_map/ppermute | solution.py:487
  60.3 9.6 %collective-permute-done.17.side_ref = f32[64,32,128]{2,1,0:T(8,128)S(1)} collective-permute-done((f32[64,32,128]{2,1,0:T(8,128)S(1)}, f32[64,32,128]{2,1,0:T(8,128)S(1)}, u32[]{:S(2)}, u32[]{:S(2)}) %collective-permute-start.17) | collective-permute-done | bytes 1048608 | tf_op jit(solution)/shard_map/ppermute | solution.py:486
  69.9 1.3 collective-permute-start.18
  72.0 3.8 %propagate.6 = (f32[32,32,128]{2,1,0:T(8,128)S(1)}, f32[32,32,128]{2,1,0:T(8,128)S(1)}) custom-call(f32[288]{0:T(512)S(1)} %copy-done.12, f32[288]{0:T(512)S(1)} %copy-done.13, s32[2]{0:T(128)S(1)} %pad_add_fusion.place_ref, f32[3,32,128]{2,1,0:T(8,128)S(1)} %pad_maximum_fusion.mask_ref, f32[288,32,128]{2,1,0:T(8,128)} %bitcast.28, ...), custom_call_target="tpu_custom_call" | custom-call | flops 10485760 | bytes 5242880 | tf_op jit(solution)/shard_map/propagate/pallas_call | solution.py:359
  75.8 2.1 %collective-permute-start.10 = (f32[32,32,128]{2,1,0:T(8,128)S(1)}, f32[32,32,128]{2,1,0:T(8,128)S(1)}, u32[]{:S(2)}, u32[]{:S(2)}) collective-permute-start(f32[32,32,128]{2,1,0:T(8,128)S(1)} %get-tuple-element.26.refs_0_), channel_id=1, source_target_pairs={{8,0},{16,8},{24,16},{9,1},{17,9},{25,17},{10,2},{18,10},{26,18},{... | collective-permute-start | bytes 1572872 | tf_op jit(solution)/shard_map/ppermute | solution.py:501
  77.9 1.3 collective-permute-start.9
  79.2 4.5 %propagate.8 = (f32[32,32,128]{2,1,0:T(8,128)S(1)}, f32[32,32,128]{2,1,0:T(8,128)}) custom-call(f32[288]{0:T(512)S(1)} %copy-done.12, f32[288]{0:T(512)S(1)} %copy-done.13, s32[2]{0:T(128)S(1)} %pad_add_fusion.place_ref, f32[3,32,128]{2,1,0:T(8,128)S(1)} %pad_maximum_fusion.mask_ref, f32[288,32,128]{2,1,0:T(8,128)} %bitcast.29, ...), custom_call_target="tpu_custom_call" | custom-call | flops 10485760 | bytes 5242880 | tf_op jit(solution)/shard_map/propagate/pallas_call | solution.py:359
  83.8 4.0 %collective-permute-start.20 = (f32[32,32,128]{2,1,0:T(8,128)S(1)}, f32[32,32,128]{2,1,0:T(8,128)S(1)}, u32[]{:S(2)}, u32[]{:S(2)}) collective-permute-start(f32[32,32,128]{2,1,0:T(8,128)S(1)} %get-tuple-element.32.refs_8_), channel_id=1, source_target_pairs={{8,0},{16,8},{24,16},{9,1},{17,9},{25,17},{10,2},{18,10},{26,18},{... | collective-permute-start | bytes 1572872 | tf_op jit(solution)/shard_map/ppermute | solution.py:501
  87.8 5.4 %propagate.7 = (f32[40,32,128]{2,1,0:T(8,128)S(1)}, f32[40,32,128]{2,1,0:T(8,128)}) custom-call(f32[288]{0:T(512)S(1)} %copy-done.12, f32[288]{0:T(512)S(1)} %copy-done.13, s32[2]{0:T(128)S(1)} %pad_add_fusion.place_ref, f32[3,32,128]{2,1,0:T(8,128)S(1)} %pad_maximum_fusion.mask_ref, f32[288,32,128]{2,1,0:T(8,128)} %bitcast.30, ...), custom_call_target="tpu_custom_call" | custom-call | flops 13107200 | bytes 6553600 | tf_op jit(solution)/shard_map/propagate/pallas_call | solution.py:359
  93.2 2.9 %collective-permute-start.15 = (f32[40,32,128]{2,1,0:T(8,128)S(1)}, f32[40,32,128]{2,1,0:T(8,128)}, u32[]{:S(2)}, u32[]{:S(2)}) collective-permute-start(f32[40,32,128]{2,1,0:T(8,128)S(1)} %get-tuple-element.29.refs_4_), channel_id=1, source_target_pairs={{8,0},{16,8},{24,16},{9,1},{17,9},{25,17},{10,2},{18,10},{26,18},{... | collective-permute-start | bytes 1966088 | tf_op jit(solution)/shard_map/ppermute | solution.py:501
  96.1 1.3 collective-permute-start.14
  97.4 1.3 collective-permute-start.19
  98.7 3.9 %propagate.5 = (f32[24,32,128]{2,1,0:T(8,128)}, f32[24,32,128]{2,1,0:T(8,128)}) custom-call(f32[288]{0:T(512)S(1)} %copy-done.12, f32[288]{0:T(512)S(1)} %copy-done.13, s32[2]{0:T(128)S(1)} %pad_add_fusion.place_ref, f32[3,32,128]{2,1,0:T(8,128)S(1)} %pad_maximum_fusion.mask_ref, f32[288,32,128]{2,1,0:T(8,128)} %bitcast.31, ...), custom_call_target="tpu_custom_call" | custom-call | flops 7864320 | bytes 3932160 | tf_op jit(solution)/shard_map/propagate/pallas_call | solution.py:359
  103.4 1.3 collective-permute-start.7
  105.5 6.0 %collective-permute-start.8 = (f32[24,32,128]{2,1,0:T(8,128)}, f32[24,32,128]{2,1,0:T(8,128)}, u32[]{:S(2)}, u32[]{:S(2)}) collective-permute-start(f32[24,32,128]{2,1,0:T(8,128)} %get-tuple-element.25.refs_12_), channel_id=1, source_target_pairs={{8,0},{16,8},{24,16},{9,1},{17,9},{25,17},{10,2},{18,10},{26,18},{... | collective-permute-start | bytes 1179656 | tf_op jit(solution)/shard_map/ppermute | solution.py:501
  111.5 3.1 %propagate.9.refs_14_ = f32[32,32,128]{2,1,0:T(8,128)S(1)} custom-call(f32[288]{0:T(512)S(1)} %copy-done.12, f32[288]{0:T(512)S(1)} %copy-done.13, s32[2]{0:T(128)S(1)} %pad_add_fusion.place_ref, f32[3,32,128]{2,1,0:T(8,128)S(1)} %pad_maximum_fusion.mask_ref, f32[288,32,128]{2,1,0:T(8,128)} %bitcast.32, f32[288,32,128]{2,1,0:T(8,128)} %collective-permute-done.3.mate_hbm, ...), custom_call_target="tpu_custom_call" | custom-call | flops 5242880 | bytes 2621440 | tf_op jit(solution)/shard_map/propagate/pallas_call | solution.py:359
  114.6 11.6 %collective-permute-done.19.refs_10_ = f32[32,32,128]{2,1,0:T(8,128)} collective-permute-done((f32[32,32,128]{2,1,0:T(8,128)}, f32[32,32,128]{2,1,0:T(8,128)}, u32[]{:S(2)}, u32[]{:S(2)}) %collective-permute-start.19) | collective-permute-done | bytes 524320 | tf_op jit(solution)/shard_map/ppermute | solution.py:501
  126.3 5.4 %quadruplets.2 = (f32[544,32,128]{2,1,0:T(8,128)S(1)}, f32[288,32,128]{2,1,0:T(8,128)}) custom-call(f32[1152]{0:T(1024)S(1)} %copy-done.14, s32[2,4]{1,0:T(2,128)S(1)} %bitcast.20, s32[1]{0:T(128)} %bitcast.1.first_ref, f32[32,32,128]{2,1,0:T(8,128)S(1)} %copy-done.1, f32[32,32,128]{2,1,0:T(8,128)S(1)} %copy-done.3, f32[32,32,128]{2,1,0:T(8,128)S(1)} %copy-done.7, ...), custom_call_target="tpu_custom_call" | custom-call | flops 13762560 | bytes 22020096 | tf_op jit(solution)/shard_map/quadruplets/pallas_call | solution.py:429
  132.5 3.0 %quadruplets.3 = (f32[544,32,128]{2,1,0:T(8,128)S(1)}, f32[288,32,128]{2,1,0:T(8,128)}) custom-call(f32[1152]{0:T(1024)S(1)} %copy-done.14, s32[2,4]{1,0:T(2,128)S(1)} %bitcast.21, s32[1]{0:T(128)} %bitcast.1.first_ref, f32[24,32,128]{2,1,0:T(8,128)} %collective-permute-done.7.refs_0_, ...), custom_call_target="tpu_custom_call", output_to_operand_aliasing={{0}: (5, {}), {1}: (6, {})} | custom-call | flops 3932160 | bytes 6291456 | tf_op jit(solution)/shard_map/quadruplets/pallas_call | solution.py:429
  (61 shorter events, 7.0 us)
Async XLA Ops:
  0.0 72.0 %collective-permute-start.3 = (f32[288,32,128]{2,1,0:T(8,128)}, f32[288,32,128]{2,1,0:T(8,128)}, u32[]{:S(2)}, u32[]{:S(2)}) collective-permute-start(f32[288,32,128]{2,1,0:T(8,128)} %bitcast.22), channel_id=1, source_target_pairs={{0,1},{1,0},{2,3},{3,2},{4,5},{5,4},{6,7},{7,6},{8,9},{9,8},{10,11... | collective-permute-start | bytes 14155784 | tf_op jit(solution)/shard_map/ppermute | solution.py:482
  4.4 6.5 %collective-permute-start = (f32[65,32,128]{2,1,0:T(8,128)}, f32[65,32,128]{2,1,0:T(8,128)}, u32[]{:S(2)}, u32[]{:S(2)}) collective-permute-start(f32[65,32,128]{2,1,0:T(8,128)} %get-tuple-element.22.own_ref), channel_id=1, source_target_pairs={{0,1},{1,0},{2,3},{3,2},{4,5},{5,4},{6,7},{7,6},{8,9},{9,8},{10,11... | collective-permute-start | bytes 3194888 | tf_op jit(solution)/shard_map/ppermute | solution.py:476
  4.5 12.6 %collective-permute-start.11 = (f32[80,32,128]{2,1,0:T(8,128)}, f32[80,32,128]{2,1,0:T(8,128)S(1)}, u32[]{:S(2)}, u32[]{:S(2)}) collective-permute-start(f32[80,32,128]{2,1,0:T(8,128)} %get-tuple-element.28), channel_id=1, source_target_pairs={{3,6},{4,1},{11,14},{12,9},{19,22},{20,17},{27,30},{28,25}} | collective-permute-start | bytes 3932168 | tf_op jit(solution)/shard_map/ppermute | solution.py:477
  8.4 20.9 %collective-permute-start.4 = (f32[80,32,128]{2,1,0:T(8,128)}, f32[80,32,128]{2,1,0:T(8,128)S(1)}, u32[]{:S(2)}, u32[]{:S(2)}) collective-permute-start(f32[80,32,128]{2,1,0:T(8,128)} %get-tuple-element.23), channel_id=1, source_target_pairs={{3,6},{4,1},{11,14},{12,9},{19,22},{20,17},{27,30},{28,25}} | collective-permute-start | bytes 3932168 | tf_op jit(solution)/shard_map/ppermute | solution.py:481
  9.2 34.2 %collective-permute-start.16 = (f32[64,32,128]{2,1,0:T(8,128)}, f32[64,32,128]{2,1,0:T(8,128)}, u32[]{:S(2)}, u32[]{:S(2)}) collective-permute-start(f32[64,32,128]{2,1,0:T(8,128)} %get-tuple-element.31), channel_id=1, source_target_pairs={{3,6},{4,1},{11,14},{12,9},{19,22},{20,17},{27,30},{28,25}} | collective-permute-start | bytes 3145736 | tf_op jit(solution)/shard_map/ppermute | solution.py:481
  12.8 42.5 %collective-permute-start.1 = (f32[66,32,128]{2,1,0:T(8,128)S(1)}, f32[66,32,128]{2,1,0:T(8,128)S(1)}, u32[]{:S(2)}, u32[]{:S(2)}) collective-permute-start(f32[66,32,128]{2,1,0:T(8,128)S(1)} %pack_first.1), channel_id=1, source_target_pairs={{1,2},{5,6},{2,1},{6,5},{9,10},{13,14},{10,9},{14,13},{17,18},{21,... | collective-permute-start | bytes 3244040 | tf_op jit(solution)/shard_map/ppermute | solution.py:478
  19.2 36.8 %collective-permute-start.12 = (f32[80,32,128]{2,1,0:T(8,128)S(1)}, f32[80,32,128]{2,1,0:T(8,128)S(1)}, u32[]{:S(2)}, u32[]{:S(2)}) collective-permute-start(f32[80,32,128]{2,1,0:T(8,128)S(1)} %pack_message.4), channel_id=1, source_target_pairs={{1,2},{5,6},{2,1},{6,5},{9,10},{13,14},{10,9},{14,13},{17,18},{21,... | collective-permute-start | bytes 3932168 | tf_op jit(solution)/shard_map/ppermute | solution.py:486
  31.3 40.7 %copy-start.13 = (f32[288]{0:T(512)S(1)}, f32[288]{0:T(512)}, u32[]{:S(2)}) copy-start(f32[288]{0:T(512)} %b_ref.9) | copy-start | bytes 3460
  31.3 27.6 %collective-permute-start.5 = (f32[80,32,128]{2,1,0:T(8,128)S(1)}, f32[80,32,128]{2,1,0:T(8,128)S(1)}, u32[]{:S(2)}, u32[]{:S(2)}) collective-permute-start(f32[80,32,128]{2,1,0:T(8,128)S(1)} %pack_message.3), channel_id=1, source_target_pairs={{1,2},{5,6},{2,1},{6,5},{9,10},{13,14},{10,9},{14,13},{17,18},{21,... | collective-permute-start | bytes 3932168 | tf_op jit(solution)/shard_map/ppermute | solution.py:486
  45.9 23.9 %collective-permute-start.17 = (f32[64,32,128]{2,1,0:T(8,128)S(1)}, f32[64,32,128]{2,1,0:T(8,128)S(1)}, u32[]{:S(2)}, u32[]{:S(2)}) collective-permute-start(f32[64,32,128]{2,1,0:T(8,128)S(1)} %pack_message.5), channel_id=1, source_target_pairs={{1,2},{5,6},{2,1},{6,5},{9,10},{13,14},{10,9},{14,13},{17,18},{21,... | collective-permute-start | bytes 3145736 | tf_op jit(solution)/shard_map/ppermute | solution.py:486
  55.3 16.7 %collective-permute-start.2 = (f32[66,32,128]{2,1,0:T(8,128)S(1)}, f32[66,32,128]{2,1,0:T(8,128)S(1)}, u32[]{:S(2)}, u32[]{:S(2)}) collective-permute-start(f32[66,32,128]{2,1,0:T(8,128)S(1)} %collective-permute-done.1.side_ref), channel_id=1, source_target_pairs={{1,4},{6,3},{9,12},{14,11},{17,20},{22,19},{25,28},{30,27}} | collective-permute-start | bytes 3244040 | tf_op jit(solution)/shard_map/ppermute | solution.py:479
  56.0 31.8 %collective-permute-start.13 = (f32[80,32,128]{2,1,0:T(8,128)S(1)}, f32[80,32,128]{2,1,0:T(8,128)S(1)}, u32[]{:S(2)}, u32[]{:S(2)}) collective-permute-start(f32[80,32,128]{2,1,0:T(8,128)S(1)} %collective-permute-done.12.side_ref), channel_id=1, source_target_pairs={{5,4},{2,3},{13,12},{10,11},{21,20},{18,19},{29,28},{26,27}} | collective-permute-start | bytes 3932168 | tf_op jit(solution)/shard_map/ppermute | solution.py:487
  58.9 37.1 %collective-permute-start.6 = (f32[80,32,128]{2,1,0:T(8,128)S(1)}, f32[80,32,128]{2,1,0:T(8,128)S(1)}, u32[]{:S(2)}, u32[]{:S(2)}) collective-permute-start(f32[80,32,128]{2,1,0:T(8,128)S(1)} %collective-permute-done.5.side_ref), channel_id=1, source_target_pairs={{5,4},{2,3},{13,12},{10,11},{21,20},{18,19},{29,28},{26,27}} | collective-permute-start | bytes 3932168 | tf_op jit(solution)/shard_map/ppermute | solution.py:487
  69.9 9.3 %collective-permute-start.18 = (f32[64,32,128]{2,1,0:T(8,128)S(1)}, f32[64,32,128]{2,1,0:T(8,128)S(1)}, u32[]{:S(2)}, u32[]{:S(2)}) collective-permute-start(f32[64,32,128]{2,1,0:T(8,128)S(1)} %collective-permute-done.17.side_ref), channel_id=1, source_target_pairs={{5,4},{2,3},{13,12},{10,11},{21,20},{18,19},{29,28},{26,27}} | collective-permute-start | bytes 3145736 | tf_op jit(solution)/shard_map/ppermute | solution.py:487
  75.8 8.0 %copy-start = (f32[32,32,128]{2,1,0:T(8,128)}, f32[32,32,128]{2,1,0:T(8,128)S(1)}, u32[]{:S(2)}) copy-start(f32[32,32,128]{2,1,0:T(8,128)S(1)} %get-tuple-element.26.refs_0_) | copy-start | bytes 1572868
  75.8 21.5 %collective-permute-start.10 = (f32[32,32,128]{2,1,0:T(8,128)S(1)}, f32[32,32,128]{2,1,0:T(8,128)S(1)}, u32[]{:S(2)}, u32[]{:S(2)}) collective-permute-start(f32[32,32,128]{2,1,0:T(8,128)S(1)} %get-tuple-element.26.refs_0_), channel_id=1, source_target_pairs={{8,0},{16,8},{24,16},{9,1},{17,9},{25,17},{10,2},{18,10},{26,18},{... | collective-permute-start | bytes 1572872 | tf_op jit(solution)/shard_map/ppermute | solution.py:501
  77.9 24.7 %collective-permute-start.9 = (f32[32,32,128]{2,1,0:T(8,128)S(1)}, f32[32,32,128]{2,1,0:T(8,128)S(1)}, u32[]{:S(2)}, u32[]{:S(2)}) collective-permute-start(f32[32,32,128]{2,1,0:T(8,128)S(1)} %get-tuple-element.27.refs_1_), channel_id=1, source_target_pairs={{0,8},{8,16},{16,24},{1,9},{9,17},{17,25},{2,10},{10,18},{18,26},{... | collective-permute-start | bytes 1572872 | tf_op jit(solution)/shard_map/ppermute | solution.py:501
  83.8 9.4 %copy-start.8 = (f32[32,32,128]{2,1,0:T(8,128)}, f32[32,32,128]{2,1,0:T(8,128)S(1)}, u32[]{:S(2)}) copy-start(f32[32,32,128]{2,1,0:T(8,128)S(1)} %get-tuple-element.32.refs_8_) | copy-start | bytes 1572868
  83.8 20.9 %collective-permute-start.20 = (f32[32,32,128]{2,1,0:T(8,128)S(1)}, f32[32,32,128]{2,1,0:T(8,128)S(1)}, u32[]{:S(2)}, u32[]{:S(2)}) collective-permute-start(f32[32,32,128]{2,1,0:T(8,128)S(1)} %get-tuple-element.32.refs_8_), channel_id=1, source_target_pairs={{8,0},{16,8},{24,16},{9,1},{17,9},{25,17},{10,2},{18,10},{26,18},{... | collective-permute-start | bytes 1572872 | tf_op jit(solution)/shard_map/ppermute | solution.py:501
  93.2 33.1 %collective-permute-start.15 = (f32[40,32,128]{2,1,0:T(8,128)S(1)}, f32[40,32,128]{2,1,0:T(8,128)}, u32[]{:S(2)}, u32[]{:S(2)}) collective-permute-start(f32[40,32,128]{2,1,0:T(8,128)S(1)} %get-tuple-element.29.refs_4_), channel_id=1, source_target_pairs={{8,0},{16,8},{24,16},{9,1},{17,9},{25,17},{10,2},{18,10},{26,18},{... | collective-permute-start | bytes 1966088 | tf_op jit(solution)/shard_map/ppermute | solution.py:501
  96.1 30.2 %collective-permute-start.14 = (f32[40,32,128]{2,1,0:T(8,128)}, f32[40,32,128]{2,1,0:T(8,128)}, u32[]{:S(2)}, u32[]{:S(2)}) collective-permute-start(f32[40,32,128]{2,1,0:T(8,128)} %get-tuple-element.30.refs_5_), channel_id=1, source_target_pairs={{0,8},{8,16},{16,24},{1,9},{9,17},{17,25},{2,10},{10,18},{18,26},{... | collective-permute-start | bytes 1966088 | tf_op jit(solution)/shard_map/ppermute | solution.py:501
  97.4 28.9 %collective-permute-start.19 = (f32[32,32,128]{2,1,0:T(8,128)}, f32[32,32,128]{2,1,0:T(8,128)}, u32[]{:S(2)}, u32[]{:S(2)}) collective-permute-start(f32[32,32,128]{2,1,0:T(8,128)} %get-tuple-element.33.refs_9_), channel_id=1, source_target_pairs={{0,8},{8,16},{16,24},{1,9},{9,17},{17,25},{2,10},{10,18},{18,26},{... | collective-permute-start | bytes 1572872 | tf_op jit(solution)/shard_map/ppermute | solution.py:501
  103.4 29.1 %collective-permute-start.7 = (f32[24,32,128]{2,1,0:T(8,128)}, f32[24,32,128]{2,1,0:T(8,128)}, u32[]{:S(2)}, u32[]{:S(2)}) collective-permute-start(f32[24,32,128]{2,1,0:T(8,128)} %get-tuple-element.24.refs_13_), channel_id=1, source_target_pairs={{0,8},{8,16},{16,24},{1,9},{9,17},{17,25},{2,10},{10,18},{18,26},{... | collective-permute-start | bytes 1179656 | tf_op jit(solution)/shard_map/ppermute | solution.py:501
  105.5 27.0 %collective-permute-start.8 = (f32[24,32,128]{2,1,0:T(8,128)}, f32[24,32,128]{2,1,0:T(8,128)}, u32[]{:S(2)}, u32[]{:S(2)}) collective-permute-start(f32[24,32,128]{2,1,0:T(8,128)} %get-tuple-element.25.refs_12_), channel_id=1, source_target_pairs={{8,0},{16,8},{24,16},{9,1},{17,9},{25,17},{10,2},{18,10},{26,18},{... | collective-permute-start | bytes 1179656 | tf_op jit(solution)/shard_map/ppermute | solution.py:501
  111.5 14.8 %copy-start.1 = (f32[32,32,128]{2,1,0:T(8,128)S(1)}, f32[32,32,128]{2,1,0:T(8,128)}, u32[]{:S(2)}) copy-start(f32[32,32,128]{2,1,0:T(8,128)} %copy-done) | copy-start | bytes 1572868
  111.5 14.8 %copy-start.3 = (f32[32,32,128]{2,1,0:T(8,128)S(1)}, f32[32,32,128]{2,1,0:T(8,128)}, u32[]{:S(2)}) copy-start(f32[32,32,128]{2,1,0:T(8,128)} %copy-done.2) | copy-start | bytes 1572868
  111.5 14.8 %copy-start.5 = (f32[32,32,128]{2,1,0:T(8,128)S(1)}, f32[32,32,128]{2,1,0:T(8,128)}, u32[]{:S(2)}) copy-start(f32[32,32,128]{2,1,0:T(8,128)} %copy-done.4) | copy-start | bytes 1572868
  111.5 14.8 %copy-start.7 = (f32[32,32,128]{2,1,0:T(8,128)S(1)}, f32[32,32,128]{2,1,0:T(8,128)}, u32[]{:S(2)}) copy-start(f32[32,32,128]{2,1,0:T(8,128)} %copy-done.6) | copy-start | bytes 1572868
  111.5 14.8 %copy-start.9 = (f32[32,32,128]{2,1,0:T(8,128)S(1)}, f32[32,32,128]{2,1,0:T(8,128)}, u32[]{:S(2)}) copy-start(f32[32,32,128]{2,1,0:T(8,128)} %copy-done.8) | copy-start | bytes 1572868
  111.5 14.8 %copy-start.11 = (f32[32,32,128]{2,1,0:T(8,128)S(1)}, f32[32,32,128]{2,1,0:T(8,128)}, u32[]{:S(2)}) copy-start(f32[32,32,128]{2,1,0:T(8,128)} %copy-done.10) | copy-start | bytes 1572868
  111.5 14.8 %copy-start.14 = (f32[1152]{0:T(1024)S(1)}, f32[1152]{0:T(1024)}, u32[]{:S(2)}) copy-start(f32[1152]{0:T(1024)} %strength_ref.3) | copy-start | bytes 13828
  111.5 14.8 %copy-start.16 = (s32[4,2]{0,1:T(2,128)S(1)}, s32[4,2]{0,1:T(2,128)}, u32[]{:S(2)}) copy-start(s32[4,2]{0,1:T(2,128)} %param.11) | copy-start | bytes 100
  (6 other events, 21.9 us)
